TPU v7x, 128 devices: a whole 4x4x4 slice. The times are simulated.
128 devices in a mesh: leaf: 16 (over z, y), front: 8 (over x, core).
Axes of the slice: x: 4, y: 4, z: 4, core: 2. Of those that a mesh axis runs over, the one named last changes fastest.
Arguments:
- right_side: bfloat16 [32, 81920], P(None, ('leaf', 'front')), may hold values from -6 to 6
- send_order: int32 [81920], P(('leaf', 'front')), may hold values from 0 to 639, as said below
- owner_order: int32 [81920], P(('leaf', 'front')), may hold values from 0 to 639, as said below
- live_rows: int32 [14], replicated, may hold values from 2048 to 4096, as said below
- lower_leaf: bfloat16 [1536, 24576], P(None, ('leaf', 'front')), may hold values from -0.109375 to 0.109375
- upper_leaf: bfloat16 [1536, 24576], P(None, ('leaf', 'front')), may hold values from -0.109375 to 0.109375
- lower_first: bfloat16 [4096, 32768], P(None, ('leaf', 'front')), may hold values from -0.0625 to 0.0625
- lower_second: bfloat16 [4096, 16384], P(None, ('leaf', 'front')), may hold values from -0.0625 to 0.0625
- lower_third: bfloat16 [4096, 8192], P(None, ('leaf', 'front')), may hold values from -0.0625 to 0.0625
- upper_first: bfloat16 [4096, 32768], P(None, ('leaf', 'front')), may hold values from -0.0625 to 0.0625
- upper_second: bfloat16 [4096, 16384], P(None, ('leaf', 'front')), may hold values from -0.0625 to 0.0625
- upper_third: bfloat16 [4096, 8192], P(None, ('leaf', 'front')), may hold values from -0.0625 to 0.0625
- downlink_first: bfloat16 [4096, 24576], P(None, ('leaf', 'front')), may hold values from -0.4375 to 0.4375
- downlink_second: bfloat16 [4096, 32768], P(None, ('leaf', 'front')), may hold values from -0.25 to 0.25
- downlink_third: bfloat16 [4096, 16384], P(None, ('leaf', 'front')), may hold values from -0.25 to 0.25
- uplink_first: bfloat16 [4096, 24576], P(None, ('leaf', 'front')), may hold values from -0.0625 to 0.0625
- uplink_second: bfloat16 [4096, 32768], P(None, ('leaf', 'front')), may hold values from -0.0625 to 0.0625
- uplink_third: bfloat16 [4096, 16384], P(None, ('leaf', 'front')), may hold values from -0.0625 to 0.0625
- pattern_first: int32 [64, 384], P(None, ('leaf', 'front')), may hold values 0 or 1
- pattern_second: int32 [64, 512], P(None, ('leaf', 'front')), may hold values 0 or 1
- pattern_third: int32 [64, 256], P(None, ('leaf', 'front')), may hold values 0 or 1
Outputs:
- solution: bfloat16 [32, 81920], P(None, ('leaf', 'front'))
Inputs may be any that keep to these rules, and one draw needn't show every extreme that they name: `send_order`: each device's 640 entries are a permutation of 0 to 639. `owner_order`: each device's 640 entries are a permutation of 0 to 639. `live_rows`: multiples of 64.
All inputs are finite; a program needn't handle non-finite values. No bound on the sum of `pattern_first` or of `pattern_second` or of `pattern_third` on one device may be relied on, other than what follows from the above.
Results may differ from a plain program's by a relative error of at most 0.023.
Values may be sent and summed in bfloat16 or wider, within the bound.
No kernel may reach another device: no remote copies, remote signals or barrier semaphores. Data moves between devices by JAX's collectives and lax.ppermute only.
A program may use at most 128 MiB of HBM per device.

v0:
```python
import jax
import jax.numpy as jnp
from jax import lax
from jax.sharding import PartitionSpec as P


def partner_2(value, axis, distance):
    mask = 2**distance
    pairs = [(source, source ^ mask) for source in range(lax.axis_size(axis))]
    return lax.ppermute(value, axis, pairs)


def spread(pattern, block):
    wide = jnp.repeat(pattern, block, axis=0)
    return jnp.repeat(wide, block, axis=1).astype(jnp.bfloat16)


def collect_group(portion, level, place):
    gathered = lax.all_gather(portion, "front", axis=1, tiled=True)
    for level_bit in range(level):
        partner = partner_2(gathered, "leaf", level_bit)
        upper_side = place >> level_bit & 1 == 1
        gathered = jnp.where(
            upper_side,
            jnp.concatenate([partner, gathered], axis=1),
            jnp.concatenate([gathered, partner], axis=1),
        )
    return gathered


def leaf_term(portion, matrix):
    return jnp.dot(portion, matrix, preferred_element_type=jnp.float32)


def per_device(
    right_side,
    send_order,
    owner_order,
    live_rows,
    lower_leaf,
    upper_leaf,
    lower_first,
    lower_second,
    lower_third,
    upper_first,
    upper_second,
    upper_third,
    downlink_first,
    downlink_second,
    downlink_third,
    uplink_first,
    uplink_second,
    uplink_third,
    pattern_first,
    pattern_second,
    pattern_third,
):
    fronts = lax.axis_size("front")
    leaves = lax.axis_size("leaf")
    place = lax.axis_index("leaf")
    column = lax.axis_index("front")
    columns = right_side.shape[0]
    leaf_rows = lower_leaf.shape[1]
    sep = lower_first.shape[0]
    lowers = [lower_first, lower_second, lower_third]
    uppers = [upper_first, upper_second, upper_third]
    downs = [downlink_first, downlink_second, downlink_third]
    backs = [uplink_first, uplink_second, uplink_third]
    patterns = [pattern_first, pattern_second, pattern_third]
    block = downlink_first.shape[0] // pattern_first.shape[0]
    pieces = [lower_first.shape[1], lower_second.shape[1], lower_third.shape[1]]
    starts = [0, leaves // 2, leaves // 2 + leaves // 4]
    outgoing = jnp.take(right_side, send_order, axis=1)
    arrived = lax.all_to_all(outgoing, ("leaf", "front"), split_axis=1, concat_axis=1, tiled=True)
    ordered = jnp.take(arrived, owner_order, axis=1)
    leaf_rhs = ordered[:, :leaf_rows]
    level_rhs = []
    offset = leaf_rows
    for level in range(1, 4):
        level_rhs.append(ordered[:, offset : offset + pieces[level - 1]])
        offset = offset + pieces[level - 1]
    piece_masks = []
    full_masks = []
    within = []
    for level in range(1, 4):
        group = 2**level
        member = place & group - 1
        node_live = lax.dynamic_index_in_dim(
            live_rows, starts[level - 1] + (place >> level), 0, keepdims=False
        )
        first_row = (member * fronts + column) * pieces[level - 1]
        piece_masks.append(
            (first_row + jnp.arange(pieces[level - 1], dtype=jnp.int32) < node_live).astype(
                jnp.float32
            )[None, :]
        )
        full_masks.append(
            (jnp.arange(sep, dtype=jnp.int32) < node_live).astype(jnp.float32)[None, :]
        )
        within.append(member)
    expanded = [spread(patterns[index], block) for index in range(3)]
    leaf_y = leaf_term(
        lax.all_gather(leaf_rhs, "front", axis=1, tiled=True), matrix=lower_leaf
    ).astype(jnp.bfloat16)
    children = leaf_y
    level_y = []
    for level in range(1, 4):
        group = 2**level
        piece = pieces[level - 1]
        member = within[level - 1]
        link = downs[level - 1] * expanded[level - 1]
        own_rhs = level_rhs[level - 1].astype(jnp.float32)
        shaped = link.reshape(group, fronts, piece, link.shape[1])
        term = jnp.einsum(
            "kc,jfpc->kfjp", children, shaped, preferred_element_type=jnp.float32
        ).reshape(columns, sep)
        first_row = (column * group + member) * piece
        current = lax.dynamic_slice_in_dim(term, first_row, piece, 1)
        term = lax.dynamic_update_slice_in_dim(term, current - own_rhs, first_row, 1)
        share = lax.psum_scatter(
            term.astype(jnp.bfloat16), "front", scatter_dimension=1, tiled=True
        ).astype(jnp.float32)
        for level_bit in reversed(range(level)):
            middle = share.shape[1] // 2
            lower_half = share[:, :middle]
            upper_half = share[:, middle:]
            high_side = place >> level_bit & 1 == 1
            keeping = jnp.where(high_side, upper_half, lower_half)
            sending = jnp.where(high_side, lower_half, upper_half)
            share = keeping + partner_2(sending.astype(jnp.bfloat16), "leaf", level_bit).astype(
                sending.dtype
            )
        reduced_piece = (-share * piece_masks[level - 1]).astype(jnp.bfloat16)
        reduced_full = collect_group(reduced_piece, level, place)
        solved = jnp.dot(reduced_full, lowers[level - 1], preferred_element_type=jnp.float32)
        found = (solved * piece_masks[level - 1]).astype(jnp.bfloat16)
        level_y.append(found)
        children = found
    level_x = [None, None, None]
    top_full = collect_group(level_y[2], 3, place)
    level_x[2] = (
        jnp.dot(top_full, upper_third, preferred_element_type=jnp.float32) * piece_masks[2]
    ).astype(jnp.bfloat16)
    for level in (2, 1):
        back = backs[level] * expanded[level]
        parent_full = collect_group(level_x[level], level + 1, place)
        update = level_y[level - 1].astype(jnp.float32) - jnp.dot(
            parent_full, back, preferred_element_type=jnp.float32
        )
        reduced = (update * piece_masks[level - 1]).astype(jnp.bfloat16)
        reduced_full = collect_group(reduced, level, place)
        solved = jnp.dot(reduced_full, uppers[level - 1], preferred_element_type=jnp.float32)
        level_x[level - 1] = (solved * piece_masks[level - 1]).astype(jnp.bfloat16)
    back = uplink_first * expanded[0]
    parent_full = collect_group(level_x[0], 1, place)
    update = (
        leaf_y.astype(jnp.float32) - jnp.dot(parent_full, back, preferred_element_type=jnp.float32)
    ).astype(jnp.bfloat16)
    leaf_x = leaf_term(
        lax.all_gather(update, "front", axis=1, tiled=True), matrix=upper_leaf
    ).astype(jnp.bfloat16)
    placed = jnp.concatenate([leaf_x, level_x[0], level_x[1], level_x[2]], axis=1)
    outbound = jnp.zeros_like(placed).at[:, owner_order].set(placed)
    returned = lax.all_to_all(outbound, ("leaf", "front"), split_axis=1, concat_axis=1, tiled=True)
    return jnp.zeros_like(returned).at[:, send_order].set(returned)


def solution(mesh):
    placed = (
        P(None, ("leaf", "front")),
        P(("leaf", "front")),
        P(("leaf", "front")),
        P(),
        P(None, ("leaf", "front")),
        P(None, ("leaf", "front")),
        P(None, ("leaf", "front")),
        P(None, ("leaf", "front")),
        P(None, ("leaf", "front")),
        P(None, ("leaf", "front")),
        P(None, ("leaf", "front")),
        P(None, ("leaf", "front")),
        P(None, ("leaf", "front")),
        P(None, ("leaf", "front")),
        P(None, ("leaf", "front")),
        P(None, ("leaf", "front")),
        P(None, ("leaf", "front")),
        P(None, ("leaf", "front")),
        P(None, ("leaf", "front")),
        P(None, ("leaf", "front")),
        P(None, ("leaf", "front")),
    )
    return jax.shard_map(
        per_device,
        mesh=mesh,
        in_specs=placed,
        out_specs=P(None, ("leaf", "front")),
        check_vma=False,
    )
```

profile of v0, /device:TPU:1, one launch (start us, length us, event | category | flops | bytes accessed | tf_op | source)
XLA Modules:
  0.0 459.3 jit_solution(6995919365814859507)
XLA Ops:
  12.0 11.5 %all-to-all-start = ((bf16[32,128,5]{0,2,1:T(8,128)(2,1)}), bf16[32,128,5]{0,2,1:T(8,128)(2,1)S(1)}, u32[]{:S(2)}, u32[]{:S(2)}) async-start(bf16[32,128,5]{0,2,1:T(8,128)(2,1)} %all_to_all.16), calls=%async_computation | async-start | bytes 524288 | tf_op jit(solution)/shard_map/all_to_all | solution.py:74
  30.7 3.8 all-to-all-done
  36.8 13.3 %all-gather = bf16[8,192,32]{1,2,0:T(8,128)(2,1)S(1)} all-gather(bf16[1,192,32]{1,2,0:T(8,128)(2,1)S(1)} %slice_bitcast_fusion), channel_id=1, replica_groups=mesh['leaf'=16,'front'=8] {'front'}, dimensions={0}, use_global_device_ids=true | all-gather | bytes 110592 | tf_op jit(solution)/shard_map/all_gather | solution.py:103
  55.0 24.1 %reduce-scatter.4.cloned.1.call-done = bf16[32,512]{1,0:T(8,128)(2,1)} async-done(((bf16[32,4096]{1,0:T(8,128)(2,1)}), bf16[32,512]{1,0:T(8,128)(2,1)}) %reduce-scatter.4.cloned.1.call-update) | async-done | bytes 32784 | tf_op jit(solution)/shard_map/reduce_scatter | solution.py:120
  82.6 17.1 %all_gather.34 = bf16[32,2048]{1,0:T(8,128)(2,1)S(1)} all-gather(bf16[32,256]{1,0:T(8,128)(2,1)S(1)} %multiply_convert_fusion), channel_id=1, replica_groups=mesh['leaf'=16,'front'=8] {'front'}, dimensions={1}, use_global_device_ids=true | all-gather | bytes 147456 | tf_op jit(solution)/shard_map/all_gather | solution.py:19
  100.9 4.1 copy.74
  105.0 4.2 copy.84
  109.4 4.5 bitcast_multiply_fusion
  113.9 4.1 copy.91
  121.8 27.1 %reduce-scatter.6.cloned.1.call-done = bf16[32,512]{1,0:T(8,128)(2,1)} async-done(((bf16[32,4096]{1,0:T(8,128)(2,1)}), bf16[32,512]{1,0:T(8,128)(2,1)}) %reduce-scatter.6.cloned.1.call-update) | async-done | bytes 32784 | tf_op jit(solution)/shard_map/reduce_scatter | solution.py:120
  156.4 16.6 %all_gather.35 = bf16[32,1024]{1,0:T(8,128)(2,1)S(1)} all-gather(bf16[32,128]{1,0:T(8,128)(2,1)S(1)} %multiply_convert_fusion.2), channel_id=1, replica_groups=mesh['leaf'=16,'front'=8] {'front'}, dimensions={1}, use_global_device_ids=true | all-gather | bytes 73728 | tf_op jit(solution)/shard_map/all_gather | solution.py:19
  196.3 27.5 %reduce-scatter.8.cloned.1.call-done = bf16[32,512]{1,0:T(8,128)(2,1)} async-done(((bf16[32,4096]{1,0:T(8,128)(2,1)}), bf16[32,512]{1,0:T(8,128)(2,1)}) %reduce-scatter.8.cloned.1.call-update) | async-done | bytes 32784 | tf_op jit(solution)/shard_map/reduce_scatter | solution.py:120
  234.0 19.3 %all-gather.1 = bf16[8,64,32]{1,2,0:T(8,128)(2,1)S(1)} all-gather(bf16[1,64,32]{1,2,0:T(8,128)(2,1)S(1)} %fusion.79), channel_id=1, replica_groups=mesh['leaf'=16,'front'=8] {'front'}, dimensions={0}, use_global_device_ids=true | all-gather | bytes 36864 | tf_op jit(solution)/shard_map/all_gather | solution.py:19
  266.3 16.2 %all-gather.2 = bf16[8,64,32]{1,2,0:T(8,128)(2,1)S(1)} all-gather(bf16[1,64,32]{1,2,0:T(8,128)(2,1)S(1)} %fusion.17), channel_id=1, replica_groups=mesh['leaf'=16,'front'=8] {'front'}, dimensions={0}, use_global_device_ids=true | all-gather | bytes 36864 | tf_op jit(solution)/shard_map/all_gather | solution.py:19
  295.5 16.2 %all-gather.3 = bf16[8,64,32]{1,2,0:T(8,128)(2,1)S(1)} all-gather(bf16[1,64,32]{1,2,0:T(8,128)(2,1)S(1)} %bitcast.122), channel_id=1, replica_groups=mesh['leaf'=16,'front'=8] {'front'}, dimensions={0}, use_global_device_ids=true | all-gather | bytes 36864 | tf_op jit(solution)/shard_map/all_gather | solution.py:19
  323.8 14.7 %all_gather.39 = bf16[32,1024]{1,0:T(8,128)(2,1)S(1)} all-gather(bf16[32,128]{1,0:T(8,128)(2,1)S(1)} %fusion.12), channel_id=1, replica_groups=mesh['leaf'=16,'front'=8] {'front'}, dimensions={1}, use_global_device_ids=true | all-gather | bytes 73728 | tf_op jit(solution)/shard_map/all_gather | solution.py:19
  347.8 13.1 %all_gather.40 = bf16[32,1024]{1,0:T(8,128)(2,1)S(1)} all-gather(bf16[32,128]{1,0:T(8,128)(2,1)S(1)} %fusion.16), channel_id=1, replica_groups=mesh['leaf'=16,'front'=8] {'front'}, dimensions={1}, use_global_device_ids=true | all-gather | bytes 73728 | tf_op jit(solution)/shard_map/all_gather | solution.py:19
  370.6 14.9 %all_gather.41 = bf16[32,2048]{1,0:T(8,128)(2,1)S(1)} all-gather(bf16[32,256]{1,0:T(8,128)(2,1)S(1)} %fusion.8), channel_id=1, replica_groups=mesh['leaf'=16,'front'=8] {'front'}, dimensions={1}, use_global_device_ids=true | all-gather | bytes 147456 | tf_op jit(solution)/shard_map/all_gather | solution.py:19
  386.7 3.8 collective-permute-done.22
  390.9 13.6 %all_gather.42 = bf16[32,2048]{1,0:T(8,128)(2,1)S(1)} all-gather(bf16[32,256]{1,0:T(8,128)(2,1)S(1)} %fusion.9), channel_id=1, replica_groups=mesh['leaf'=16,'front'=8] {'front'}, dimensions={1}, use_global_device_ids=true | all-gather | bytes 147456 | tf_op jit(solution)/shard_map/all_gather | solution.py:19
  410.1 13.6 %all-gather.4 = bf16[8,192,32]{1,2,0:T(8,128)(2,1)S(1)} all-gather(bf16[1,192,32]{1,2,0:T(8,128)(2,1)S(1)} %fusion.10), channel_id=1, replica_groups=mesh['leaf'=16,'front'=8] {'front'}, dimensions={0}, use_global_device_ids=true | all-gather | bytes 110592 | tf_op jit(solution)/shard_map/all_gather | solution.py:160
  424.4 4.3 scatter_custom_fusion
  428.8 18.5 %all_to_all.24 = bf16[32,128,5]{0,2,1:T(8,128)(2,1)S(1)} all-to-all(bf16[32,128,5]{0,2,1:T(8,128)(2,1)S(1)} %all_to_all.19), channel_id=1, replica_groups=mesh['leaf'=16,'front'=8] {'leaf','front'}, dimensions={1} | all-to-all | bytes 81920 | tf_op jit(solution)/shard_map/all_to_all | solution.py:164
  447.4 4.6 %scatter_custom_fusion.1 = bf16[32,640]{0,1:T(8,128)(2,1)S(1)} fusion(s32[640]{0:T(1024)S(1)} %compare_select_fusion.1, bf16[32,640]{0,1:T(8,128)(2,1)S(1)} %reshape.88, bf16[]{:T(256)} %constant.15.clone.1), kind=kCustom, calls=%fused_computation.102 | custom fusion | bytes 204802 | tf_op jit(solution)/shard_map/scatter | solution.py:165
  (177 shorter events, 135.1 us)
Async XLA Ops:
  12.0 22.6 %all-to-all-start = ((bf16[32,128,5]{0,2,1:T(8,128)(2,1)}), bf16[32,128,5]{0,2,1:T(8,128)(2,1)S(1)}, u32[]{:S(2)}, u32[]{:S(2)}) async-start(bf16[32,128,5]{0,2,1:T(8,128)(2,1)} %all_to_all.16), calls=%async_computation | async-start | bytes 524288 | tf_op jit(solution)/shard_map/all_to_all | solution.py:74
  23.5 55.7 %reduce-scatter.4.cloned.1.call-start = ((), (), s32[]{:S(2)}) async-start(), calls=%async_computation.5 | async-start | bytes 294912 | tf_op jit(solution)/shard_map/reduce_scatter | solution.py:120
  54.3 94.5 %reduce-scatter.6.cloned.1.call-start = ((), (), s32[]{:S(2)}) async-start(), calls=%async_computation.6 | async-start | bytes 294912 | tf_op jit(solution)/shard_map/reduce_scatter | solution.py:120
  99.7 18.3 %collective-permute-start.1 = (bf16[32,2048]{1,0:T(8,128)(2,1)S(1)}, bf16[32,2048]{1,0:T(8,128)(2,1)S(1)}, u32[]{:S(2)}, u32[]{:S(2)}) collective-permute-start(bf16[32,2048]{1,0:T(8,128)(2,1)S(1)} %all_gather.34), channel_id=1, source_target_pairs={{0,8},{8,0},{16,24},{24,16},{32,40},{40,32},{48,56},{56,48},{64,72... | collective-permute-start | bytes 393224 | tf_op jit(solution)/shard_map/ppermute | solution.py:10
  121.7 102.1 %reduce-scatter.8.cloned.1.call-start = ((), (), s32[]{:S(2)}) async-start(), calls=%async_computation.7 | async-start | bytes 294912 | tf_op jit(solution)/shard_map/reduce_scatter | solution.py:120
  149.6 4.2 collective-permute-start.2
  173.0 3.5 collective-permute-start.4
  176.5 11.4 %collective-permute-start.5 = (bf16[32,2048]{1,0:T(8,128)(2,1)S(1)}, bf16[32,2048]{1,0:T(8,128)(2,1)S(1)}, u32[]{:S(2)}, u32[]{:S(2)}) collective-permute-start(bf16[32,2048]{1,0:T(8,128)(2,1)S(1)} %maximum_select_fusion.18), channel_id=1, source_target_pairs={{0,16},{8,24},{16,0},{24,8},{32,48},{40,56},{48,32},{56,40},{64,80... | collective-permute-start | bytes 393224 | tf_op jit(solution)/shard_map/ppermute | solution.py:10
  227.3 4.1 collective-permute-start.7
  253.5 2.8 collective-permute-start.9
  256.4 4.7 %collective-permute-start.10 = (bf16[32,1024]{1,0:T(8,128)(2,1)S(1)}, bf16[32,1024]{1,0:T(8,128)(2,1)S(1)}, u32[]{:S(2)}, u32[]{:S(2)}) collective-permute-start(bf16[32,1024]{1,0:T(8,128)(2,1)S(1)} %maximum_select_fusion.24), channel_id=1, source_target_pairs={{0,16},{8,24},{16,0},{24,8},{32,48},{40,56},{48,32},{56,40},{64,80... | collective-permute-start | bytes 196616 | tf_op jit(solution)/shard_map/ppermute | solution.py:10
  261.1 3.9 collective-permute-start.11
  282.7 2.8 collective-permute-start.12
  285.5 4.7 %collective-permute-start.13 = (bf16[32,1024]{1,0:T(8,128)(2,1)S(1)}, bf16[32,1024]{1,0:T(8,128)(2,1)S(1)}, u32[]{:S(2)}, u32[]{:S(2)}) collective-permute-start(bf16[32,1024]{1,0:T(8,128)(2,1)S(1)} %maximum_select_fusion.25), channel_id=1, source_target_pairs={{0,16},{8,24},{16,0},{24,8},{32,48},{40,56},{48,32},{56,40},{64,80... | collective-permute-start | bytes 196616 | tf_op jit(solution)/shard_map/ppermute | solution.py:10
  290.3 3.9 collective-permute-start.14
  311.8 2.8 collective-permute-start.15
  314.7 4.7 %collective-permute-start.16 = (bf16[32,1024]{1,0:T(8,128)(2,1)S(1)}, bf16[32,1024]{1,0:T(8,128)(2,1)S(1)}, u32[]{:S(2)}, u32[]{:S(2)}) collective-permute-start(bf16[32,1024]{1,0:T(8,128)(2,1)S(1)} %maximum_select_fusion.26), channel_id=1, source_target_pairs={{0,16},{8,24},{16,0},{24,8},{32,48},{40,56},{48,32},{56,40},{64,80... | collective-permute-start | bytes 196616 | tf_op jit(solution)/shard_map/ppermute | solution.py:10
  319.5 3.9 collective-permute-start.17
  338.5 3.5 collective-permute-start.18
  342.0 5.4 %collective-permute-start.19 = (bf16[32,2048]{1,0:T(8,128)(2,1)S(1)}, bf16[32,2048]{1,0:T(8,128)(2,1)S(1)}, u32[]{:S(2)}, u32[]{:S(2)}) collective-permute-start(bf16[32,2048]{1,0:T(8,128)(2,1)S(1)} %maximum_select_fusion.22), channel_id=1, source_target_pairs={{0,16},{8,24},{16,0},{24,8},{32,48},{40,56},{48,32},{56,40},{64,80... | collective-permute-start | bytes 393224 | tf_op jit(solution)/shard_map/ppermute | solution.py:10
  360.9 3.5 collective-permute-start.20
  364.5 5.4 %collective-permute-start.21 = (bf16[32,2048]{1,0:T(8,128)(2,1)S(1)}, bf16[32,2048]{1,0:T(8,128)(2,1)S(1)}, u32[]{:S(2)}, u32[]{:S(2)}) collective-permute-start(bf16[32,2048]{1,0:T(8,128)(2,1)S(1)} %maximum_select_fusion.23), channel_id=1, source_target_pairs={{0,16},{8,24},{16,0},{24,8},{32,48},{40,56},{48,32},{56,40},{64,80... | collective-permute-start | bytes 393224 | tf_op jit(solution)/shard_map/ppermute | solution.py:10
  385.6 4.9 %collective-permute-start.22 = (bf16[32,2048]{1,0:T(8,128)(2,1)S(1)}, bf16[32,2048]{1,0:T(8,128)(2,1)S(1)}, u32[]{:S(2)}, u32[]{:S(2)}) collective-permute-start(bf16[32,2048]{1,0:T(8,128)(2,1)S(1)} %all_gather.41), channel_id=1, source_target_pairs={{0,8},{8,0},{16,24},{24,16},{32,40},{40,32},{48,56},{56,48},{64,72... | collective-permute-start | bytes 393224 | tf_op jit(solution)/shard_map/ppermute | solution.py:10
  404.5 4.9 %collective-permute-start.23 = (bf16[32,2048]{1,0:T(8,128)(2,1)S(1)}, bf16[32,2048]{1,0:T(8,128)(2,1)S(1)}, u32[]{:S(2)}, u32[]{:S(2)}) collective-permute-start(bf16[32,2048]{1,0:T(8,128)(2,1)S(1)} %all_gather.42), channel_id=1, source_target_pairs={{0,8},{8,0},{16,24},{24,16},{32,40},{40,32},{48,56},{56,48},{64,72... | collective-permute-start | bytes 393224 | tf_op jit(solution)/shard_map/ppermute | solution.py:10
  (16 other events, 433.8 us)
Sparse Core Ops, SparseCore 0:
  54.4 24.6 reduce-scatter.3
  121.8 26.9 reduce-scatter.5
  196.4 27.3 reduce-scatter.7
where the time goes:
time: 461 us; the launch traced here: 459 us
  blocking collectives  187 us (41%)
  waiting for transfers between devices  126 us (27%)
  starting transfers between devices  55 us (12%)
  local copies, waits for them, and re-layouts  43.1 us (9%)
  other arithmetic  23.3 us (5%)
  between operations  13.6 us (3%)
  matrix products  11.4 us (2%)
    all_gather x9, blocking collectives, collect_group(): gathered = lax.all_gather(portion, 'front', axis=1, tiled=True)  142 us
    reduce_scatter x3, waiting for transfers between devices, per_device(): lax.psum_scatter(term.astype(jnp.bfloat16), 'front', scatter_dimension=1,...  78.7 us
    ppermute x24, starting transfers between devices, partner_2(): return lax.ppermute(value, axis, pairs)  43.4 us
    ppermute x24, waiting for transfers between devices, partner_2(): return lax.ppermute(value, axis, pairs)  43.3 us
    all_to_all x1, blocking collectives, per_device(): lax.all_to_all(outbound, ('leaf', 'front'), split_axis=1, concat_axis=1,...  18.5 us
    unnamed x36, local copies, waits for them, and re-layouts  16.5 us
    all_gather x1, blocking collectives, per_device(): lax.all_gather(update, 'front', axis=1, tiled=True)  13.6 us
    all_gather x1, blocking collectives, per_device(): lax.all_gather(leaf_rhs, 'front', axis=1, tiled=True)  13.3 us
  transfers between devices with their start and end apart: 28, of which 26 were waited for; matrix products, arithmetic and copies ran while one was open for 8% of the time, Pallas kernels for 0%

commit v1 on v0

v1 whole, which is shorter than its diff:
```python
import jax
import jax.numpy as jnp
from jax import lax
from jax.sharding import Mesh, PartitionSpec as P


def spread(pattern, block):
    wide = jnp.repeat(pattern, block, axis=0)
    return jnp.repeat(wide, block, axis=1).astype(jnp.bfloat16)


GROUPS = {
    0: ("x", "c"),
    1: ("y0", "x", "c"),
    2: ("y1", "y0", "x", "c"),
    3: ("z0", "y1", "y0", "x", "c"),
}
EVERY = ("z1", "z0", "y1", "y0", "x", "c")


def collect_group(portion, level):
    axes = GROUPS[level]
    members = lax.axis_size(axes)
    copies = jnp.broadcast_to(portion[None], (members,) + portion.shape)
    gathered = lax.all_to_all(copies, axes, split_axis=0, concat_axis=0, tiled=True)
    return jnp.transpose(gathered, (1, 0, 2)).reshape(portion.shape[0], -1)


def reduce_group(term, level):
    axes = GROUPS[level]
    members = lax.axis_size(axes)
    split = jnp.transpose(term.reshape(term.shape[0], members, -1), (1, 0, 2))
    received = lax.all_to_all(split, axes, split_axis=0, concat_axis=0, tiled=True)
    return jnp.sum(received.astype(jnp.float32), axis=0)


def leaf_term(portion, matrix):
    return jnp.dot(portion, matrix, preferred_element_type=jnp.float32)


def per_device(
    right_side,
    send_order,
    owner_order,
    live_rows,
    lower_leaf,
    upper_leaf,
    lower_first,
    lower_second,
    lower_third,
    upper_first,
    upper_second,
    upper_third,
    downlink_first,
    downlink_second,
    downlink_third,
    uplink_first,
    uplink_second,
    uplink_third,
    pattern_first,
    pattern_second,
    pattern_third,
):
    fronts = lax.axis_size(("x", "c"))
    leaves = lax.axis_size(("z1", "z0", "y1", "y0"))
    place = lax.axis_index(("z1", "z0", "y1", "y0"))
    column = lax.axis_index(("x", "c"))
    columns = right_side.shape[0]
    leaf_rows = lower_leaf.shape[1]
    sep = lower_first.shape[0]
    lowers = [lower_first, lower_second, lower_third]
    uppers = [upper_first, upper_second, upper_third]
    downs = [downlink_first, downlink_second, downlink_third]
    backs = [uplink_first, uplink_second, uplink_third]
    patterns = [pattern_first, pattern_second, pattern_third]
    block = downlink_first.shape[0] // pattern_first.shape[0]
    pieces = [lower_first.shape[1], lower_second.shape[1], lower_third.shape[1]]
    starts = [0, leaves // 2, leaves // 2 + leaves // 4]
    outgoing = jnp.take(right_side, send_order, axis=1)
    arrived = lax.all_to_all(outgoing, EVERY, split_axis=1, concat_axis=1, tiled=True)
    ordered = jnp.take(arrived, owner_order, axis=1)
    leaf_rhs = ordered[:, :leaf_rows]
    level_rhs = []
    offset = leaf_rows
    for level in range(1, 4):
        level_rhs.append(ordered[:, offset : offset + pieces[level - 1]])
        offset = offset + pieces[level - 1]
    piece_masks = []
    within = []
    for level in range(1, 4):
        group = 2**level
        member = place & group - 1
        node_live = lax.dynamic_index_in_dim(
            live_rows, starts[level - 1] + (place >> level), 0, keepdims=False
        )
        first_row = (member * fronts + column) * pieces[level - 1]
        piece_masks.append(
            (first_row + jnp.arange(pieces[level - 1], dtype=jnp.int32) < node_live).astype(
                jnp.float32
            )[None, :]
        )
        within.append(member)
    expanded = [spread(patterns[index], block) for index in range(3)]
    leaf_y = leaf_term(
        collect_group(leaf_rhs, 0), matrix=lower_leaf
    ).astype(jnp.bfloat16)
    children = leaf_y
    level_y = []
    for level in range(1, 4):
        group = 2**level
        piece = pieces[level - 1]
        member = within[level - 1]
        link = downs[level - 1] * expanded[level - 1]
        term = lax.dot_general(
            children, link, (((1,), (1,)), ((), ())), preferred_element_type=jnp.float32
        ).astype(jnp.bfloat16)
        share = reduce_group(term, level)
        own_rhs = level_rhs[level - 1].astype(jnp.float32)
        reduced_piece = ((own_rhs - share) * piece_masks[level - 1]).astype(jnp.bfloat16)
        reduced_full = collect_group(reduced_piece, level)
        solved = jnp.dot(reduced_full, lowers[level - 1], preferred_element_type=jnp.float32)
        found = (solved * piece_masks[level - 1]).astype(jnp.bfloat16)
        level_y.append(found)
        children = found
    level_x = [None, None, None]
    top_full = collect_group(level_y[2], 3)
    level_x[2] = (
        jnp.dot(top_full, upper_third, preferred_element_type=jnp.float32) * piece_masks[2]
    ).astype(jnp.bfloat16)
    for level in (2, 1):
        back = backs[level] * expanded[level]
        parent_full = collect_group(level_x[level], level + 1)
        update = level_y[level - 1].astype(jnp.float32) - jnp.dot(
            parent_full, back, preferred_element_type=jnp.float32
        )
        reduced = (update * piece_masks[level - 1]).astype(jnp.bfloat16)
        reduced_full = collect_group(reduced, level)
        solved = jnp.dot(reduced_full, uppers[level - 1], preferred_element_type=jnp.float32)
        level_x[level - 1] = (solved * piece_masks[level - 1]).astype(jnp.bfloat16)
    back = uplink_first * expanded[0]
    parent_full = collect_group(level_x[0], 1)
    update = (
        leaf_y.astype(jnp.float32) - jnp.dot(parent_full, back, preferred_element_type=jnp.float32)
    ).astype(jnp.bfloat16)
    leaf_x = leaf_term(
        collect_group(update, 0), matrix=upper_leaf
    ).astype(jnp.bfloat16)
    placed = jnp.concatenate([leaf_x, level_x[0], level_x[1], level_x[2]], axis=1)
    outbound = jnp.zeros_like(placed).at[:, owner_order].set(placed)
    returned = lax.all_to_all(outbound, EVERY, split_axis=1, concat_axis=1, tiled=True)
    return jnp.zeros_like(returned).at[:, send_order].set(returned)


def solution(mesh):
    fine = Mesh(mesh.devices.reshape(2, 2, 2, 2, 4, 2), EVERY)
    by_column = P(None, EVERY)
    placed = (by_column, P(EVERY), P(EVERY), P()) + (by_column,) * 17
    return jax.shard_map(
        per_device, mesh=fine, in_specs=placed, out_specs=by_column, check_vma=False
    )
```

time: 461 us -> 264 us (0.57)
  waiting for transfers between devices: 126 us -> 37 us
  blocking collectives: 187 us -> 112 us
  starting transfers between devices: 55 us -> 38.8 us
  between operations: 13.6 us -> 0.53 us
  other arithmetic: 23.3 us -> 16.5 us
    all_gather x11 -> x0, blocking collectives: 169 us -> none  [the longest x9 142 us: collect_group(): gathered = lax.all_gather(portion, 'front', axis=1, tiled=True)]
    all_to_all x1 -> x9, blocking collectives: 18.5 us -> 112 us  [the longest x8 96.1 us: collect_group(): lax.all_to_all(copies, axes, split_axis=0, concat_axis=0, tiled=True)]
    reduce_scatter x3 -> x0, waiting for transfers between devices: 78.7 us -> none  [per_device(): lax.psum_scatter(term.astype(jnp.bfloat16), 'front', scatter_dimension=1,...]
    ppermute x24 -> x0, starting transfers between devices: 43.4 us -> none  [partner_2(): return lax.ppermute(value, axis, pairs)]
    ppermute x24 -> x0, waiting for transfers between devices: 43.3 us -> none  [partner_2(): return lax.ppermute(value, axis, pairs)]
    all_to_all x1 -> x7, waiting for transfers between devices: 3.84 us -> 37 us  [the longest x3 23.5 us: reduce_group(): lax.all_to_all(split, axes, split_axis=0, concat_axis=0, tiled=True)]
    all_to_all x1 -> x7, starting transfers between devices: 11.5 us -> 38.8 us  [the longest x3 15.5 us: reduce_group(): lax.all_to_all(split, axes, split_axis=0, concat_axis=0, tiled=True)]
    convert_element_type x14 -> x3, other arithmetic: 5.67 us -> 0.24 us  [per_device(): ((own_rhs - share) * piece_masks[level - 1]).astype(jnp.bfloat16)]
  transfers between devices with their start and end apart: 28 -> 7, of which waited for: 26 -> 6; matrix products, arithmetic and copies ran while one was open for 8% -> 10% of each run, Pallas kernels for 0% -> 0%
where the time goes in v1:
time: 264 us; the launch traced here: 263 us
  blocking collectives  112 us (42%)
  local copies, waits for them, and re-layouts  47.2 us (18%)
  starting transfers between devices  38.8 us (15%)
  waiting for transfers between devices  37 us (14%)
  other arithmetic  16.5 us (6%)
  matrix products  10.2 us (4%)
    all_to_all x8, blocking collectives, collect_group(): lax.all_to_all(copies, axes, split_axis=0, concat_axis=0, tiled=True)  96.1 us
    all_to_all x3, waiting for transfers between devices, reduce_group(): lax.all_to_all(split, axes, split_axis=0, concat_axis=0, tiled=True)  23.5 us
    unnamed x41, local copies, waits for them, and re-layouts  20.1 us
    all_to_all x1, blocking collectives, per_device(): lax.all_to_all(outbound, EVERY, split_axis=1, concat_axis=1, tiled=True)  16.2 us
    all_to_all x3, starting transfers between devices, reduce_group(): lax.all_to_all(split, axes, split_axis=0, concat_axis=0, tiled=True)  15.5 us
    all_to_all x3, starting transfers between devices, collect_group(): lax.all_to_all(copies, axes, split_axis=0, concat_axis=0, tiled=True)  11.9 us
    all_to_all x1, starting transfers between devices, per_device(): lax.all_to_all(outgoing, EVERY, split_axis=1, concat_axis=1, tiled=True)  11.5 us
    all_to_all x1, waiting for transfers between devices, per_device(): lax.all_to_all(outgoing, EVERY, split_axis=1, concat_axis=1, tiled=True)  9.7 us
  transfers between devices with their start and end apart: 7, of which 6 were waited for; matrix products, arithmetic and copies ran while one was open for 10% of the time, Pallas kernels for 0%

profile of v1, /device:TPU:1, one launch (start us, length us, event | category | flops | bytes accessed | tf_op | source)
XLA Modules:
  0.0 262.6 jit_solution(5495975179071172690)
XLA Ops:
  5.4 11.5 %all-to-all-start = ((bf16[32,128,5]{0,2,1:T(8,128)(2,1)}), bf16[32,128,5]{0,2,1:T(8,128)(2,1)S(1)}, u32[]{:S(2)}, u32[]{:S(2)}) async-start(bf16[32,128,5]{0,2,1:T(8,128)(2,1)} %all_to_all.58), calls=%async_computation | async-start | bytes 524288 | tf_op jit(solution)/shard_map/all_to_all | solution.py:80
  18.3 9.7 %all-to-all-done = bf16[32,128,5]{0,2,1:T(8,128)(2,1)S(1)} async-done(((bf16[32,128,5]{0,2,1:T(8,128)(2,1)}), bf16[32,128,5]{0,2,1:T(8,128)(2,1)S(1)}, u32[]{:S(2)}, u32[]{:S(2)}) %all-to-all-start) | async-done | bytes 40992 | tf_op jit(solution)/shard_map/all_to_all | solution.py:80
  31.0 4.0 %all-to-all-start.1 = ((bf16[8,32,192]{2,1,0:T(8,128)(2,1)}), bf16[8,32,192]{2,1,0:T(8,128)(2,1)S(1)}, u32[]{:S(2)}, u32[]{:S(2)}) async-start(bf16[8,32,192]{2,1,0:T(8,128)(2,1)} %broadcast_in_dim.49), calls=%async_computation.1 | async-start | bytes 262144 | tf_op jit(solution)/shard_map/all_to_all | solution.py:25
  43.3 4.2 %all-to-all-start.2 = ((bf16[16,32,256]{2,1,0:T(8,128)(2,1)}), bf16[16,32,256]{2,1,0:T(8,128)(2,1)S(1)}, u32[]{:S(2)}, u32[]{:S(2)}) async-start(bf16[16,32,256]{2,1,0:T(8,128)(2,1)} %bitcast.115), calls=%async_computation.2 | async-start | bytes 524288 | tf_op jit(solution)/shard_map/all_to_all | solution.py:33
  48.7 6.0 %all-to-all-done.2 = bf16[16,32,256]{2,1,0:T(8,128)(2,1)S(1)} async-done(((bf16[16,32,256]{2,1,0:T(8,128)(2,1)}), bf16[16,32,256]{2,1,0:T(8,128)(2,1)S(1)}, u32[]{:S(2)}, u32[]{:S(2)}) %all-to-all-start.2) | async-done | bytes 262176 | tf_op jit(solution)/shard_map/all_to_all | solution.py:33
  55.6 4.1 %all-to-all-start.3 = ((bf16[16,32,256]{2,1,0:T(8,128)(2,1)}), bf16[16,32,256]{2,1,0:T(8,128)(2,1)S(1)}, u32[]{:S(2)}, u32[]{:S(2)}) async-start(bf16[16,32,256]{2,1,0:T(8,128)(2,1)} %broadcast_in_dim.52), calls=%async_computation.3 | async-start | bytes 524288 | tf_op jit(solution)/shard_map/all_to_all | solution.py:25
  59.7 4.1 %copy.41 = bf16[4096,256]{0,1:T(8,128)(2,1)} copy(bf16[4096,256]{1,0:T(8,128)(2,1)} %param.36) | data formatting | bytes 4194304 | tf_op args[13]
  63.8 4.1 %copy.52 = bf16[4096,256]{0,1:T(8,128)(2,1)} copy(bf16[4096,256]{1,0:T(8,128)(2,1)} %param.39) | data formatting | bytes 4194304 | tf_op args[16]
  68.2 4.5 %bitcast_multiply_fusion = (bf16[4096,256]{0,1:T(8,128)(2,1)}, bf16[4096,256]{0,1:T(8,128)(2,1)}) fusion(bf16[4096,256]{0,1:T(8,128)(2,1)} %copy.52, bf16[4096,4]{0,1:T(4,128)(2,1)S(1)} %convert_element_type.146, bf16[4096,256]{0,1:T(8,128)(2,1)} %copy.41), kind=kLoop, calls=%fused_computation.7 | loop fusion | flops 2097152 | bytes 8421376 | tf_op jit(solution)/shard_map/mul | solution.py:131
  75.4 5.9 %all-to-all-start.4 = ((bf16[32,32,128]{2,1,0:T(8,128)(2,1)}), bf16[32,32,128]{2,1,0:T(8,128)(2,1)S(1)}, u32[]{:S(2)}, u32[]{:S(2)}) async-start(bf16[32,32,128]{2,1,0:T(8,128)(2,1)} %bitcast.125), calls=%async_computation.4 | async-start | bytes 524288 | tf_op jit(solution)/shard_map/all_to_all | solution.py:33
  82.0 8.3 %all-to-all-done.4 = bf16[32,32,128]{2,1,0:T(8,128)(2,1)S(1)} async-done(((bf16[32,32,128]{2,1,0:T(8,128)(2,1)}), bf16[32,32,128]{2,1,0:T(8,128)(2,1)S(1)}, u32[]{:S(2)}, u32[]{:S(2)}) %all-to-all-start.4) | async-done | bytes 262176 | tf_op jit(solution)/shard_map/all_to_all | solution.py:33
  107.6 5.4 %all-to-all-start.6 = ((bf16[64,2,1024]{2,1,0:T(2,128)(2,1)}), bf16[64,2,1024]{2,1,0:T(2,128)(2,1)S(1)}, u32[]{:S(2)}, u32[]{:S(2)}) async-start(bf16[64,2,1024]{2,1,0:T(2,128)(2,1)} %reshape.150), calls=%async_computation.6 | async-start | bytes 524288 | tf_op jit(solution)/shard_map/all_to_all | solution.py:33
  113.7 9.2 %all-to-all-done.6 = bf16[64,2,1024]{2,1,0:T(2,128)(2,1)S(1)} async-done(((bf16[64,2,1024]{2,1,0:T(2,128)(2,1)}), bf16[64,2,1024]{2,1,0:T(2,128)(2,1)S(1)}, u32[]{:S(2)}, u32[]{:S(2)}) %all-to-all-start.6) | async-done | bytes 262176 | tf_op jit(solution)/shard_map/all_to_all | solution.py:33
  123.8 13.8 %all_to_all.94 = bf16[64,2,1024]{2,1,0:T(2,128)(2,1)S(1)} all-to-all(bf16[64,2,1024]{2,1,0:T(2,128)(2,1)S(1)} %reshape.152), channel_id=1, replica_groups=mesh['z1'=2,'z0'=2,'y1'=2,'y0'=2,'x'=4,'c'=2] {'z0','y1','y0','x','c'}, dimensions={0} | all-to-all | bytes 524288 | tf_op jit(solution)/shard_map/all_to_all | solution.py:25
  140.3 13.8 %all_to_all.95 = bf16[64,2,1024]{2,1,0:T(2,128)(2,1)S(1)} all-to-all(bf16[64,2,1024]{2,1,0:T(2,128)(2,1)S(1)} %reshape.154), channel_id=1, replica_groups=mesh['z1'=2,'z0'=2,'y1'=2,'y0'=2,'x'=4,'c'=2] {'z0','y1','y0','x','c'}, dimensions={0} | all-to-all | bytes 524288 | tf_op jit(solution)/shard_map/all_to_all | solution.py:25
  158.8 14.3 %all_to_all.96 = bf16[64,2,1024]{2,1,0:T(2,128)(2,1)} all-to-all(bf16[64,2,1024]{2,1,0:T(2,128)(2,1)S(1)} %reshape.156), channel_id=1, replica_groups=mesh['z1'=2,'z0'=2,'y1'=2,'y0'=2,'x'=4,'c'=2] {'z0','y1','y0','x','c'}, dimensions={0} | all-to-all | bytes 524288 | tf_op jit(solution)/shard_map/all_to_all | solution.py:25
  179.3 12.6 %all_to_all.97 = bf16[32,32,128]{2,1,0:T(8,128)(2,1)S(1)} all-to-all(bf16[32,32,128]{2,1,0:T(8,128)(2,1)S(1)} %broadcast_in_dim.116), channel_id=1, replica_groups=mesh['z1'=2,'z0'=2,'y1'=2,'y0'=2,'x'=4,'c'=2] {'y1','y0','x','c'}, dimensions={0} | all-to-all | bytes 524288 | tf_op jit(solution)/shard_map/all_to_all | solution.py:25
  192.2 12.6 %all_to_all.98 = bf16[32,32,128]{2,1,0:T(8,128)(2,1)S(1)} all-to-all(bf16[32,32,128]{2,1,0:T(8,128)(2,1)S(1)} %broadcast_in_dim.117), channel_id=1, replica_groups=mesh['z1'=2,'z0'=2,'y1'=2,'y0'=2,'x'=4,'c'=2] {'y1','y0','x','c'}, dimensions={0} | all-to-all | bytes 524288 | tf_op jit(solution)/shard_map/all_to_all | solution.py:25
  205.6 9.9 %all_to_all.99 = bf16[16,32,256]{2,1,0:T(8,128)(2,1)S(1)} all-to-all(bf16[16,32,256]{2,1,0:T(8,128)(2,1)S(1)} %broadcast_in_dim.118), channel_id=1, replica_groups=mesh['z1'=2,'z0'=2,'y1'=2,'y0'=2,'x'=4,'c'=2] {'y0','x','c'}, dimensions={0} | all-to-all | bytes 524288 | tf_op jit(solution)/shard_map/all_to_all | solution.py:25
  216.0 10.6 %all_to_all.100 = bf16[16,32,256]{2,1,0:T(8,128)(2,1)S(1)} all-to-all(bf16[16,32,256]{2,1,0:T(8,128)(2,1)S(1)} %broadcast_in_dim.119), channel_id=1, replica_groups=mesh['z1'=2,'z0'=2,'y1'=2,'y0'=2,'x'=4,'c'=2] {'y0','x','c'}, dimensions={0} | all-to-all | bytes 524288 | tf_op jit(solution)/shard_map/all_to_all | solution.py:25
  227.3 8.5 %all_to_all.101 = bf16[8,32,192]{2,1,0:T(8,128)(2,1)S(1)} all-to-all(bf16[8,32,192]{2,1,0:T(8,128)(2,1)S(1)} %broadcast_in_dim.120), channel_id=1, replica_groups=mesh['z1'=2,'z0'=2,'y1'=2,'y0'=2,'x'=4,'c'=2] {'x','c'}, dimensions={0} | all-to-all | bytes 196608 | tf_op jit(solution)/shard_map/all_to_all | solution.py:25
  236.6 4.3 %scatter_custom_fusion = bf16[32,640]{0,1:T(8,128)(2,1)S(1)} fusion(s32[640]{0:T(1024)S(1)} %compare_select_fusion, bf16[640,32]{1,0:T(8,128)(2,1)S(1)} %copy.56, bf16[]{:T(256)} %constant.23.clone.1), kind=kCustom, calls=%fused_computation.52 | custom fusion | bytes 40962 | tf_op jit(solution)/shard_map/scatter | solution.py:149
  240.9 16.2 %all_to_all.102 = bf16[32,128,5]{0,2,1:T(8,128)(2,1)S(1)} all-to-all(bf16[32,128,5]{0,2,1:T(8,128)(2,1)S(1)} %all_to_all.75), channel_id=1, replica_groups=mesh['z1'=2,'z0'=2,'y1'=2,'y0'=2,'x'=4,'c'=2] {'z1','z0','y1','y0','x','c'}, dimensions={1} | all-to-all | bytes 81920 | tf_op jit(solution)/shard_map/all_to_all | solution.py:150
  257.3 4.6 %scatter_custom_fusion.1 = bf16[32,640]{0,1:T(8,128)(2,1)S(1)} fusion(s32[640]{0:T(1024)S(1)} %compare_select_fusion.1, bf16[32,640]{0,1:T(8,128)(2,1)S(1)} %reshape.131, bf16[]{:T(256)} %constant.23.clone.1), kind=kCustom, calls=%fused_computation.48 | custom fusion | bytes 204802 | tf_op jit(solution)/shard_map/scatter | solution.py:151
  (125 shorter events, 60.0 us)
Async XLA Ops:
  0.0 72.7 %copy-start = (bf16[4096,256]{1,0:T(8,128)(2,1)S(1)}, bf16[4096,256]{1,0:T(8,128)(2,1)}, u32[]{:S(2)}) copy-start(bf16[4096,256]{1,0:T(8,128)(2,1)} %param.29) | copy-start | bytes 6291460
  0.0 34.9 %copy-start.11 = (s32[64,3]{0,1:T(4,128)S(1)}, s32[64,3]{0,1:T(4,128)}, u32[]{:S(2)}) copy-start(s32[64,3]{0,1:T(4,128)} %param.41) | copy-start | bytes 2308
  5.4 22.6 %all-to-all-start = ((bf16[32,128,5]{0,2,1:T(8,128)(2,1)}), bf16[32,128,5]{0,2,1:T(8,128)(2,1)S(1)}, u32[]{:S(2)}, u32[]{:S(2)}) async-start(bf16[32,128,5]{0,2,1:T(8,128)(2,1)} %all_to_all.58), calls=%async_computation | async-start | bytes 524288 | tf_op jit(solution)/shard_map/all_to_all | solution.py:80
  31.0 9.3 %all-to-all-start.1 = ((bf16[8,32,192]{2,1,0:T(8,128)(2,1)}), bf16[8,32,192]{2,1,0:T(8,128)(2,1)S(1)}, u32[]{:S(2)}, u32[]{:S(2)}) async-start(bf16[8,32,192]{2,1,0:T(8,128)(2,1)} %broadcast_in_dim.49), calls=%async_computation.1 | async-start | bytes 262144 | tf_op jit(solution)/shard_map/all_to_all | solution.py:25
  35.1 5.3 %copy-start.8 = (bf16[1536,192]{0,1:T(8,128)(2,1)S(1)}, bf16[1536,192]{0,1:T(8,128)(2,1)}, u32[]{:S(2)}) copy-start(bf16[1536,192]{0,1:T(8,128)(2,1)} %param.27) | copy-start | bytes 1769476
  39.0 8.5 %copy-start.10 = (s32[14]{0:T(128)S(1)}, s32[14]{0:T(128)}, u32[]{:S(2)}) copy-start(s32[14]{0:T(128)} %param.26) | copy-start | bytes 172
  43.3 11.4 %all-to-all-start.2 = ((bf16[16,32,256]{2,1,0:T(8,128)(2,1)}), bf16[16,32,256]{2,1,0:T(8,128)(2,1)S(1)}, u32[]{:S(2)}, u32[]{:S(2)}) async-start(bf16[16,32,256]{2,1,0:T(8,128)(2,1)} %bitcast.115), calls=%async_computation.2 | async-start | bytes 524288 | tf_op jit(solution)/shard_map/all_to_all | solution.py:33
  55.6 17.1 %all-to-all-start.3 = ((bf16[16,32,256]{2,1,0:T(8,128)(2,1)}), bf16[16,32,256]{2,1,0:T(8,128)(2,1)S(1)}, u32[]{:S(2)}, u32[]{:S(2)}) async-start(bf16[16,32,256]{2,1,0:T(8,128)(2,1)} %broadcast_in_dim.52), calls=%async_computation.3 | async-start | bytes 524288 | tf_op jit(solution)/shard_map/all_to_all | solution.py:25
  63.8 4.1 %copy-start.12 = (s32[64,4]{0,1:T(4,128)S(1)}, s32[64,4]{0,1:T(4,128)}, u32[]{:S(2)}) copy-start(s32[64,4]{0,1:T(4,128)} %param.42) | copy-start | bytes 3076
  72.6 1.6 copy-start.2
  74.2 20.7 %copy-start.7 = (bf16[4096,128]{1,0:T(8,128)(2,1)S(1)}, bf16[4096,128]{1,0:T(8,128)(2,1)}, u32[]{:S(2)}) copy-start(bf16[4096,128]{1,0:T(8,128)(2,1)} %param.37) | copy-start | bytes 3145732
  75.4 14.8 %all-to-all-start.4 = ((bf16[32,32,128]{2,1,0:T(8,128)(2,1)}), bf16[32,32,128]{2,1,0:T(8,128)(2,1)S(1)}, u32[]{:S(2)}, u32[]{:S(2)}) async-start(bf16[32,32,128]{2,1,0:T(8,128)(2,1)} %bitcast.125), calls=%async_computation.4 | async-start | bytes 524288 | tf_op jit(solution)/shard_map/all_to_all | solution.py:33
  91.1 12.8 %all-to-all-start.5 = ((bf16[32,32,128]{2,1,0:T(8,128)(2,1)}), bf16[32,32,128]{2,1,0:T(8,128)(2,1)S(1)}, u32[]{:S(2)}, u32[]{:S(2)}) async-start(bf16[32,32,128]{2,1,0:T(8,128)(2,1)} %broadcast_in_dim.55), calls=%async_computation.5 | async-start | bytes 524288 | tf_op jit(solution)/shard_map/all_to_all | solution.py:25
  94.9 3.6 %copy-start.13 = (s32[64,2]{0,1:T(2,128)S(1)}, s32[64,2]{0,1:T(2,128)}, u32[]{:S(2)}) copy-start(s32[64,2]{0,1:T(2,128)} %param.43) | copy-start | bytes 1540
  107.6 15.2 %all-to-all-start.6 = ((bf16[64,2,1024]{2,1,0:T(2,128)(2,1)}), bf16[64,2,1024]{2,1,0:T(2,128)(2,1)S(1)}, u32[]{:S(2)}, u32[]{:S(2)}) async-start(bf16[64,2,1024]{2,1,0:T(2,128)(2,1)} %reshape.150), calls=%async_computation.6 | async-start | bytes 524288 | tf_op jit(solution)/shard_map/all_to_all | solution.py:33
  157.4 21.4 %copy-start.4 = (bf16[4096,128]{0,1:T(8,128)(2,1)S(1)}, bf16[4096,128]{0,1:T(8,128)(2,1)}, u32[]{:S(2)}) copy-start(bf16[4096,128]{0,1:T(8,128)(2,1)} %get-tuple-element.10) | copy-start | bytes 3145732
  178.7 13.1 %copy-start.6 = (bf16[4096,128]{1,0:T(8,128)(2,1)S(1)}, bf16[4096,128]{1,0:T(8,128)(2,1)}, u32[]{:S(2)}) copy-start(bf16[4096,128]{1,0:T(8,128)(2,1)} %param.33) | copy-start | bytes 3145732
  178.8 26.1 %copy-start.1 = (bf16[4096,256]{0,1:T(8,128)(2,1)S(1)}, bf16[4096,256]{0,1:T(8,128)(2,1)}, u32[]{:S(2)}) copy-start(bf16[4096,256]{0,1:T(8,128)(2,1)} %get-tuple-element.8) | copy-start | bytes 6291460
  192.2 23.3 %copy-start.5 = (bf16[4096,256]{1,0:T(8,128)(2,1)S(1)}, bf16[4096,256]{1,0:T(8,128)(2,1)}, u32[]{:S(2)}) copy-start(bf16[4096,256]{1,0:T(8,128)(2,1)} %param.32) | copy-start | bytes 6291460
  215.5 11.2 %copy-start.3 = (bf16[4096,192]{0,1:T(8,128)(2,1)S(1)}, bf16[4096,192]{0,1:T(8,128)(2,1)}, u32[]{:S(2)}) copy-start(bf16[4096,192]{0,1:T(8,128)(2,1)} %get-tuple-element.6) | copy-start | bytes 4718596
  216.0 20.0 %copy-start.9 = (bf16[1536,192]{0,1:T(8,128)(2,1)S(1)}, bf16[1536,192]{0,1:T(8,128)(2,1)}, u32[]{:S(2)}) copy-start(bf16[1536,192]{0,1:T(8,128)(2,1)} %param.28) | copy-start | bytes 1769476

commit v2 on v1

v2 whole, which is shorter than its diff:
```python
import functools

import jax
import jax.numpy as jnp
from jax import lax
from jax.experimental import pallas as pl
from jax.experimental.pallas import tpu as pltpu
from jax.sharding import Mesh, PartitionSpec as P

EVERY = ("z1", "z0", "y1", "y0", "x", "c")
LEAVES = ("z1", "z0", "y1", "y0")
CHIPS = {
    0: ("x",),
    1: ("y0", "x"),
    2: ("y1", "y0", "x"),
    3: ("z0", "y1", "y0", "x"),
    4: ("z1", "z0", "y1", "y0", "x"),
}
MEMBERS = {0: 4, 1: 8, 2: 16, 3: 32, 4: 64}
FIRST = ("lower0", "down1")
SECOND = ("lower1", "down2", "lower2", "down3")
THIRD = ("lower3", "upper3", "back3", "upper2")
FOURTH = ("back2", "upper1", "back1", "upper0")
HALF = 16
SEP = 4096
BLOCK = 64
LEAF = 192
WIDTHS = {0: 192, 1: 256, 2: 128, 3: 64}
FIRST_NODE = {1: 0, 2: 8, 3: 12}
F32 = jnp.float32
BF16 = jnp.bfloat16
VMEM_SPEC = pl.BlockSpec(memory_space=pltpu.VMEM)
SMEM_SPEC = pl.BlockSpec(memory_space=pltpu.SMEM)


def swap(value):
    return lax.ppermute(value, "c", [(0, 1), (1, 0)])


def exchange(value, level):
    return lax.all_to_all(value, CHIPS[level], split_axis=0, concat_axis=0, tiled=True)


def call(body, name, outs, operands, live=None, scratch=()):
    scalars = () if live is None else (live,)
    return pl.pallas_call(
        body,
        name=name,
        out_shape=[jax.ShapeDtypeStruct(shape, dtype) for shape, dtype in outs],
        in_specs=[SMEM_SPEC] * len(scalars) + [VMEM_SPEC] * len(operands),
        out_specs=[VMEM_SPEC] * len(outs),
        scratch_shapes=list(scratch),
        compiler_params=pltpu.CompilerParams(vmem_limit_bytes=12 * 1024 * 1024),
    )(*scalars, *operands)


def dot(left, right):
    return jnp.dot(left, right, preferred_element_type=F32)


def lanes(shape):
    return lax.broadcasted_iota(jnp.int32, shape, len(shape) - 1)


def rows_of(shape):
    return lax.broadcasted_iota(jnp.int32, shape, 0)


def one_hot(matches):
    return jnp.where(matches, 1.0, 0.0).astype(BF16)


def dot_turned(left, right):
    return lax.dot_general(left, right, (((1,), (1,)), ((), ())), preferred_element_type=F32)


def core_index():
    return lax.axis_index("c")


def source_and_turn(order):
    source = (order * 6554) >> 15
    return source, order - source * 5


def in_order(own, other):
    core = core_index()
    first = jnp.where(core == 0, own, other)
    second = jnp.where(core == 0, other, own)
    return jnp.concatenate([first, second], axis=1)


def chip_mask(masks, level):
    start = {1: 0, 2: 512, 3: 768}[level]
    return masks[0:1, start : start + 2 * WIDTHS[level]]


def piece_masks(masks, level):
    width = WIDTHS[level]
    whole = chip_mask(masks, level)
    core = core_index()
    first = whole[:, :width]
    second = whole[:, width:]
    return jnp.where(core == 0, first, second), jnp.where(core == 0, second, first)


def pattern_rows(patterns, level):
    start = {1: 0, 2: 3, 3: 7}[level]
    count = {1: 3, 2: 4, 3: 2}[level]
    return [patterns[start + row : start + row + 1, :].astype(F32) for row in range(count)]


def pick_kernel(send_order, owner_order, right, mine, theirs):
    core = core_index()
    send = send_order[...].reshape(1, 640)
    owner = owner_order[...].reshape(1, 640)
    natural = dot(right[...], one_hot(rows_of((640, 640)) == send)).astype(BF16)
    lane = lanes((1, 1024))
    turn = lane & 7
    wanted = (((lane >> 3) & 15) * 8 + (lane >> 7)) * 5 + turn
    wanted = jnp.where(turn < 5, wanted, -1)
    picked = dot(natural, one_hot(rows_of((640, 1024)) == wanted))
    source, turn = source_and_turn(owner)
    high = jnp.broadcast_to(source[:, :256].astype(F32), (8, 256))
    low = jnp.broadcast_to(turn[:, :256].astype(F32), (8, 256))
    high_left = pltpu.roll(high, 192, 1)[:, :128]
    low_left = pltpu.roll(low, 192, 1)[:, :128]
    high_right = pltpu.roll(high, 64, 1)[:, :128]
    main_high = jnp.where(core == 0, high[:, :128], high_left)
    main_low = jnp.where(core == 0, low[:, :128], low_left)
    lane = lanes((8, 128))
    tail = jnp.where(
        core == 0,
        jnp.where(lane < 64, high[:, 128:], low_left),
        jnp.where(lane < 64, low[:, :128], high_right),
    )
    row = rows_of((8, 128))
    info = jnp.where(row == 5, main_high, 0.0)
    info = jnp.where(row == 6, main_low, info)
    info = jnp.where(row == 7, tail, info)
    tiles = []
    for half in range(2):
        part = picked[half * HALF : (half + 1) * HALF]
        stacked = jnp.concatenate([part[:, f * 128 : (f + 1) * 128] for f in range(8)], axis=0)
        tiles.append(stacked.T.reshape(16, 8, 128) + info[None])
    mine[...] = jnp.where(core == 0, tiles[0], tiles[1]).astype(BF16)
    theirs[...] = jnp.where(core == 0, tiles[1], tiles[0]).astype(BF16)


def pack_kernel(mine, other, out):
    core = core_index()
    own = mine[...].astype(F32)
    far = other[...].astype(F32)
    first = jnp.where(core == 0, own, far)
    second = jnp.where(core == 0, far, own)
    tiles = jnp.concatenate([first, second], axis=1).astype(BF16)
    for copy in range(4):
        out[:, copy] = tiles


def table_kernel(live, send_order, first, second, third, wide, masks, columns):
    hot = one_hot(lanes((BLOCK, SEP)) // BLOCK == rows_of((BLOCK, SEP)))
    start = 0
    wide[...] = jnp.zeros_like(wide)
    for pattern in (first, second, third):
        count = pattern.shape[0]
        wide[start : start + count, :] = dot(
            pattern[...].astype(F32).astype(BF16), hot
        ).astype(BF16)
        start += count
    leaf = lax.axis_index(LEAVES)
    chip = lax.axis_index("x")
    for level, start in ((1, 0), (2, 512), (3, 768)):
        width = 2 * WIDTHS[level]
        member = leaf & (2**level - 1)
        row = (member * 4 + chip) * width + lanes((8, width))
        count = live[FIRST_NODE[level] + (leaf >> level)]
        masks[:, start : start + width] = (row < count).astype(F32)
    lane = lanes((1, 1024))
    turn = lane & 7
    wanted = jnp.where(turn < 5, (lane >> 3) * 5 + turn, -1)
    hot = one_hot(rows_of((640, 1024)) == wanted)
    send = send_order[...].reshape(1, 640) + 1
    stacked = jnp.concatenate(
        [
            jnp.broadcast_to(digit.astype(F32), (8, 640))
            for digit in (send >> 3, send & 7)
        ],
        axis=0,
    )
    placed = dot(stacked.astype(BF16), hot)
    columns[...] = (placed[:8] * 8.0 + placed[8:]).astype(jnp.int32) - 1


def stack_blocks(piece, count):
    block = lanes(piece.shape) // BLOCK
    zero = jnp.zeros_like(piece)
    return jnp.concatenate(
        [jnp.where(block == index, piece, zero) for index in range(count)], axis=0
    ).astype(BF16)


def masked_sum(product, rows):
    total = None
    for index, row in enumerate(rows):
        part = product[index * HALF : (index + 1) * HALF] * row
        total = part if total is None else total + part
    return total


def store_columns(out, value):
    width = out.shape[2]
    value = value.astype(BF16)
    for index in range(out.shape[0]):
        out[index] = value[:, index * width : (index + 1) * width]


def down_product(level, pieces, links, patterns, out):
    total = None
    for piece, link, pattern in zip(pieces, links, patterns):
        rows = pattern_rows(pattern, level)
        stack = stack_blocks(piece, len(rows))
        product = dot(stack, link[...]) if level == 1 else dot_turned(stack, link[...])
        part = masked_sum(product, rows)
        total = part if total is None else total + part
    store_columns(out, total)


def apply_factor(full, factor):
    if factor.shape[0] < full.shape[1]:
        return dot_turned(full, factor[...])
    return dot(full, factor[...])


def back_product(level, full, link, pattern):
    rows = pattern_rows(pattern, level)
    stacked = jnp.concatenate([full * row for row in rows], axis=0).astype(BF16)
    product = apply_factor(stacked, link)
    block = lanes((HALF, product.shape[1])) // BLOCK
    total = product[:HALF]
    for index in range(1, len(rows)):
        part = product[index * HALF : (index + 1) * HALF]
        total = jnp.where(block == index, part, total)
    return total


def store_copies(out, value):
    value = value.astype(BF16)
    for index in range(out.shape[0]):
        out[index] = value


def joined(gathered):
    return jnp.concatenate([gathered[index] for index in range(gathered.shape[0])], axis=1)


def in_kernel(
    received, own_pattern, other_pattern, own_lower, other_lower, own_link, other_link,
    own_out, other_out, rows_out, out, turned,
):
    flat = received[...].reshape(1024, 128)
    turned[...] = flat.astype(F32).T.astype(BF16)
    info = received[pl.ds(lax.axis_index(LEAVES) * 4, 4)].astype(F32)
    rows = rows_of((1024, 128))
    lane = lanes((1, 128))
    fronts = []
    for chip in range(4):
        tile = info[chip]
        tails = (tile[7:8, :], tile[15:16, :])
        tail_high = jnp.where(lane < 64, tails[0], tails[1])
        tail_low = jnp.broadcast_to(jnp.where(lane < 64, tails[1], tails[0]), (8, 128))
        tail_low = pltpu.roll(tail_low, 64, 1)[0:1, :]
        positions = (
            tile[5:6, :] * 8.0 + tile[6:7, :],
            tail_high * 8.0 + tail_low,
            tile[13:14, :] * 8.0 + tile[14:15, :],
        )
        hot = jnp.concatenate(
            [one_hot(rows == position.astype(jnp.int32)) for position in positions], axis=1
        )
        picked = dot(turned[chip * 32 : (chip + 1) * 32, :], hot)
        fronts.append(
            jnp.where(lanes((HALF, 384)) < LEAF, picked[:HALF], picked[HALF:]).astype(BF16)
        )
    start = pl.multiple_of(lax.axis_index("x") * 32, 32)
    rows_out[...] = turned[pl.ds(start, 32), :]
    front = jnp.concatenate(fronts, axis=1)
    own = apply_factor(front, own_lower).astype(BF16)
    other = apply_factor(front, other_lower).astype(BF16)
    own_out[...] = own
    other_out[...] = other
    pieces = (own.astype(F32), other.astype(F32))
    down_product(1, pieces, (own_link, other_link), (own_pattern, other_pattern), out)


def rest_kernel(turned, own_owner, other_owner, first_out, second_out, third_out):
    core = core_index()
    parts = []
    for owner, which in ((own_owner, core), (other_owner, 1 - core)):
        source, turn = source_and_turn(owner[...].reshape(1, 640))
        hot = one_hot(rows_of((1024, 640)) == source * 8 + turn)
        rows = turned[pl.ds(pl.multiple_of(which * HALF, HALF), HALF), :]
        parts.append(dot(rows, hot))
    offset = LEAF
    for out in (first_out, second_out, third_out):
        width = out.shape[1] // 2
        own, other = (part[:, offset : offset + width] for part in parts)
        out[...] = in_order(own, other).astype(BF16)
        offset += width


def reduce_kernel(level, received, right, masks, out):
    share = received[0].astype(F32)
    for index in range(1, received.shape[0]):
        share = share + received[index].astype(F32)
    store_copies(out, (right[...].astype(F32) - share) * chip_mask(masks, level))


def solve_pieces(level, gathered, masks, own_factor, other_factor):
    full = joined(gathered)
    own_mask, other_mask = piece_masks(masks, level)
    own = (apply_factor(full, own_factor) * own_mask).astype(BF16)
    other = (apply_factor(full, other_factor) * other_mask).astype(BF16)
    return own, other


def up_kernel(
    level, gathered, masks, own_pattern, other_pattern, own_lower, other_lower, own_link,
    other_link, own_out, other_out, out,
):
    own, other = solve_pieces(level, gathered, masks, own_lower, other_lower)
    own_out[...] = own
    other_out[...] = other
    pieces = (own.astype(F32), other.astype(F32))
    links = (own_link, other_link)
    down_product(level + 1, pieces, links, (own_pattern, other_pattern), out)


def solve_kernel(level, gathered, masks, own_factor, other_factor, own_out, other_out, out):
    own, other = solve_pieces(level, gathered, masks, own_factor, other_factor)
    own_out[...] = own
    other_out[...] = other
    store_copies(out, in_order(own.astype(F32), other.astype(F32)))


def back_kernel(
    level, gathered, masks, own_pattern, other_pattern, own_y, other_y, own_link, other_link, out
):
    full = joined(gathered).astype(F32)
    own = own_y[...].astype(F32) - back_product(level + 1, full, own_link, own_pattern)
    other = other_y[...].astype(F32) - back_product(level + 1, full, other_link, other_pattern)
    if level:
        own_mask, other_mask = piece_masks(masks, level)
        own = own * own_mask
        other = other * other_mask
    store_copies(out, in_order(own, other))


def out_kernel(
    gathered, own_owner, other_owner, own_first, other_first, own_second, other_second,
    own_third, other_third, own_upper, other_upper, out,
):
    core = core_index()
    full = joined(gathered)
    tails = ((own_first, own_second, own_third), (other_first, other_second, other_third))
    placed = []
    uppers = (own_upper, other_upper)
    for which, owner in enumerate((own_owner, other_owner)):
        source, turn = source_and_turn(owner[...].reshape(1, 640))
        slot = (source & 1) * 512 + (source >> 1) * 8 + turn
        hot = one_hot(rows_of((1024, 640)) == slot)
        leaf = apply_factor(full, uppers[which])
        front = jnp.concatenate([leaf] + [tail[...].astype(F32) for tail in tails[which]], axis=1)
        total = dot_turned(front.astype(BF16), hot)
        stacked = jnp.concatenate([total[:, :512], total[:, 512:]], axis=0)
        placed.append(stacked.T.reshape(64, 8, 32))
    first = jnp.where(core == 0, placed[0], placed[1])
    second = jnp.where(core == 0, placed[1], placed[0])
    out[:, :, :32] = jnp.concatenate([first, second], axis=1).astype(BF16)
    out[:, :, 32:] = jnp.zeros((64, 16, 96), BF16)


def final_kernel(received, own_columns, other_columns, own_out, other_out):
    core = core_index()
    turned = received[...].reshape(1024, 128).astype(F32).T
    first = turned[:HALF]
    second = turned[HALF : 2 * HALF]
    own = jnp.where(core == 0, first, second).astype(BF16)
    other = jnp.where(core == 0, second, first).astype(BF16)
    work = ((own, own_columns, own_out), (other, other_columns, other_out))
    for value, columns, out in work:
        hot = one_hot(rows_of((640, 1024)) == columns[0:1, :])
        out[...] = dot_turned(value, hot).astype(BF16)


def per_device(
    right_side,
    send_order,
    owner_order,
    live_rows,
    lower_leaf,
    upper_leaf,
    lower_first,
    lower_second,
    lower_third,
    upper_first,
    upper_second,
    upper_third,
    downlink_first,
    downlink_second,
    downlink_third,
    uplink_first,
    uplink_second,
    uplink_third,
    pattern_first,
    pattern_second,
    pattern_third,
):
    core = lax.axis_index("c")
    factors = {
        "lower0": lower_leaf.T,
        "down1": downlink_first.T,
        "lower1": lower_first,
        "down2": downlink_second,
        "lower2": lower_second,
        "down3": downlink_third,
        "lower3": lower_third.T,
        "upper3": upper_third.T,
        "back3": uplink_third,
        "upper2": upper_second,
        "back2": uplink_second,
        "upper1": upper_first,
        "back1": uplink_first.T,
        "upper0": upper_leaf.T,
    }
    pairs = {}

    def begin(value, names):
        tied = lax.optimization_barrier((value,) + tuple(factors[name] for name in names))
        for name, factor in zip(names, tied[1:]):
            pairs[name] = (factors[name], swap(factor))
        return tied[0]

    def finish(value, names):
        tied = lax.optimization_barrier((value,) + tuple(pairs[name][1] for name in names))
        for name, other in zip(names, tied[1:]):
            pairs[name] = (pairs[name][0], other)
        return tied[0]

    mine, theirs = call(
        pick_kernel,
        "pick_rows",
        [((16, 8, 128), BF16)] * 2,
        (send_order, owner_order, right_side),
    )
    theirs = begin(theirs, FIRST)
    own_patterns, masks, own_columns = call(
        table_kernel,
        "tables",
        [((16, SEP), BF16), ((8, 896), F32), ((8, 1024), jnp.int32)],
        (send_order, pattern_first.T, pattern_second.T, pattern_third.T),
        live=live_rows,
    )
    other_owner = swap(owner_order)
    other_columns = swap(own_columns)
    other_patterns = swap(own_patterns)
    payload = call(
        pack_kernel, "pack_rows", [((16, 4, 16, 128), BF16)], (mine, swap(theirs))
    )[0]
    payload, masks, other_owner, other_columns, other_patterns = lax.optimization_barrier(
        (payload, masks, other_owner, other_columns, other_patterns)
    )
    patterns = (own_patterns, other_patterns)
    payload = finish(payload, FIRST)
    payload = begin(payload, SECOND)
    received = exchange(payload.reshape(64, 16, 128), 4)
    own_y, other_y, own_rows, term = call(
        in_kernel,
        "leaf_front",
        [
            ((HALF, LEAF), BF16),
            ((HALF, LEAF), BF16),
            ((32, 1024), BF16),
            ((8, HALF, 512), BF16),
        ],
        (received,) + patterns + pairs["lower0"] + pairs["down1"],
        scratch=[pltpu.VMEM((128, 1024), BF16)],
    )
    level_y = {0: (own_y, other_y)}
    rights = call(
        rest_kernel,
        "separator_rows",
        [((HALF, 512), BF16), ((HALF, 256), BF16), ((HALF, 128), BF16)],
        (own_rows, owner_order, other_owner),
    )
    for level in (1, 2, 3):
        members = MEMBERS[level]
        chip_width = SEP // members
        piece = ((HALF, WIDTHS[level]), BF16)
        if level == 1:
            term, rights = lax.optimization_barrier((term, rights))
        shared = exchange(term, level)
        reduced = call(
            functools.partial(reduce_kernel, level),
            "reduce_%d" % level,
            [((members, HALF, chip_width), BF16)],
            (shared, rights[level - 1], masks),
        )[0]
        if level == 1:
            reduced = begin(finish(reduced, SECOND), THIRD)
        elif level == 2:
            reduced = begin(finish(reduced, THIRD), FOURTH)
        else:
            reduced = finish(reduced, FOURTH)
        gathered = exchange(reduced, level)
        if level < 3:
            above = MEMBERS[level + 1]
            own_y, other_y, term = call(
                functools.partial(up_kernel, level),
                "up_%d" % level,
                [piece, piece, ((above, HALF, SEP // above), BF16)],
                (gathered, masks)
                + patterns
                + pairs["lower%d" % level]
                + pairs["down%d" % (level + 1)],
            )
        else:
            own_y, other_y, copies = call(
                functools.partial(solve_kernel, level),
                "top_lower",
                [piece, piece, ((members, HALF, chip_width), BF16)],
                (gathered, masks) + pairs["lower3"],
            )
        level_y[level] = (own_y, other_y)
    level_x = {}
    for level in (3, 2, 1):
        members = MEMBERS[level]
        chip_width = SEP // members
        piece = ((HALF, WIDTHS[level]), BF16)
        gathered = exchange(copies, level)
        own_x, other_x, copies = call(
            functools.partial(solve_kernel, level),
            "solve_%d" % level,
            [piece, piece, ((members, HALF, chip_width), BF16)],
            (gathered, masks) + pairs["upper%d" % level],
        )
        level_x[level] = (own_x, other_x)
        gathered = exchange(copies, level)
        below = level - 1
        copies = call(
            functools.partial(back_kernel, below),
            "back_%d" % below,
            [((MEMBERS[below], HALF, 2 * WIDTHS[below]), BF16)],
            (gathered, masks) + patterns + level_y[below] + pairs["back%d" % level],
        )[0]
    gathered = exchange(copies, 0)
    outbound = call(
        out_kernel,
        "leaf_solution",
        [((64, 16, 128), BF16)],
        (gathered, owner_order, other_owner)
        + level_x[1]
        + level_x[2]
        + level_x[3]
        + pairs["upper0"],
    )[0]
    returned = exchange(outbound, 4)
    own_half, other_half = call(
        final_kernel,
        "natural_order",
        [((HALF, 640), BF16), ((HALF, 640), BF16)],
        (returned, own_columns, other_columns),
    )
    far_half = swap(other_half)
    return jnp.where(
        core == 0,
        jnp.concatenate([own_half, far_half]),
        jnp.concatenate([far_half, own_half]),
    )


def solution(mesh):
    fine = Mesh(mesh.devices.reshape(2, 2, 2, 2, 4, 2), EVERY)
    by_column = P(None, EVERY)
    placed = (by_column, P(EVERY), P(EVERY), P()) + (by_column,) * 17
    return jax.shard_map(
        per_device, mesh=fine, in_specs=placed, out_specs=by_column, check_vma=False
    )
```

time: 264 us -> 211 us (0.80)
  blocking collectives: 112 us -> 158 us
  local copies, waits for them, and re-layouts: 47.2 us -> 8.06 us
  waiting for transfers between devices: 37 us -> 2.74 us
  other arithmetic: 16.5 us -> 0.63 us
  Pallas kernels: 0 us -> 14.9 us
  starting transfers between devices: 38.8 us -> 25.7 us
  matrix products: 10.2 us -> 0 us
    all_to_all x9 -> x15, blocking collectives: 112 us -> 158 us  [exchange(): lax.all_to_all(value, CHIPS[level], split_axis=0, concat_axis=0, tiled=True)]
    all_to_all x7 -> x0, starting transfers between devices: 38.8 us -> none  [the longest x3 15.5 us: reduce_group(): lax.all_to_all(split, axes, split_axis=0, concat_axis=0, tiled=True)]
    all_to_all x7 -> x0, waiting for transfers between devices: 37 us -> none  [the longest x3 23.5 us: reduce_group(): lax.all_to_all(split, axes, split_axis=0, concat_axis=0, tiled=True)]
    ppermute x0 -> x19, starting transfers between devices: none -> 25.7 us  [swap(): return lax.ppermute(value, 'c', [(0, 1), (1, 0)])]
    pallas_call x0 -> x19, Pallas kernels: none -> 14.9 us  [call(): pl.pallas_call(body, name=name, out_shape=[jax.ShapeDtypeStruct(shape, dt...]
    unnamed x41 -> x46, local copies, waits for them, and re-layouts: 20.1 us -> 8.06 us
    mul x3 -> x0, other arithmetic: 11 us -> none  [the longest x2 7.16 us: per_device(): back = backs[level] * expanded[level]]
    dot_general x14 -> x0, matrix products: 10.2 us -> none  [the longest x3 3.28 us: per_device(): jnp.dot(reduced_full, lowers[level - 1], preferred_element_type=jnp.float32)]
  transfers between devices with their start and end apart: 7 -> 19, of which waited for: 6 -> 3; matrix products, arithmetic and copies ran while one was open for 10% -> 0% of each run, Pallas kernels for 0% -> 3%
where the time goes in v2:
time: 211 us; the launch traced here: 210 us
  blocking collectives  158 us (75%)
  starting transfers between devices  25.7 us (12%)
  Pallas kernels  14.9 us (7%)
  local copies, waits for them, and re-layouts  8.06 us (4%)
  waiting for transfers between devices  2.74 us (1%)
    all_to_all x15, blocking collectives, exchange(): lax.all_to_all(value, CHIPS[level], split_axis=0, concat_axis=0, tiled=True)  158 us
    ppermute x19, starting transfers between devices, swap(): return lax.ppermute(value, 'c', [(0, 1), (1, 0)])  25.7 us
    pallas_call x19, Pallas kernels, call(): pl.pallas_call(body, name=name, out_shape=[jax.ShapeDtypeStruct(shape, dt...  14.9 us
    unnamed x46, local copies, waits for them, and re-layouts  8.06 us
  transfers between devices with their start and end apart: 19, of which 3 were waited for; matrix products, arithmetic and copies ran while one was open for 0% of the time, Pallas kernels for 3%

profile of v2, /device:TPU:1, one launch (start us, length us, event | category | flops | bytes accessed | tf_op | source)
XLA Modules:
  0.0 210.0 jit_solution(3460052548352070698)
XLA Ops:
  2.8 1.5 collective-permute-start.5
  13.1 21.3 %all_to_all.75.received = bf16[64,16,128]{2,1,0:T(8,128)(2,1)S(1)} all-to-all(bf16[64,16,128]{2,1,0:T(8,128)(2,1)S(1)} %bitcast.14), channel_id=1, replica_groups=mesh['z1'=2,'z0'=2,'y1'=2,'y0'=2,'x'=4,'c'=2] {'z1','z0','y1','y0','x'}, dimensions={0} | all-to-all | bytes 524288 | tf_op jit(solution)/shard_map/all_to_all | solution.py:41
  34.5 1.4 copy-done.5
  36.9 2.0 leaf_front.1
  39.5 7.8 %all_to_all.76.received = bf16[8,16,512]{2,1,0:T(8,128)(2,1)S(1)} all-to-all(bf16[8,16,512]{2,1,0:T(8,128)(2,1)S(1)} %get-tuple-element.100), channel_id=1, replica_groups=mesh['z1'=2,'z0'=2,'y1'=2,'y0'=2,'x'=4,'c'=2] {'y0','x'}, dimensions={0} | all-to-all | bytes 262144 | tf_op jit(solution)/shard_map/all_to_all | solution.py:41
  47.4 2.6 %collective-permute-start.12 = (bf16[4096,128]{1,0:T(8,128)(2,1)S(1)}, bf16[4096,128]{1,0:T(8,128)(2,1)S(1)}, u32[]{:S(2)}, u32[]{:S(2)}) collective-permute-start(bf16[4096,128]{1,0:T(8,128)(2,1)S(1)} %copy-done.6), channel_id=1, source_target_pairs={{0,1},{1,0},{2,3},{3,2},{4,5},{5,4},{6,7},{7,6},{8,9},{9,8},{10,11... | collective-permute-start | bytes 3145736 | tf_op jit(solution)/shard_map/ppermute | solution.py:37
  50.6 7.8 %all_to_all.77.gathered = bf16[8,16,512]{2,1,0:T(8,128)(2,1)S(1)} all-to-all(bf16[8,16,512]{2,1,0:T(8,128)(2,1)S(1)} %reduce_1.1), channel_id=1, replica_groups=mesh['z1'=2,'z0'=2,'y1'=2,'y0'=2,'x'=4,'c'=2] {'y0','x'}, dimensions={0} | all-to-all | bytes 262144 | tf_op jit(solution)/shard_map/all_to_all | solution.py:41
  58.5 2.0 up_1.1
  60.5 10.5 %all_to_all.78.received = bf16[16,16,256]{2,1,0:T(8,128)(2,1)S(1)} all-to-all(bf16[16,16,256]{2,1,0:T(8,128)(2,1)S(1)} %get-tuple-element.111), channel_id=1, replica_groups=mesh['z1'=2,'z0'=2,'y1'=2,'y0'=2,'x'=4,'c'=2] {'y1','y0','x'}, dimensions={0} | all-to-all | bytes 262144 | tf_op jit(solution)/shard_map/all_to_all | solution.py:41
  71.1 3.1 %collective-permute-start.14 = (bf16[4096,256]{1,0:T(8,128)(2,1)S(1)}, bf16[4096,256]{1,0:T(8,128)(2,1)S(1)}, u32[]{:S(2)}, u32[]{:S(2)}) collective-permute-start(bf16[4096,256]{1,0:T(8,128)(2,1)S(1)} %copy-done.3), channel_id=1, source_target_pairs={{0,1},{1,0},{2,3},{3,2},{4,5},{5,4},{6,7},{7,6},{8,9},{9,8},{10,11... | collective-permute-start | bytes 6291464 | tf_op jit(solution)/shard_map/ppermute | solution.py:37
  74.8 9.6 %all_to_all.79.gathered = bf16[16,16,256]{2,1,0:T(8,128)(2,1)S(1)} all-to-all(bf16[16,16,256]{2,1,0:T(8,128)(2,1)S(1)} %reduce_2.1), channel_id=1, replica_groups=mesh['z1'=2,'z0'=2,'y1'=2,'y0'=2,'x'=4,'c'=2] {'y1','y0','x'}, dimensions={0} | all-to-all | bytes 262144 | tf_op jit(solution)/shard_map/all_to_all | solution.py:41
  85.5 10.9 %all_to_all.80.received = bf16[32,16,128]{2,1,0:T(8,128)(2,1)S(1)} all-to-all(bf16[32,16,128]{2,1,0:T(8,128)(2,1)S(1)} %get-tuple-element.121), channel_id=1, replica_groups=mesh['z1'=2,'z0'=2,'y1'=2,'y0'=2,'x'=4,'c'=2] {'z0','y1','y0','x'}, dimensions={0} | all-to-all | bytes 262144 | tf_op jit(solution)/shard_map/all_to_all | solution.py:41
  96.6 10.7 %all_to_all.81.gathered = bf16[32,16,128]{2,1,0:T(8,128)(2,1)S(1)} all-to-all(bf16[32,16,128]{2,1,0:T(8,128)(2,1)S(1)} %reduce_3.1), channel_id=1, replica_groups=mesh['z1'=2,'z0'=2,'y1'=2,'y0'=2,'x'=4,'c'=2] {'z0','y1','y0','x'}, dimensions={0} | all-to-all | bytes 262144 | tf_op jit(solution)/shard_map/all_to_all | solution.py:41
  108.3 10.7 %all_to_all.82.gathered = bf16[32,16,128]{2,1,0:T(8,128)(2,1)S(1)} all-to-all(bf16[32,16,128]{2,1,0:T(8,128)(2,1)S(1)} %get-tuple-element.129), channel_id=1, replica_groups=mesh['z1'=2,'z0'=2,'y1'=2,'y0'=2,'x'=4,'c'=2] {'z0','y1','y0','x'}, dimensions={0} | all-to-all | bytes 262144 | tf_op jit(solution)/shard_map/all_to_all | solution.py:41
  119.5 10.7 %all_to_all.83.gathered = bf16[32,16,128]{2,1,0:T(8,128)(2,1)S(1)} all-to-all(bf16[32,16,128]{2,1,0:T(8,128)(2,1)S(1)} %get-tuple-element.131), channel_id=1, replica_groups=mesh['z1'=2,'z0'=2,'y1'=2,'y0'=2,'x'=4,'c'=2] {'z0','y1','y0','x'}, dimensions={0} | all-to-all | bytes 262144 | tf_op jit(solution)/shard_map/all_to_all | solution.py:41
  130.7 10.0 %all_to_all.84.gathered = bf16[16,16,256]{2,1,0:T(8,128)(2,1)S(1)} all-to-all(bf16[16,16,256]{2,1,0:T(8,128)(2,1)S(1)} %back_2.1), channel_id=1, replica_groups=mesh['z1'=2,'z0'=2,'y1'=2,'y0'=2,'x'=4,'c'=2] {'y1','y0','x'}, dimensions={0} | all-to-all | bytes 262144 | tf_op jit(solution)/shard_map/all_to_all | solution.py:41
  141.0 9.6 %all_to_all.85.gathered = bf16[16,16,256]{2,1,0:T(8,128)(2,1)S(1)} all-to-all(bf16[16,16,256]{2,1,0:T(8,128)(2,1)S(1)} %get-tuple-element.136), channel_id=1, replica_groups=mesh['z1'=2,'z0'=2,'y1'=2,'y0'=2,'x'=4,'c'=2] {'y1','y0','x'}, dimensions={0} | all-to-all | bytes 262144 | tf_op jit(solution)/shard_map/all_to_all | solution.py:41
  151.5 8.2 %all_to_all.86.gathered = bf16[8,16,512]{2,1,0:T(8,128)(2,1)S(1)} all-to-all(bf16[8,16,512]{2,1,0:T(8,128)(2,1)S(1)} %back_1.1), channel_id=1, replica_groups=mesh['z1'=2,'z0'=2,'y1'=2,'y0'=2,'x'=4,'c'=2] {'y0','x'}, dimensions={0} | all-to-all | bytes 262144 | tf_op jit(solution)/shard_map/all_to_all | solution.py:41
  160.4 7.8 %all_to_all.87.gathered = bf16[8,16,512]{2,1,0:T(8,128)(2,1)S(1)} all-to-all(bf16[8,16,512]{2,1,0:T(8,128)(2,1)S(1)} %get-tuple-element.141), channel_id=1, replica_groups=mesh['z1'=2,'z0'=2,'y1'=2,'y0'=2,'x'=4,'c'=2] {'y0','x'}, dimensions={0} | all-to-all | bytes 262144 | tf_op jit(solution)/shard_map/all_to_all | solution.py:41
  168.2 1.2 back_0.1
  169.4 6.7 %all_to_all.88.gathered = bf16[4,16,384]{2,1,0:T(8,128)(2,1)S(1)} all-to-all(bf16[4,16,384]{2,1,0:T(8,128)(2,1)S(1)} %back_0.1), channel_id=1, replica_groups=mesh['z1'=2,'z0'=2,'y1'=2,'y0'=2,'x'=4,'c'=2] {'x'}, dimensions={0} | all-to-all | bytes 98304 | tf_op jit(solution)/shard_map/all_to_all | solution.py:41
  176.2 1.6 leaf_solution.1
  177.8 15.0 %all_to_all.89.received = bf16[64,16,128]{2,1,0:T(8,128)(2,1)S(1)} all-to-all(bf16[64,16,128]{2,1,0:T(8,128)(2,1)S(1)} %leaf_solution.1), channel_id=1, replica_groups=mesh['z1'=2,'z0'=2,'y1'=2,'y0'=2,'x'=4,'c'=2] {'z1','z0','y1','y0','x'}, dimensions={0} | all-to-all | bytes 524288 | tf_op jit(solution)/shard_map/all_to_all | solution.py:41
  193.6 14.9 %collective-permute-start.18 = (bf16[16,640]{1,0:T(8,128)(2,1)S(1)}, bf16[16,640]{1,0:T(8,128)(2,1)S(1)}, u32[]{:S(2)}, u32[]{:S(2)}) collective-permute-start(bf16[16,640]{1,0:T(8,128)(2,1)S(1)} %get-tuple-element.154), channel_id=1, source_target_pairs={{0,1},{1,0},{2,3},{3,2},{4,5},{5,4},{6,7},{7,6},{8,9},{9,8},{10,11... | collective-permute-start | bytes 61448 | tf_op jit(solution)/shard_map/ppermute | solution.py:37
  (95 shorter events, 21.8 us)
Async XLA Ops:
  2.8 9.2 %collective-permute-start.5 = (bf16[192,4096]{1,0:T(8,128)(2,1)}, bf16[192,4096]{1,0:T(8,128)(2,1)S(1)}, u32[]{:S(2)}, u32[]{:S(2)}) collective-permute-start(bf16[192,4096]{1,0:T(8,128)(2,1)} %bitcast.12), channel_id=1, source_target_pairs={{0,1},{1,0},{2,3},{3,2},{4,5},{5,4},{6,7},{7,6},{8,9},{9,8},{10,11... | collective-permute-start | bytes 4718600 | tf_op jit(solution)/shard_map/ppermute | solution.py:37
  4.3 7.7 %collective-permute-start.4 = (bf16[192,1536]{1,0:T(8,128)(2,1)}, bf16[192,1536]{1,0:T(8,128)(2,1)S(1)}, u32[]{:S(2)}, u32[]{:S(2)}) collective-permute-start(bf16[192,1536]{1,0:T(8,128)(2,1)} %bitcast.15), channel_id=1, source_target_pairs={{0,1},{1,0},{2,3},{3,2},{4,5},{5,4},{6,7},{7,6},{8,9},{9,8},{10,11... | collective-permute-start | bytes 1769480 | tf_op jit(solution)/shard_map/ppermute | solution.py:37
  8.9 3.1 %collective-permute-start.3 = (bf16[16,4096]{1,0:T(8,128)(2,1)S(1)}, bf16[16,4096]{1,0:T(8,128)(2,1)S(1)}, u32[]{:S(2)}, u32[]{:S(2)}) collective-permute-start(bf16[16,4096]{1,0:T(8,128)(2,1)S(1)} %get-tuple-element.85.own_pattern), channel_id=1, source_target_pairs={{0,1},{1,0},{2,3},{3,2},{4,5},{5,4},{6,7},{7,6},{8,9},{9,8},{10,11... | collective-permute-start | bytes 393224 | tf_op jit(solution)/shard_map/ppermute | solution.py:37
  9.4 1.2 collective-permute-start
  9.5 2.5 %collective-permute-start.2 = (s32[8,1024]{1,0:T(8,128)S(1)}, s32[8,1024]{1,0:T(8,128)S(1)}, u32[]{:S(2)}, u32[]{:S(2)}) collective-permute-start(s32[8,1024]{1,0:T(8,128)S(1)} %get-tuple-element.84.own_columns), channel_id=1, source_target_pairs={{0,1},{1,0},{2,3},{3,2},{4,5},{5,4},{6,7},{7,6},{8,9},{9,8},{10,11... | collective-permute-start | bytes 98312 | tf_op jit(solution)/shard_map/ppermute | solution.py:37
  10.6 1.4 collective-permute-start.1
  10.8 28.1 %copy-start.16 = (s32[640]{0:T(1024)S(1)}, s32[640]{0:T(1024)}, u32[]{:S(2)}) copy-start(s32[640]{0:T(1024)} %own_owner.3) | copy-start | bytes 7684
  12.0 35.3 %collective-permute-start.6 = (bf16[4096,256]{1,0:T(8,128)(2,1)}, bf16[4096,256]{1,0:T(8,128)(2,1)S(1)}, u32[]{:S(2)}, u32[]{:S(2)}) collective-permute-start(bf16[4096,256]{1,0:T(8,128)(2,1)} %own_lower.2), channel_id=1, source_target_pairs={{0,1},{1,0},{2,3},{3,2},{4,5},{5,4},{6,7},{7,6},{8,9},{9,8},{10,11... | collective-permute-start | bytes 6291464 | tf_op jit(solution)/shard_map/ppermute | solution.py:37
  12.3 35.1 %collective-permute-start.7 = (bf16[4096,256]{1,0:T(8,128)(2,1)}, bf16[4096,256]{1,0:T(8,128)(2,1)S(1)}, u32[]{:S(2)}, u32[]{:S(2)}) collective-permute-start(bf16[4096,256]{1,0:T(8,128)(2,1)} %own_link.4), channel_id=1, source_target_pairs={{0,1},{1,0},{2,3},{3,2},{4,5},{5,4},{6,7},{7,6},{8,9},{9,8},{10,11... | collective-permute-start | bytes 6291464 | tf_op jit(solution)/shard_map/ppermute | solution.py:37
  12.6 34.7 %collective-permute-start.8 = (bf16[4096,128]{1,0:T(8,128)(2,1)}, bf16[4096,128]{1,0:T(8,128)(2,1)S(1)}, u32[]{:S(2)}, u32[]{:S(2)}) collective-permute-start(bf16[4096,128]{1,0:T(8,128)(2,1)} %own_lower.3), channel_id=1, source_target_pairs={{0,1},{1,0},{2,3},{3,2},{4,5},{5,4},{6,7},{7,6},{8,9},{9,8},{10,11... | collective-permute-start | bytes 3145736 | tf_op jit(solution)/shard_map/ppermute | solution.py:37
  12.8 34.6 %collective-permute-start.9 = (bf16[4096,128]{1,0:T(8,128)(2,1)}, bf16[4096,128]{1,0:T(8,128)(2,1)S(1)}, u32[]{:S(2)}, u32[]{:S(2)}) collective-permute-start(bf16[4096,128]{1,0:T(8,128)(2,1)} %own_link.5), channel_id=1, source_target_pairs={{0,1},{1,0},{2,3},{3,2},{4,5},{5,4},{6,7},{7,6},{8,9},{9,8},{10,11... | collective-permute-start | bytes 3145736 | tf_op jit(solution)/shard_map/ppermute | solution.py:37
  13.1 37.0 %copy-start.12 = (bf16[4096,64]{0,1:T(8,128)(2,1)S(1)}, bf16[4096,64]{0,1:T(8,128)(2,1)}, u32[]{:S(2)}) copy-start(bf16[4096,64]{0,1:T(8,128)(2,1)} %param.29) | copy-start | bytes 1572868
  47.4 23.7 %collective-permute-start.12 = (bf16[4096,128]{1,0:T(8,128)(2,1)S(1)}, bf16[4096,128]{1,0:T(8,128)(2,1)S(1)}, u32[]{:S(2)}, u32[]{:S(2)}) collective-permute-start(bf16[4096,128]{1,0:T(8,128)(2,1)S(1)} %copy-done.6), channel_id=1, source_target_pairs={{0,1},{1,0},{2,3},{3,2},{4,5},{5,4},{6,7},{7,6},{8,9},{9,8},{10,11... | collective-permute-start | bytes 3145736 | tf_op jit(solution)/shard_map/ppermute | solution.py:37
  50.0 21.1 %collective-permute-start.13 = (bf16[4096,128]{1,0:T(8,128)(2,1)}, bf16[4096,128]{1,0:T(8,128)(2,1)S(1)}, u32[]{:S(2)}, u32[]{:S(2)}) collective-permute-start(bf16[4096,128]{1,0:T(8,128)(2,1)} %own_factor.2), channel_id=1, source_target_pairs={{0,1},{1,0},{2,3},{3,2},{4,5},{5,4},{6,7},{7,6},{8,9},{9,8},{10,11... | collective-permute-start | bytes 3145736 | tf_op jit(solution)/shard_map/ppermute | solution.py:37
  50.1 21.0 %collective-permute-start.10 = (bf16[64,4096]{1,0:T(8,128)(2,1)S(1)}, bf16[64,4096]{1,0:T(8,128)(2,1)S(1)}, u32[]{:S(2)}, u32[]{:S(2)}) collective-permute-start(bf16[64,4096]{1,0:T(8,128)(2,1)S(1)} %bitcast.19), channel_id=1, source_target_pairs={{0,1},{1,0},{2,3},{3,2},{4,5},{5,4},{6,7},{7,6},{8,9},{9,8},{10,11... | collective-permute-start | bytes 1572872 | tf_op jit(solution)/shard_map/ppermute | solution.py:37
  50.5 20.5 %collective-permute-start.11 = (bf16[64,4096]{1,0:T(8,128)(2,1)}, bf16[64,4096]{1,0:T(8,128)(2,1)S(1)}, u32[]{:S(2)}, u32[]{:S(2)}) collective-permute-start(bf16[64,4096]{1,0:T(8,128)(2,1)} %bitcast.21), channel_id=1, source_target_pairs={{0,1},{1,0},{2,3},{3,2},{4,5},{5,4},{6,7},{7,6},{8,9},{9,8},{10,11... | collective-permute-start | bytes 1572872 | tf_op jit(solution)/shard_map/ppermute | solution.py:37
  58.4 26.0 %copy-start.8 = (bf16[4096,128]{1,0:T(8,128)(2,1)S(1)}, bf16[4096,128]{1,0:T(8,128)(2,1)}, u32[]{:S(2)}) copy-start(bf16[4096,128]{1,0:T(8,128)(2,1)} %own_lower.3) | copy-start | bytes 3145732
  58.5 26.0 %copy-start.9 = (bf16[4096,128]{1,0:T(8,128)(2,1)S(1)}, bf16[4096,128]{1,0:T(8,128)(2,1)}, u32[]{:S(2)}) copy-start(bf16[4096,128]{1,0:T(8,128)(2,1)} %own_link.5) | copy-start | bytes 3145732
  71.1 25.5 %collective-permute-start.14 = (bf16[4096,256]{1,0:T(8,128)(2,1)S(1)}, bf16[4096,256]{1,0:T(8,128)(2,1)S(1)}, u32[]{:S(2)}, u32[]{:S(2)}) collective-permute-start(bf16[4096,256]{1,0:T(8,128)(2,1)S(1)} %copy-done.3), channel_id=1, source_target_pairs={{0,1},{1,0},{2,3},{3,2},{4,5},{5,4},{6,7},{7,6},{8,9},{9,8},{10,11... | collective-permute-start | bytes 6291464 | tf_op jit(solution)/shard_map/ppermute | solution.py:37
  74.2 22.4 %collective-permute-start.15 = (bf16[4096,256]{1,0:T(8,128)(2,1)S(1)}, bf16[4096,256]{1,0:T(8,128)(2,1)S(1)}, u32[]{:S(2)}, u32[]{:S(2)}) collective-permute-start(bf16[4096,256]{1,0:T(8,128)(2,1)S(1)} %copy-done.2), channel_id=1, source_target_pairs={{0,1},{1,0},{2,3},{3,2},{4,5},{5,4},{6,7},{7,6},{8,9},{9,8},{10,11... | collective-permute-start | bytes 6291464 | tf_op jit(solution)/shard_map/ppermute | solution.py:37
  74.3 22.3 %collective-permute-start.16 = (bf16[192,4096]{1,0:T(8,128)(2,1)S(1)}, bf16[192,4096]{1,0:T(8,128)(2,1)S(1)}, u32[]{:S(2)}, u32[]{:S(2)}) collective-permute-start(bf16[192,4096]{1,0:T(8,128)(2,1)S(1)} %bitcast.10), channel_id=1, source_target_pairs={{0,1},{1,0},{2,3},{3,2},{4,5},{5,4},{6,7},{7,6},{8,9},{9,8},{10,11... | collective-permute-start | bytes 4718600 | tf_op jit(solution)/shard_map/ppermute | solution.py:37
  74.7 21.8 %collective-permute-start.17 = (bf16[192,1536]{1,0:T(8,128)(2,1)S(1)}, bf16[192,1536]{1,0:T(8,128)(2,1)S(1)}, u32[]{:S(2)}, u32[]{:S(2)}) collective-permute-start(bf16[192,1536]{1,0:T(8,128)(2,1)S(1)} %bitcast.17), channel_id=1, source_target_pairs={{0,1},{1,0},{2,3},{3,2},{4,5},{5,4},{6,7},{7,6},{8,9},{9,8},{10,11... | collective-permute-start | bytes 1769480 | tf_op jit(solution)/shard_map/ppermute | solution.py:37
  85.5 33.5 %copy-start.13 = (bf16[4096,64]{0,1:T(8,128)(2,1)S(1)}, bf16[4096,64]{0,1:T(8,128)(2,1)}, u32[]{:S(2)}) copy-start(bf16[4096,64]{0,1:T(8,128)(2,1)} %param.32) | copy-start | bytes 1572868
  193.6 15.8 %collective-permute-start.18 = (bf16[16,640]{1,0:T(8,128)(2,1)S(1)}, bf16[16,640]{1,0:T(8,128)(2,1)S(1)}, u32[]{:S(2)}, u32[]{:S(2)}) collective-permute-start(bf16[16,640]{1,0:T(8,128)(2,1)S(1)} %get-tuple-element.154), channel_id=1, source_target_pairs={{0,1},{1,0},{2,3},{3,2},{4,5},{5,4},{6,7},{7,6},{8,9},{9,8},{10,11... | collective-permute-start | bytes 61448 | tf_op jit(solution)/shard_map/ppermute | solution.py:37
  (18 other events, 143.6 us)

commit v3 on v2

--- a/solution.py
+++ b/solution.py
@@ -17,8 +17,8 @@
     4: ("z1", "z0", "y1", "y0", "x"),
 }
 MEMBERS = {0: 4, 1: 8, 2: 16, 3: 32, 4: 64}
-FIRST = ("lower0", "down1")
-SECOND = ("lower1", "down2", "lower2", "down3")
+FIRST = ("lower0", "down1", "lower1", "down2")
+SECOND = ("lower2", "down3")
 THIRD = ("lower3", "upper3", "back3", "upper2")
 FOURTH = ("back2", "upper1", "back1", "upper0")
 HALF = 16
@@ -30,7 +30,7 @@
 F32 = jnp.float32
 BF16 = jnp.bfloat16
 VMEM_SPEC = pl.BlockSpec(memory_space=pltpu.VMEM)
-SMEM_SPEC = pl.BlockSpec(memory_space=pltpu.SMEM)
+HBM_SPEC = pl.BlockSpec(memory_space=pltpu.HBM)
 
 
 def swap(value):
@@ -41,17 +41,30 @@
     return lax.all_to_all(value, CHIPS[level], split_axis=0, concat_axis=0, tiled=True)
 
 
-def call(body, name, outs, operands, live=None, scratch=()):
-    scalars = () if live is None else (live,)
+def call(body, name, outs, operands, distant=(), scratch=()):
+    constrained = [pltpu.with_memory_space_constraint(value, pltpu.HBM) for value in distant]
+    scratch = list(scratch)
+    if distant:
+        scratch.append(pltpu.SemaphoreType.DMA((len(distant),)))
     return pl.pallas_call(
         body,
         name=name,
         out_shape=[jax.ShapeDtypeStruct(shape, dtype) for shape, dtype in outs],
-        in_specs=[SMEM_SPEC] * len(scalars) + [VMEM_SPEC] * len(operands),
+        in_specs=[HBM_SPEC] * len(distant) + [VMEM_SPEC] * len(operands),
         out_specs=[VMEM_SPEC] * len(outs),
-        scratch_shapes=list(scratch),
+        scratch_shapes=scratch,
         compiler_params=pltpu.CompilerParams(vmem_limit_bytes=12 * 1024 * 1024),
-    )(*scalars, *operands)
+    )(*constrained, *operands)
+
+
+def fetch(sources, buffers, semaphores):
+    copies = [
+        pltpu.make_async_copy(source, buffer, semaphores.at[index])
+        for index, (source, buffer) in enumerate(zip(sources, buffers))
+    ]
+    for copy in copies:
+        copy.start()
+    return copies
 
 
 def dot(left, right):
@@ -110,7 +123,7 @@
     return [patterns[start + row : start + row + 1, :].astype(F32) for row in range(count)]
 
 
-def pick_kernel(send_order, owner_order, right, mine, theirs):
+def pick_rows(send_order, owner_order, right, mine, theirs):
     core = core_index()
     send = send_order[...].reshape(1, 640)
     owner = owner_order[...].reshape(1, 640)
@@ -158,7 +171,7 @@
         out[:, copy] = tiles
 
 
-def table_kernel(live, send_order, first, second, third, wide, masks, columns):
+def make_tables(live, send_order, owner_order, first, second, third, wide, masks, columns):
     hot = one_hot(lanes((BLOCK, SEP)) // BLOCK == rows_of((BLOCK, SEP)))
     start = 0
     wide[...] = jnp.zeros_like(wide)
@@ -178,7 +191,8 @@
         masks[:, start : start + width] = (row < count).astype(F32)
     lane = lanes((1, 1024))
     turn = lane & 7
-    wanted = jnp.where(turn < 5, (lane >> 3) * 5 + turn, -1)
+    device = ((lane >> 3) & 63) * 2 + (lane >> 9)
+    wanted = jnp.where(turn < 5, device * 5 + turn, -1)
     hot = one_hot(rows_of((640, 1024)) == wanted)
     send = send_order[...].reshape(1, 640) + 1
     stacked = jnp.concatenate(
@@ -189,7 +203,30 @@
         axis=0,
     )
     placed = dot(stacked.astype(BF16), hot)
-    columns[...] = (placed[:8] * 8.0 + placed[8:]).astype(jnp.int32) - 1
+    row = rows_of((8, 1024))
+    owner = jnp.broadcast_to(owner_order[...].reshape(1, 640), (8, 640))
+    owner = jnp.concatenate([owner, jnp.zeros((8, 384), jnp.int32)], axis=1)
+    values = (placed[:8] * 8.0 + placed[8:]).astype(jnp.int32) - 1
+    columns[...] = jnp.where(row == 0, values, owner)
+
+
+def start_kernel(
+    live, send_order, owner_order, right, first, second, third, mine, theirs, wide, masks,
+    columns, live_buffer, send_buffer, owner_buffer, right_buffer, first_buffer, second_buffer,
+    third_buffer, semaphores,
+):
+    buffers = (
+        live_buffer, send_buffer, owner_buffer, right_buffer, first_buffer, second_buffer,
+        third_buffer,
+    )
+    sources = (live, send_order, owner_order, right, first, second, third)
+    for copy in fetch(sources, buffers, semaphores):
+        copy.wait()
+    pick_rows(send_buffer, owner_buffer, right_buffer, mine, theirs)
+    make_tables(
+        live_buffer, send_buffer, owner_buffer, first_buffer, second_buffer, third_buffer, wide,
+        masks, columns,
+    )
 
 
 def stack_blocks(piece, count):
@@ -255,9 +292,10 @@
 
 
 def in_kernel(
-    received, own_pattern, other_pattern, own_lower, other_lower, own_link, other_link,
-    own_out, other_out, rows_out, out, turned,
+    far_lower, far_link, received, own_pattern, other_pattern, other_lower, other_link,
+    own_out, other_out, rows_out, out, turned, own_lower, own_link, semaphores,
 ):
+    copies = fetch((far_lower, far_link), (own_lower, own_link), semaphores)
     flat = received[...].reshape(1024, 128)
     turned[...] = flat.astype(F32).T.astype(BF16)
     info = received[pl.ds(lax.axis_index(LEAVES) * 4, 4)].astype(F32)
@@ -285,11 +323,13 @@
     start = pl.multiple_of(lax.axis_index("x") * 32, 32)
     rows_out[...] = turned[pl.ds(start, 32), :]
     front = jnp.concatenate(fronts, axis=1)
+    copies[0].wait()
     own = apply_factor(front, own_lower).astype(BF16)
     other = apply_factor(front, other_lower).astype(BF16)
     own_out[...] = own
     other_out[...] = other
     pieces = (own.astype(F32), other.astype(F32))
+    copies[1].wait()
     down_product(1, pieces, (own_link, other_link), (own_pattern, other_pattern), out)
 
 
@@ -297,7 +337,7 @@
     core = core_index()
     parts = []
     for owner, which in ((own_owner, core), (other_owner, 1 - core)):
-        source, turn = source_and_turn(owner[...].reshape(1, 640))
+        source, turn = source_and_turn(owner[1:2, :640])
         hot = one_hot(rows_of((1024, 640)) == source * 8 + turn)
         rows = turned[pl.ds(pl.multiple_of(which * HALF, HALF), HALF), :]
         parts.append(dot(rows, hot))
@@ -366,25 +406,25 @@
     placed = []
     uppers = (own_upper, other_upper)
     for which, owner in enumerate((own_owner, other_owner)):
-        source, turn = source_and_turn(owner[...].reshape(1, 640))
+        source, turn = source_and_turn(owner[1:2, :640])
         slot = (source & 1) * 512 + (source >> 1) * 8 + turn
         hot = one_hot(rows_of((1024, 640)) == slot)
         leaf = apply_factor(full, uppers[which])
         front = jnp.concatenate([leaf] + [tail[...].astype(F32) for tail in tails[which]], axis=1)
         total = dot_turned(front.astype(BF16), hot)
-        stacked = jnp.concatenate([total[:, :512], total[:, 512:]], axis=0)
-        placed.append(stacked.T.reshape(64, 8, 32))
+        placed.append(jnp.concatenate([total[:, :512], total[:, 512:]], axis=0))
     first = jnp.where(core == 0, placed[0], placed[1])
     second = jnp.where(core == 0, placed[1], placed[0])
-    out[:, :, :32] = jnp.concatenate([first, second], axis=1).astype(BF16)
-    out[:, :, 32:] = jnp.zeros((64, 16, 96), BF16)
+    unused = jnp.zeros((64, 512), F32)
+    stacked = jnp.concatenate([first, second, unused], axis=0)
+    out[...] = stacked.T.reshape(64, 8, 128).astype(BF16)
 
 
 def final_kernel(received, own_columns, other_columns, own_out, other_out):
     core = core_index()
-    turned = received[...].reshape(1024, 128).astype(F32).T
-    first = turned[:HALF]
-    second = turned[HALF : 2 * HALF]
+    turned = received[...].reshape(512, 128).astype(F32).T
+    first = jnp.concatenate([turned[:HALF], turned[2 * HALF : 3 * HALF]], axis=1)
+    second = jnp.concatenate([turned[HALF : 2 * HALF], turned[3 * HALF : 4 * HALF]], axis=1)
     own = jnp.where(core == 0, first, second).astype(BF16)
     other = jnp.where(core == 0, second, first).astype(BF16)
     work = ((own, own_columns, own_out), (other, other_columns, other_out))
@@ -447,33 +487,47 @@
             pairs[name] = (pairs[name][0], other)
         return tied[0]
 
-    mine, theirs = call(
-        pick_kernel,
-        "pick_rows",
-        [((16, 8, 128), BF16)] * 2,
-        (send_order, owner_order, right_side),
-    )
-    theirs = begin(theirs, FIRST)
-    own_patterns, masks, own_columns = call(
-        table_kernel,
-        "tables",
-        [((16, SEP), BF16), ((8, 896), F32), ((8, 1024), jnp.int32)],
-        (send_order, pattern_first.T, pattern_second.T, pattern_third.T),
-        live=live_rows,
-    )
-    other_owner = swap(owner_order)
+    mine, theirs, own_patterns, masks, own_columns = call(
+        start_kernel,
+        "start",
+        [
+            ((16, 8, 128), BF16),
+            ((16, 8, 128), BF16),
+            ((16, SEP), BF16),
+            ((8, 896), F32),
+            ((8, 1024), jnp.int32),
+        ],
+        (),
+        distant=(
+            live_rows,
+            send_order,
+            owner_order,
+            right_side,
+            pattern_first.T,
+            pattern_second.T,
+            pattern_third.T,
+        ),
+        scratch=[
+            pltpu.SMEM((14,), jnp.int32),
+            pltpu.VMEM((640,), jnp.int32),
+            pltpu.VMEM((640,), jnp.int32),
+            pltpu.VMEM((32, 640), BF16),
+            pltpu.VMEM((3, BLOCK), jnp.int32),
+            pltpu.VMEM((4, BLOCK), jnp.int32),
+            pltpu.VMEM((2, BLOCK), jnp.int32),
+        ],
+    )
     other_columns = swap(own_columns)
     other_patterns = swap(own_patterns)
     payload = call(
         pack_kernel, "pack_rows", [((16, 4, 16, 128), BF16)], (mine, swap(theirs))
     )[0]
-    payload, masks, other_owner, other_columns, other_patterns = lax.optimization_barrier(
-        (payload, masks, other_owner, other_columns, other_patterns)
+    payload, other_columns, other_patterns = lax.optimization_barrier(
+        (payload, other_columns, other_patterns)
     )
     patterns = (own_patterns, other_patterns)
-    payload = finish(payload, FIRST)
-    payload = begin(payload, SECOND)
-    received = exchange(payload.reshape(64, 16, 128), 4)
+    payload = begin(payload, FIRST)
+    received = finish(exchange(payload.reshape(64, 16, 128), 4), FIRST)
     own_y, other_y, own_rows, term = call(
         in_kernel,
         "leaf_front",
@@ -483,15 +537,20 @@
             ((32, 1024), BF16),
             ((8, HALF, 512), BF16),
         ],
-        (received,) + patterns + pairs["lower0"] + pairs["down1"],
-        scratch=[pltpu.VMEM((128, 1024), BF16)],
+        (received,) + patterns + (pairs["lower0"][1], pairs["down1"][1]),
+        distant=(pairs["lower0"][0], pairs["down1"][0]),
+        scratch=[
+            pltpu.VMEM((128, 1024), BF16),
+            pltpu.VMEM((LEAF, 8 * LEAF), BF16),
+            pltpu.VMEM((LEAF, SEP), BF16),
+        ],
     )
     level_y = {0: (own_y, other_y)}
     rights = call(
         rest_kernel,
         "separator_rows",
         [((HALF, 512), BF16), ((HALF, 256), BF16), ((HALF, 128), BF16)],
-        (own_rows, owner_order, other_owner),
+        (own_rows, own_columns, other_columns),
     )
     for level in (1, 2, 3):
         members = MEMBERS[level]
@@ -499,6 +558,7 @@
         piece = ((HALF, WIDTHS[level]), BF16)
         if level == 1:
             term, rights = lax.optimization_barrier((term, rights))
+            term = begin(term, SECOND)
         shared = exchange(term, level)
         reduced = call(
             functools.partial(reduce_kernel, level),
@@ -557,8 +617,8 @@
     outbound = call(
         out_kernel,
         "leaf_solution",
-        [((64, 16, 128), BF16)],
-        (gathered, owner_order, other_owner)
+        [((64, 8, 128), BF16)],
+        (gathered, own_columns, other_columns)
         + level_x[1]
         + level_x[2]
         + level_x[3]

time: 211 us -> 201 us (0.953)
  local copies, waits for them, and re-layouts: 8.06 us -> 0.05 us
    unnamed x46 -> x24, local copies, waits for them, and re-layouts: 8.06 us -> 0.05 us
    pallas_call x19 -> x18, Pallas kernels: 14.9 us -> 15.9 us  [call(): pl.pallas_call(body, name=name, out_shape=[jax.ShapeDtypeStruct(shape, dt...]
    ppermute x19 -> x18, starting transfers between devices: 25.7 us -> 25.5 us  [swap(): return lax.ppermute(value, 'c', [(0, 1), (1, 0)])]
  transfers between devices with their start and end apart: 19 -> 18, of which waited for: 3 -> 3; matrix products, arithmetic and copies ran while one was open for 0% -> 0% of each run, Pallas kernels for 3% -> 2%
where the time goes in v3:
time: 201 us
  blocking collectives  157 us (78%)
  starting transfers between devices  25.5 us (13%)
  Pallas kernels  15.9 us (8%)
    all_to_all x15, blocking collectives, exchange(): lax.all_to_all(value, CHIPS[level], split_axis=0, concat_axis=0, tiled=True)  157 us
    ppermute x18, starting transfers between devices, swap(): return lax.ppermute(value, 'c', [(0, 1), (1, 0)])  25.5 us
    pallas_call x18, Pallas kernels, call(): pl.pallas_call(body, name=name, out_shape=[jax.ShapeDtypeStruct(shape, dt...  15.9 us
  transfers between devices with their start and end apart: 18, of which 3 were waited for; matrix products, arithmetic and copies ran while one was open for 0% of the time, Pallas kernels for 2%

profile of v3, /device:TPU:1, one launch (start us, length us, event | category | flops | bytes accessed | tf_op | source)
XLA Modules:
  0.0 200.7 jit_solution(13067375596410331912)
XLA Ops:
  0.0 1.9 start.1
  1.9 1.5 collective-permute-start.2
  5.8 21.0 %all_to_all.75.received = bf16[64,16,128]{2,1,0:T(8,128)(2,1)S(1)} all-to-all(bf16[64,16,128]{2,1,0:T(8,128)(2,1)S(1)} %bitcast.12), channel_id=1, replica_groups=mesh['z1'=2,'z0'=2,'y1'=2,'y0'=2,'x'=4,'c'=2] {'z1','z0','y1','y0','x'}, dimensions={0} | all-to-all | bytes 524288 | tf_op jit(solution)/shard_map/all_to_all | solution.py:41
  26.9 2.7 %leaf_front.1 = (bf16[16,192]{1,0:T(8,128)(2,1)S(1)}, bf16[16,192]{1,0:T(8,128)(2,1)S(1)}, bf16[32,1024]{1,0:T(8,128)(2,1)S(1)}, bf16[8,16,512]{2,1,0:T(8,128)(2,1)S(1)}) custom-call(bf16[192,1536]{1,0:T(8,128)(2,1)} %bitcast.22, bf16[192,4096]{1,0:T(8,128)(2,1)} %bitcast.20, bf16[64,16,128]{2,1,0:T(8,128)(2,1)S(1)} %all_to_all.75.received, ...), custom_call_target="tpu_custom_call" | custom-call | tf_op jit(solution)/shard_map/leaf_front/pallas_call | solution.py:49
  30.2 1.6 collective-permute-start.7
  31.9 7.8 %all_to_all.76.received = bf16[8,16,512]{2,1,0:T(8,128)(2,1)S(1)} all-to-all(bf16[8,16,512]{2,1,0:T(8,128)(2,1)S(1)} %get-tuple-element.99), channel_id=1, replica_groups=mesh['z1'=2,'z0'=2,'y1'=2,'y0'=2,'x'=4,'c'=2] {'y0','x'}, dimensions={0} | all-to-all | bytes 262144 | tf_op jit(solution)/shard_map/all_to_all | solution.py:41
  39.8 1.6 collective-permute-start.11
  42.0 7.8 %all_to_all.77.gathered = bf16[8,16,512]{2,1,0:T(8,128)(2,1)S(1)} all-to-all(bf16[8,16,512]{2,1,0:T(8,128)(2,1)S(1)} %reduce_1.1), channel_id=1, replica_groups=mesh['z1'=2,'z0'=2,'y1'=2,'y0'=2,'x'=4,'c'=2] {'y0','x'}, dimensions={0} | all-to-all | bytes 262144 | tf_op jit(solution)/shard_map/all_to_all | solution.py:41
  49.9 2.0 %up_1.1 = (bf16[16,256]{1,0:T(8,128)(2,1)S(1)}, bf16[16,256]{1,0:T(8,128)(2,1)S(1)}, bf16[16,16,256]{2,1,0:T(8,128)(2,1)S(1)}) custom-call(bf16[8,16,512]{2,1,0:T(8,128)(2,1)S(1)} %all_to_all.77.gathered, f32[8,896]{1,0:T(8,128)S(1)} %get-tuple-element.101.masks, bf16[16,4096]{1,0:T(8,128)(2,1)S(1)} %get-tuple-element.81.own_pattern, ...), custom_call_target="tpu_custom_call" | custom-call | tf_op jit(solution)/shard_map/up_1/pallas_call | solution.py:49
  51.9 10.5 %all_to_all.78.received = bf16[16,16,256]{2,1,0:T(8,128)(2,1)S(1)} all-to-all(bf16[16,16,256]{2,1,0:T(8,128)(2,1)S(1)} %get-tuple-element.108), channel_id=1, replica_groups=mesh['z1'=2,'z0'=2,'y1'=2,'y0'=2,'x'=4,'c'=2] {'y1','y0','x'}, dimensions={0} | all-to-all | bytes 262144 | tf_op jit(solution)/shard_map/all_to_all | solution.py:41
  62.5 3.1 %collective-permute-start.13 = (bf16[4096,256]{1,0:T(8,128)(2,1)S(1)}, bf16[4096,256]{1,0:T(8,128)(2,1)S(1)}, u32[]{:S(2)}, u32[]{:S(2)}) collective-permute-start(bf16[4096,256]{1,0:T(8,128)(2,1)S(1)} %copy-done.3), channel_id=1, source_target_pairs={{0,1},{1,0},{2,3},{3,2},{4,5},{5,4},{6,7},{7,6},{8,9},{9,8},{10,11... | collective-permute-start | bytes 6291464 | tf_op jit(solution)/shard_map/ppermute | solution.py:37
  66.2 9.6 %all_to_all.79.gathered = bf16[16,16,256]{2,1,0:T(8,128)(2,1)S(1)} all-to-all(bf16[16,16,256]{2,1,0:T(8,128)(2,1)S(1)} %reduce_2.1), channel_id=1, replica_groups=mesh['z1'=2,'z0'=2,'y1'=2,'y0'=2,'x'=4,'c'=2] {'y1','y0','x'}, dimensions={0} | all-to-all | bytes 262144 | tf_op jit(solution)/shard_map/all_to_all | solution.py:41
  77.0 10.9 %all_to_all.80.received = bf16[32,16,128]{2,1,0:T(8,128)(2,1)S(1)} all-to-all(bf16[32,16,128]{2,1,0:T(8,128)(2,1)S(1)} %get-tuple-element.118), channel_id=1, replica_groups=mesh['z1'=2,'z0'=2,'y1'=2,'y0'=2,'x'=4,'c'=2] {'z0','y1','y0','x'}, dimensions={0} | all-to-all | bytes 262144 | tf_op jit(solution)/shard_map/all_to_all | solution.py:41
  88.0 10.7 %all_to_all.81.gathered = bf16[32,16,128]{2,1,0:T(8,128)(2,1)S(1)} all-to-all(bf16[32,16,128]{2,1,0:T(8,128)(2,1)S(1)} %reduce_3.1), channel_id=1, replica_groups=mesh['z1'=2,'z0'=2,'y1'=2,'y0'=2,'x'=4,'c'=2] {'z0','y1','y0','x'}, dimensions={0} | all-to-all | bytes 262144 | tf_op jit(solution)/shard_map/all_to_all | solution.py:41
  99.7 10.7 %all_to_all.82.gathered = bf16[32,16,128]{2,1,0:T(8,128)(2,1)S(1)} all-to-all(bf16[32,16,128]{2,1,0:T(8,128)(2,1)S(1)} %get-tuple-element.126), channel_id=1, replica_groups=mesh['z1'=2,'z0'=2,'y1'=2,'y0'=2,'x'=4,'c'=2] {'z0','y1','y0','x'}, dimensions={0} | all-to-all | bytes 262144 | tf_op jit(solution)/shard_map/all_to_all | solution.py:41
  110.9 10.7 %all_to_all.83.gathered = bf16[32,16,128]{2,1,0:T(8,128)(2,1)S(1)} all-to-all(bf16[32,16,128]{2,1,0:T(8,128)(2,1)S(1)} %get-tuple-element.128), channel_id=1, replica_groups=mesh['z1'=2,'z0'=2,'y1'=2,'y0'=2,'x'=4,'c'=2] {'z0','y1','y0','x'}, dimensions={0} | all-to-all | bytes 262144 | tf_op jit(solution)/shard_map/all_to_all | solution.py:41
  122.1 10.0 %all_to_all.84.gathered = bf16[16,16,256]{2,1,0:T(8,128)(2,1)S(1)} all-to-all(bf16[16,16,256]{2,1,0:T(8,128)(2,1)S(1)} %back_2.1), channel_id=1, replica_groups=mesh['z1'=2,'z0'=2,'y1'=2,'y0'=2,'x'=4,'c'=2] {'y1','y0','x'}, dimensions={0} | all-to-all | bytes 262144 | tf_op jit(solution)/shard_map/all_to_all | solution.py:41
  132.5 9.6 %all_to_all.85.gathered = bf16[16,16,256]{2,1,0:T(8,128)(2,1)S(1)} all-to-all(bf16[16,16,256]{2,1,0:T(8,128)(2,1)S(1)} %get-tuple-element.133), channel_id=1, replica_groups=mesh['z1'=2,'z0'=2,'y1'=2,'y0'=2,'x'=4,'c'=2] {'y1','y0','x'}, dimensions={0} | all-to-all | bytes 262144 | tf_op jit(solution)/shard_map/all_to_all | solution.py:41
  143.0 8.2 %all_to_all.86.gathered = bf16[8,16,512]{2,1,0:T(8,128)(2,1)S(1)} all-to-all(bf16[8,16,512]{2,1,0:T(8,128)(2,1)S(1)} %back_1.1), channel_id=1, replica_groups=mesh['z1'=2,'z0'=2,'y1'=2,'y0'=2,'x'=4,'c'=2] {'y0','x'}, dimensions={0} | all-to-all | bytes 262144 | tf_op jit(solution)/shard_map/all_to_all | solution.py:41
  151.9 7.8 %all_to_all.87.gathered = bf16[8,16,512]{2,1,0:T(8,128)(2,1)S(1)} all-to-all(bf16[8,16,512]{2,1,0:T(8,128)(2,1)S(1)} %get-tuple-element.138), channel_id=1, replica_groups=mesh['z1'=2,'z0'=2,'y1'=2,'y0'=2,'x'=4,'c'=2] {'y0','x'}, dimensions={0} | all-to-all | bytes 262144 | tf_op jit(solution)/shard_map/all_to_all | solution.py:41
  160.9 6.7 %all_to_all.88.gathered = bf16[4,16,384]{2,1,0:T(8,128)(2,1)S(1)} all-to-all(bf16[4,16,384]{2,1,0:T(8,128)(2,1)S(1)} %back_0.1), channel_id=1, replica_groups=mesh['z1'=2,'z0'=2,'y1'=2,'y0'=2,'x'=4,'c'=2] {'x'}, dimensions={0} | all-to-all | bytes 98304 | tf_op jit(solution)/shard_map/all_to_all | solution.py:41
  167.6 1.6 leaf_solution.1
  169.2 14.4 %all_to_all.89.received = bf16[64,8,128]{2,1,0:T(8,128)(2,1)S(1)} all-to-all(bf16[64,8,128]{2,1,0:T(8,128)(2,1)S(1)} %leaf_solution.1), channel_id=1, replica_groups=mesh['z1'=2,'z0'=2,'y1'=2,'y0'=2,'x'=4,'c'=2] {'z1','z0','y1','y0','x'}, dimensions={0} | all-to-all | bytes 262144 | tf_op jit(solution)/shard_map/all_to_all | solution.py:41
  184.4 14.8 %collective-permute-start.17 = (bf16[16,640]{1,0:T(8,128)(2,1)S(1)}, bf16[16,640]{1,0:T(8,128)(2,1)S(1)}, u32[]{:S(2)}, u32[]{:S(2)}) collective-permute-start(bf16[16,640]{1,0:T(8,128)(2,1)S(1)} %get-tuple-element.150), channel_id=1, source_target_pairs={{0,1},{1,0},{2,3},{3,2},{4,5},{5,4},{6,7},{7,6},{8,9},{9,8},{10,11... | collective-permute-start | bytes 61448 | tf_op jit(solution)/shard_map/ppermute | solution.py:37
  (70 shorter events, 12.8 us)
Async XLA Ops:
  1.9 2.9 %collective-permute-start.2 = (bf16[16,4096]{1,0:T(8,128)(2,1)S(1)}, bf16[16,4096]{1,0:T(8,128)(2,1)S(1)}, u32[]{:S(2)}, u32[]{:S(2)}) collective-permute-start(bf16[16,4096]{1,0:T(8,128)(2,1)S(1)} %get-tuple-element.81.own_pattern), channel_id=1, source_target_pairs={{0,1},{1,0},{2,3},{3,2},{4,5},{5,4},{6,7},{7,6},{8,9},{9,8},{10,11... | collective-permute-start | bytes 393224 | tf_op jit(solution)/shard_map/ppermute | solution.py:37
  3.5 1.2 collective-permute-start
  3.5 1.3 collective-permute-start.1
  4.7 36.7 %copy-start.6 = (bf16[4096,128]{1,0:T(8,128)(2,1)S(1)}, bf16[4096,128]{1,0:T(8,128)(2,1)}, u32[]{:S(2)}) copy-start(bf16[4096,128]{1,0:T(8,128)(2,1)} %own_factor.2) | copy-start | bytes 3145732
  4.8 22.1 %collective-permute-start.5 = (bf16[4096,256]{1,0:T(8,128)(2,1)}, bf16[4096,256]{1,0:T(8,128)(2,1)S(1)}, u32[]{:S(2)}, u32[]{:S(2)}) collective-permute-start(bf16[4096,256]{1,0:T(8,128)(2,1)} %own_lower.2), channel_id=1, source_target_pairs={{0,1},{1,0},{2,3},{3,2},{4,5},{5,4},{6,7},{7,6},{8,9},{9,8},{10,11... | collective-permute-start | bytes 6291464 | tf_op jit(solution)/shard_map/ppermute | solution.py:37
  5.2 21.7 %collective-permute-start.6 = (bf16[4096,256]{1,0:T(8,128)(2,1)}, bf16[4096,256]{1,0:T(8,128)(2,1)S(1)}, u32[]{:S(2)}, u32[]{:S(2)}) collective-permute-start(bf16[4096,256]{1,0:T(8,128)(2,1)} %own_link.4), channel_id=1, source_target_pairs={{0,1},{1,0},{2,3},{3,2},{4,5},{5,4},{6,7},{7,6},{8,9},{9,8},{10,11... | collective-permute-start | bytes 6291464 | tf_op jit(solution)/shard_map/ppermute | solution.py:37
  5.3 21.5 %collective-permute-start.4 = (bf16[192,4096]{1,0:T(8,128)(2,1)}, bf16[192,4096]{1,0:T(8,128)(2,1)S(1)}, u32[]{:S(2)}, u32[]{:S(2)}) collective-permute-start(bf16[192,4096]{1,0:T(8,128)(2,1)} %bitcast.19), channel_id=1, source_target_pairs={{0,1},{1,0},{2,3},{3,2},{4,5},{5,4},{6,7},{7,6},{8,9},{9,8},{10,11... | collective-permute-start | bytes 4718600 | tf_op jit(solution)/shard_map/ppermute | solution.py:37
  5.7 21.2 %collective-permute-start.3 = (bf16[192,1536]{1,0:T(8,128)(2,1)}, bf16[192,1536]{1,0:T(8,128)(2,1)S(1)}, u32[]{:S(2)}, u32[]{:S(2)}) collective-permute-start(bf16[192,1536]{1,0:T(8,128)(2,1)} %bitcast.21), channel_id=1, source_target_pairs={{0,1},{1,0},{2,3},{3,2},{4,5},{5,4},{6,7},{7,6},{8,9},{9,8},{10,11... | collective-permute-start | bytes 1769480 | tf_op jit(solution)/shard_map/ppermute | solution.py:37
  26.9 23.0 %copy-start = (bf16[4096,256]{1,0:T(8,128)(2,1)S(1)}, bf16[4096,256]{1,0:T(8,128)(2,1)}, u32[]{:S(2)}) copy-start(bf16[4096,256]{1,0:T(8,128)(2,1)} %own_lower.2) | copy-start | bytes 6291460
  26.9 23.0 %copy-start.1 = (bf16[4096,256]{1,0:T(8,128)(2,1)S(1)}, bf16[4096,256]{1,0:T(8,128)(2,1)}, u32[]{:S(2)}) copy-start(bf16[4096,256]{1,0:T(8,128)(2,1)} %own_link.4) | copy-start | bytes 6291460
  30.2 9.6 %collective-permute-start.7 = (bf16[4096,128]{1,0:T(8,128)(2,1)}, bf16[4096,128]{1,0:T(8,128)(2,1)S(1)}, u32[]{:S(2)}, u32[]{:S(2)}) collective-permute-start(bf16[4096,128]{1,0:T(8,128)(2,1)} %own_lower.3), channel_id=1, source_target_pairs={{0,1},{1,0},{2,3},{3,2},{4,5},{5,4},{6,7},{7,6},{8,9},{9,8},{10,11... | collective-permute-start | bytes 3145736 | tf_op jit(solution)/shard_map/ppermute | solution.py:37
  31.8 8.0 %collective-permute-start.8 = (bf16[4096,128]{1,0:T(8,128)(2,1)}, bf16[4096,128]{1,0:T(8,128)(2,1)S(1)}, u32[]{:S(2)}, u32[]{:S(2)}) collective-permute-start(bf16[4096,128]{1,0:T(8,128)(2,1)} %own_link.5), channel_id=1, source_target_pairs={{0,1},{1,0},{2,3},{3,2},{4,5},{5,4},{6,7},{7,6},{8,9},{9,8},{10,11... | collective-permute-start | bytes 3145736 | tf_op jit(solution)/shard_map/ppermute | solution.py:37
  39.8 22.7 %collective-permute-start.11 = (bf16[4096,128]{1,0:T(8,128)(2,1)S(1)}, bf16[4096,128]{1,0:T(8,128)(2,1)S(1)}, u32[]{:S(2)}, u32[]{:S(2)}) collective-permute-start(bf16[4096,128]{1,0:T(8,128)(2,1)S(1)} %copy-done.5), channel_id=1, source_target_pairs={{0,1},{1,0},{2,3},{3,2},{4,5},{5,4},{6,7},{7,6},{8,9},{9,8},{10,11... | collective-permute-start | bytes 3145736 | tf_op jit(solution)/shard_map/ppermute | solution.py:37
  41.4 21.1 %collective-permute-start.12 = (bf16[4096,128]{1,0:T(8,128)(2,1)S(1)}, bf16[4096,128]{1,0:T(8,128)(2,1)S(1)}, u32[]{:S(2)}, u32[]{:S(2)}) collective-permute-start(bf16[4096,128]{1,0:T(8,128)(2,1)S(1)} %copy-done.6), channel_id=1, source_target_pairs={{0,1},{1,0},{2,3},{3,2},{4,5},{5,4},{6,7},{7,6},{8,9},{9,8},{10,11... | collective-permute-start | bytes 3145736 | tf_op jit(solution)/shard_map/ppermute | solution.py:37
  41.5 21.0 %collective-permute-start.9 = (bf16[64,4096]{1,0:T(8,128)(2,1)}, bf16[64,4096]{1,0:T(8,128)(2,1)S(1)}, u32[]{:S(2)}, u32[]{:S(2)}) collective-permute-start(bf16[64,4096]{1,0:T(8,128)(2,1)} %bitcast.15), channel_id=1, source_target_pairs={{0,1},{1,0},{2,3},{3,2},{4,5},{5,4},{6,7},{7,6},{8,9},{9,8},{10,11... | collective-permute-start | bytes 1572872 | tf_op jit(solution)/shard_map/ppermute | solution.py:37
  41.9 20.6 %collective-permute-start.10 = (bf16[64,4096]{1,0:T(8,128)(2,1)}, bf16[64,4096]{1,0:T(8,128)(2,1)S(1)}, u32[]{:S(2)}, u32[]{:S(2)}) collective-permute-start(bf16[64,4096]{1,0:T(8,128)(2,1)} %bitcast.17), channel_id=1, source_target_pairs={{0,1},{1,0},{2,3},{3,2},{4,5},{5,4},{6,7},{7,6},{8,9},{9,8},{10,11... | collective-permute-start | bytes 1572872 | tf_op jit(solution)/shard_map/ppermute | solution.py:37
  49.9 26.0 %copy-start.7 = (bf16[4096,128]{1,0:T(8,128)(2,1)S(1)}, bf16[4096,128]{1,0:T(8,128)(2,1)}, u32[]{:S(2)}) copy-start(bf16[4096,128]{1,0:T(8,128)(2,1)} %own_lower.3) | copy-start | bytes 3145732
  49.9 26.0 %copy-start.8 = (bf16[4096,128]{1,0:T(8,128)(2,1)S(1)}, bf16[4096,128]{1,0:T(8,128)(2,1)}, u32[]{:S(2)}) copy-start(bf16[4096,128]{1,0:T(8,128)(2,1)} %own_link.5) | copy-start | bytes 3145732
  62.5 25.5 %collective-permute-start.13 = (bf16[4096,256]{1,0:T(8,128)(2,1)S(1)}, bf16[4096,256]{1,0:T(8,128)(2,1)S(1)}, u32[]{:S(2)}, u32[]{:S(2)}) collective-permute-start(bf16[4096,256]{1,0:T(8,128)(2,1)S(1)} %copy-done.3), channel_id=1, source_target_pairs={{0,1},{1,0},{2,3},{3,2},{4,5},{5,4},{6,7},{7,6},{8,9},{9,8},{10,11... | collective-permute-start | bytes 6291464 | tf_op jit(solution)/shard_map/ppermute | solution.py:37
  65.6 22.4 %collective-permute-start.14 = (bf16[4096,256]{1,0:T(8,128)(2,1)S(1)}, bf16[4096,256]{1,0:T(8,128)(2,1)S(1)}, u32[]{:S(2)}, u32[]{:S(2)}) collective-permute-start(bf16[4096,256]{1,0:T(8,128)(2,1)S(1)} %copy-done.2), channel_id=1, source_target_pairs={{0,1},{1,0},{2,3},{3,2},{4,5},{5,4},{6,7},{7,6},{8,9},{9,8},{10,11... | collective-permute-start | bytes 6291464 | tf_op jit(solution)/shard_map/ppermute | solution.py:37
  65.7 22.3 %collective-permute-start.15 = (bf16[192,4096]{1,0:T(8,128)(2,1)S(1)}, bf16[192,4096]{1,0:T(8,128)(2,1)S(1)}, u32[]{:S(2)}, u32[]{:S(2)}) collective-permute-start(bf16[192,4096]{1,0:T(8,128)(2,1)S(1)} %bitcast.10), channel_id=1, source_target_pairs={{0,1},{1,0},{2,3},{3,2},{4,5},{5,4},{6,7},{7,6},{8,9},{9,8},{10,11... | collective-permute-start | bytes 4718600 | tf_op jit(solution)/shard_map/ppermute | solution.py:37
  66.1 21.8 %collective-permute-start.16 = (bf16[192,1536]{1,0:T(8,128)(2,1)S(1)}, bf16[192,1536]{1,0:T(8,128)(2,1)S(1)}, u32[]{:S(2)}, u32[]{:S(2)}) collective-permute-start(bf16[192,1536]{1,0:T(8,128)(2,1)S(1)} %bitcast.13), channel_id=1, source_target_pairs={{0,1},{1,0},{2,3},{3,2},{4,5},{5,4},{6,7},{7,6},{8,9},{9,8},{10,11... | collective-permute-start | bytes 1769480 | tf_op jit(solution)/shard_map/ppermute | solution.py:37
  77.0 33.5 %copy-start.11 = (bf16[4096,64]{0,1:T(8,128)(2,1)S(1)}, bf16[4096,64]{0,1:T(8,128)(2,1)}, u32[]{:S(2)}) copy-start(bf16[4096,64]{0,1:T(8,128)(2,1)} %param.32) | copy-start | bytes 1572868
  184.4 15.7 %collective-permute-start.17 = (bf16[16,640]{1,0:T(8,128)(2,1)S(1)}, bf16[16,640]{1,0:T(8,128)(2,1)S(1)}, u32[]{:S(2)}, u32[]{:S(2)}) collective-permute-start(bf16[16,640]{1,0:T(8,128)(2,1)S(1)} %get-tuple-element.150), channel_id=1, source_target_pairs={{0,1},{1,0},{2,3},{3,2},{4,5},{5,4},{6,7},{7,6},{8,9},{9,8},{10,11... | collective-permute-start | bytes 61448 | tf_op jit(solution)/shard_map/ppermute | solution.py:37
  (6 other events, 96.3 us)

commit v4 on v3

--- a/solution.py
+++ b/solution.py
@@ -211,22 +211,25 @@
 
 
 def start_kernel(
-    live, send_order, owner_order, right, first, second, third, mine, theirs, wide, masks,
-    columns, live_buffer, send_buffer, owner_buffer, right_buffer, first_buffer, second_buffer,
-    third_buffer, semaphores,
+    live, send_order, owner_order, right, first, second, third, lower, link, mine, theirs, wide,
+    masks, columns, lower_out, link_out, live_buffer, send_buffer, owner_buffer, right_buffer,
+    first_buffer, second_buffer, third_buffer, semaphores,
 ):
     buffers = (
         live_buffer, send_buffer, owner_buffer, right_buffer, first_buffer, second_buffer,
-        third_buffer,
-    )
-    sources = (live, send_order, owner_order, right, first, second, third)
-    for copy in fetch(sources, buffers, semaphores):
+        third_buffer, lower_out, link_out,
+    )
+    sources = (live, send_order, owner_order, right, first, second, third, lower, link)
+    copies = fetch(sources, buffers, semaphores)
+    for copy in copies[:7]:
         copy.wait()
     pick_rows(send_buffer, owner_buffer, right_buffer, mine, theirs)
     make_tables(
         live_buffer, send_buffer, owner_buffer, first_buffer, second_buffer, third_buffer, wide,
         masks, columns,
     )
+    for copy in copies[7:]:
+        copy.wait()
 
 
 def stack_blocks(piece, count):
@@ -292,10 +295,9 @@
 
 
 def in_kernel(
-    far_lower, far_link, received, own_pattern, other_pattern, other_lower, other_link,
-    own_out, other_out, rows_out, out, turned, own_lower, own_link, semaphores,
+    received, own_pattern, other_pattern, own_lower, other_lower, own_link, other_link,
+    own_out, other_out, rows_out, out, turned,
 ):
-    copies = fetch((far_lower, far_link), (own_lower, own_link), semaphores)
     flat = received[...].reshape(1024, 128)
     turned[...] = flat.astype(F32).T.astype(BF16)
     info = received[pl.ds(lax.axis_index(LEAVES) * 4, 4)].astype(F32)
@@ -323,13 +325,11 @@
     start = pl.multiple_of(lax.axis_index("x") * 32, 32)
     rows_out[...] = turned[pl.ds(start, 32), :]
     front = jnp.concatenate(fronts, axis=1)
-    copies[0].wait()
     own = apply_factor(front, own_lower).astype(BF16)
     other = apply_factor(front, other_lower).astype(BF16)
     own_out[...] = own
     other_out[...] = other
     pieces = (own.astype(F32), other.astype(F32))
-    copies[1].wait()
     down_product(1, pieces, (own_link, other_link), (own_pattern, other_pattern), out)
 
 
@@ -380,6 +380,11 @@
     own, other = solve_pieces(level, gathered, masks, own_factor, other_factor)
     own_out[...] = own
     other_out[...] = other
+    store_copies(out, in_order(own.astype(F32), other.astype(F32)))
+
+
+def top_kernel(level, gathered, masks, own_factor, other_factor, out):
+    own, other = solve_pieces(level, gathered, masks, own_factor, other_factor)
     store_copies(out, in_order(own.astype(F32), other.astype(F32)))
 
 
@@ -458,8 +463,6 @@
 ):
     core = lax.axis_index("c")
     factors = {
-        "lower0": lower_leaf.T,
-        "down1": downlink_first.T,
         "lower1": lower_first,
         "down2": downlink_second,
         "lower2": lower_second,
@@ -487,7 +490,7 @@
             pairs[name] = (pairs[name][0], other)
         return tied[0]
 
-    mine, theirs, own_patterns, masks, own_columns = call(
+    mine, theirs, own_patterns, masks, own_columns, own_lower, own_link = call(
         start_kernel,
         "start",
         [
@@ -496,6 +499,8 @@
             ((16, SEP), BF16),
             ((8, 896), F32),
             ((8, 1024), jnp.int32),
+            ((LEAF, 8 * LEAF), BF16),
+            ((LEAF, SEP), BF16),
         ],
         (),
         distant=(
@@ -506,6 +511,8 @@
             pattern_first.T,
             pattern_second.T,
             pattern_third.T,
+            lower_leaf.T,
+            downlink_first.T,
         ),
         scratch=[
             pltpu.SMEM((14,), jnp.int32),
@@ -517,6 +524,8 @@
             pltpu.VMEM((2, BLOCK), jnp.int32),
         ],
     )
+    factors["lower0"] = own_lower
+    factors["down1"] = own_link
     other_columns = swap(own_columns)
     other_patterns = swap(own_patterns)
     payload = call(
@@ -537,13 +546,8 @@
             ((32, 1024), BF16),
             ((8, HALF, 512), BF16),
         ],
-        (received,) + patterns + (pairs["lower0"][1], pairs["down1"][1]),
-        distant=(pairs["lower0"][0], pairs["down1"][0]),
-        scratch=[
-            pltpu.VMEM((128, 1024), BF16),
-            pltpu.VMEM((LEAF, 8 * LEAF), BF16),
-            pltpu.VMEM((LEAF, SEP), BF16),
-        ],
+        (received,) + patterns + pairs["lower0"] + pairs["down1"],
+        scratch=[pltpu.VMEM((128, 1024), BF16)],
     )
     level_y = {0: (own_y, other_y)}
     rights = call(
@@ -585,12 +589,13 @@
                 + pairs["down%d" % (level + 1)],
             )
         else:
-            own_y, other_y, copies = call(
-                functools.partial(solve_kernel, level),
+            copies = call(
+                functools.partial(top_kernel, level),
                 "top_lower",
-                [piece, piece, ((members, HALF, chip_width), BF16)],
+                [((members, HALF, chip_width), BF16)],
                 (gathered, masks) + pairs["lower3"],
-            )
+            )[0]
+            break
         level_y[level] = (own_y, other_y)
     level_x = {}
     for level in (3, 2, 1):

time: 201 us -> 200 us (level)
  no operation moved by 1% of the time
where the time goes in v4:
time: 200 us
  blocking collectives  157 us (78%)
  starting transfers between devices  25.5 us (13%)
  Pallas kernels  14.8 us (7%)
    all_to_all x15, blocking collectives, exchange(): lax.all_to_all(value, CHIPS[level], split_axis=0, concat_axis=0, tiled=True)  157 us
    ppermute x18, starting transfers between devices, swap(): return lax.ppermute(value, 'c', [(0, 1), (1, 0)])  25.5 us
    pallas_call x18, Pallas kernels, call(): pl.pallas_call(body, name=name, out_shape=[jax.ShapeDtypeStruct(shape, dt...  14.8 us
  transfers between devices with their start and end apart: 18, of which 3 were waited for; matrix products, arithmetic and copies ran while one was open for 0% of the time, Pallas kernels for 2%

profile of v4, /device:TPU:1, one launch (start us, length us, event | category | flops | bytes accessed | tf_op | source)
XLA Modules:
  0.0 199.8 jit_solution(13379771001151145564)
XLA Ops:
  0.0 2.1 %start.1 = (bf16[16,8,128]{2,1,0:T(8,128)(2,1)S(1)}, bf16[16,8,128]{2,1,0:T(8,128)(2,1)S(1)}, bf16[16,4096]{1,0:T(8,128)(2,1)S(1)}, f32[8,896]{1,0:T(8,128)S(1)}...) custom-call(s32[14]{0:T(128)} %live.1, s32[640]{0:T(1024)} %send_order.1, ...), custom_call_target="tpu_custom_call" | custom-call | tf_op jit(solution)/shard_map/start/pallas_call | solution.py:49
  2.1 1.5 collective-permute-start.2
  6.0 21.1 %all_to_all.75.received = bf16[64,16,128]{2,1,0:T(8,128)(2,1)S(1)} all-to-all(bf16[64,16,128]{2,1,0:T(8,128)(2,1)S(1)} %bitcast.12), channel_id=1, replica_groups=mesh['z1'=2,'z0'=2,'y1'=2,'y0'=2,'x'=4,'c'=2] {'z1','z0','y1','y0','x'}, dimensions={0} | all-to-all | bytes 524288 | tf_op jit(solution)/shard_map/all_to_all | solution.py:41
  27.2 2.0 %leaf_front.1 = (bf16[16,192]{1,0:T(8,128)(2,1)S(1)}, bf16[16,192]{1,0:T(8,128)(2,1)S(1)}, bf16[32,1024]{1,0:T(8,128)(2,1)S(1)}, bf16[8,16,512]{2,1,0:T(8,128)(2,1)S(1)}) custom-call(bf16[64,16,128]{2,1,0:T(8,128)(2,1)S(1)} %all_to_all.75.received, bf16[16,4096]{1,0:T(8,128)(2,1)S(1)} %get-tuple-element.82.own_pattern, ...), custom_call_target="tpu_custom_call" | custom-call | tf_op jit(solution)/shard_map/leaf_front/pallas_call | solution.py:49
  29.8 1.6 collective-permute-start.7
  31.5 7.8 %all_to_all.76.received = bf16[8,16,512]{2,1,0:T(8,128)(2,1)S(1)} all-to-all(bf16[8,16,512]{2,1,0:T(8,128)(2,1)S(1)} %get-tuple-element.102), channel_id=1, replica_groups=mesh['z1'=2,'z0'=2,'y1'=2,'y0'=2,'x'=4,'c'=2] {'y0','x'}, dimensions={0} | all-to-all | bytes 262144 | tf_op jit(solution)/shard_map/all_to_all | solution.py:41
  39.4 1.6 collective-permute-start.11
  41.6 7.8 %all_to_all.77.gathered = bf16[8,16,512]{2,1,0:T(8,128)(2,1)S(1)} all-to-all(bf16[8,16,512]{2,1,0:T(8,128)(2,1)S(1)} %reduce_1.1), channel_id=1, replica_groups=mesh['z1'=2,'z0'=2,'y1'=2,'y0'=2,'x'=4,'c'=2] {'y0','x'}, dimensions={0} | all-to-all | bytes 262144 | tf_op jit(solution)/shard_map/all_to_all | solution.py:41
  49.5 2.0 %up_1.1 = (bf16[16,256]{1,0:T(8,128)(2,1)S(1)}, bf16[16,256]{1,0:T(8,128)(2,1)S(1)}, bf16[16,16,256]{2,1,0:T(8,128)(2,1)S(1)}) custom-call(bf16[8,16,512]{2,1,0:T(8,128)(2,1)S(1)} %all_to_all.77.gathered, f32[8,896]{1,0:T(8,128)S(1)} %get-tuple-element.104.masks, bf16[16,4096]{1,0:T(8,128)(2,1)S(1)} %get-tuple-element.82.own_pattern, ...), custom_call_target="tpu_custom_call" | custom-call | tf_op jit(solution)/shard_map/up_1/pallas_call | solution.py:49
  51.5 10.4 %all_to_all.78.received = bf16[16,16,256]{2,1,0:T(8,128)(2,1)S(1)} all-to-all(bf16[16,16,256]{2,1,0:T(8,128)(2,1)S(1)} %get-tuple-element.111), channel_id=1, replica_groups=mesh['z1'=2,'z0'=2,'y1'=2,'y0'=2,'x'=4,'c'=2] {'y1','y0','x'}, dimensions={0} | all-to-all | bytes 262144 | tf_op jit(solution)/shard_map/all_to_all | solution.py:41
  61.9 3.1 %collective-permute-start.13 = (bf16[4096,256]{1,0:T(8,128)(2,1)S(1)}, bf16[4096,256]{1,0:T(8,128)(2,1)S(1)}, u32[]{:S(2)}, u32[]{:S(2)}) collective-permute-start(bf16[4096,256]{1,0:T(8,128)(2,1)S(1)} %copy-done.3), channel_id=1, source_target_pairs={{0,1},{1,0},{2,3},{3,2},{4,5},{5,4},{6,7},{7,6},{8,9},{9,8},{10,11... | collective-permute-start | bytes 6291464 | tf_op jit(solution)/shard_map/ppermute | solution.py:37
  65.7 9.6 %all_to_all.79.gathered = bf16[16,16,256]{2,1,0:T(8,128)(2,1)S(1)} all-to-all(bf16[16,16,256]{2,1,0:T(8,128)(2,1)S(1)} %reduce_2.1), channel_id=1, replica_groups=mesh['z1'=2,'z0'=2,'y1'=2,'y0'=2,'x'=4,'c'=2] {'y1','y0','x'}, dimensions={0} | all-to-all | bytes 262144 | tf_op jit(solution)/shard_map/all_to_all | solution.py:41
  76.4 10.9 %all_to_all.80.received = bf16[32,16,128]{2,1,0:T(8,128)(2,1)S(1)} all-to-all(bf16[32,16,128]{2,1,0:T(8,128)(2,1)S(1)} %get-tuple-element.121), channel_id=1, replica_groups=mesh['z1'=2,'z0'=2,'y1'=2,'y0'=2,'x'=4,'c'=2] {'z0','y1','y0','x'}, dimensions={0} | all-to-all | bytes 262144 | tf_op jit(solution)/shard_map/all_to_all | solution.py:41
  87.4 10.9 %all_to_all.81.gathered = bf16[32,16,128]{2,1,0:T(8,128)(2,1)S(1)} all-to-all(bf16[32,16,128]{2,1,0:T(8,128)(2,1)S(1)} %reduce_3.1), channel_id=1, replica_groups=mesh['z1'=2,'z0'=2,'y1'=2,'y0'=2,'x'=4,'c'=2] {'z0','y1','y0','x'}, dimensions={0} | all-to-all | bytes 262144 | tf_op jit(solution)/shard_map/all_to_all | solution.py:41
  98.8 10.7 %all_to_all.82.gathered = bf16[32,16,128]{2,1,0:T(8,128)(2,1)S(1)} all-to-all(bf16[32,16,128]{2,1,0:T(8,128)(2,1)S(1)} %top_lower.1), channel_id=1, replica_groups=mesh['z1'=2,'z0'=2,'y1'=2,'y0'=2,'x'=4,'c'=2] {'z0','y1','y0','x'}, dimensions={0} | all-to-all | bytes 262144 | tf_op jit(solution)/shard_map/all_to_all | solution.py:41
  110.0 10.7 %all_to_all.83.gathered = bf16[32,16,128]{2,1,0:T(8,128)(2,1)S(1)} all-to-all(bf16[32,16,128]{2,1,0:T(8,128)(2,1)S(1)} %get-tuple-element.130), channel_id=1, replica_groups=mesh['z1'=2,'z0'=2,'y1'=2,'y0'=2,'x'=4,'c'=2] {'z0','y1','y0','x'}, dimensions={0} | all-to-all | bytes 262144 | tf_op jit(solution)/shard_map/all_to_all | solution.py:41
  121.2 10.0 %all_to_all.84.gathered = bf16[16,16,256]{2,1,0:T(8,128)(2,1)S(1)} all-to-all(bf16[16,16,256]{2,1,0:T(8,128)(2,1)S(1)} %back_2.1), channel_id=1, replica_groups=mesh['z1'=2,'z0'=2,'y1'=2,'y0'=2,'x'=4,'c'=2] {'y1','y0','x'}, dimensions={0} | all-to-all | bytes 262144 | tf_op jit(solution)/shard_map/all_to_all | solution.py:41
  131.6 9.6 %all_to_all.85.gathered = bf16[16,16,256]{2,1,0:T(8,128)(2,1)S(1)} all-to-all(bf16[16,16,256]{2,1,0:T(8,128)(2,1)S(1)} %get-tuple-element.135), channel_id=1, replica_groups=mesh['z1'=2,'z0'=2,'y1'=2,'y0'=2,'x'=4,'c'=2] {'y1','y0','x'}, dimensions={0} | all-to-all | bytes 262144 | tf_op jit(solution)/shard_map/all_to_all | solution.py:41
  142.1 8.2 %all_to_all.86.gathered = bf16[8,16,512]{2,1,0:T(8,128)(2,1)S(1)} all-to-all(bf16[8,16,512]{2,1,0:T(8,128)(2,1)S(1)} %back_1.1), channel_id=1, replica_groups=mesh['z1'=2,'z0'=2,'y1'=2,'y0'=2,'x'=4,'c'=2] {'y0','x'}, dimensions={0} | all-to-all | bytes 262144 | tf_op jit(solution)/shard_map/all_to_all | solution.py:41
  151.0 7.8 %all_to_all.87.gathered = bf16[8,16,512]{2,1,0:T(8,128)(2,1)S(1)} all-to-all(bf16[8,16,512]{2,1,0:T(8,128)(2,1)S(1)} %get-tuple-element.140), channel_id=1, replica_groups=mesh['z1'=2,'z0'=2,'y1'=2,'y0'=2,'x'=4,'c'=2] {'y0','x'}, dimensions={0} | all-to-all | bytes 262144 | tf_op jit(solution)/shard_map/all_to_all | solution.py:41
  160.0 6.7 %all_to_all.88.gathered = bf16[4,16,384]{2,1,0:T(8,128)(2,1)S(1)} all-to-all(bf16[4,16,384]{2,1,0:T(8,128)(2,1)S(1)} %back_0.1), channel_id=1, replica_groups=mesh['z1'=2,'z0'=2,'y1'=2,'y0'=2,'x'=4,'c'=2] {'x'}, dimensions={0} | all-to-all | bytes 98304 | tf_op jit(solution)/shard_map/all_to_all | solution.py:41
  166.7 1.6 leaf_solution.1
  168.3 14.4 %all_to_all.89.received = bf16[64,8,128]{2,1,0:T(8,128)(2,1)S(1)} all-to-all(bf16[64,8,128]{2,1,0:T(8,128)(2,1)S(1)} %leaf_solution.1), channel_id=1, replica_groups=mesh['z1'=2,'z0'=2,'y1'=2,'y0'=2,'x'=4,'c'=2] {'z1','z0','y1','y0','x'}, dimensions={0} | all-to-all | bytes 262144 | tf_op jit(solution)/shard_map/all_to_all | solution.py:41
  183.5 14.8 %collective-permute-start.17 = (bf16[16,640]{1,0:T(8,128)(2,1)S(1)}, bf16[16,640]{1,0:T(8,128)(2,1)S(1)}, u32[]{:S(2)}, u32[]{:S(2)}) collective-permute-start(bf16[16,640]{1,0:T(8,128)(2,1)S(1)} %get-tuple-element.152), channel_id=1, source_target_pairs={{0,1},{1,0},{2,3},{3,2},{4,5},{5,4},{6,7},{7,6},{8,9},{9,8},{10,11... | collective-permute-start | bytes 61448 | tf_op jit(solution)/shard_map/ppermute | solution.py:37
  (70 shorter events, 12.3 us)
Async XLA Ops:
  2.1 2.9 %collective-permute-start.2 = (bf16[16,4096]{1,0:T(8,128)(2,1)S(1)}, bf16[16,4096]{1,0:T(8,128)(2,1)S(1)}, u32[]{:S(2)}, u32[]{:S(2)}) collective-permute-start(bf16[16,4096]{1,0:T(8,128)(2,1)S(1)} %get-tuple-element.82.own_pattern), channel_id=1, source_target_pairs={{0,1},{1,0},{2,3},{3,2},{4,5},{5,4},{6,7},{7,6},{8,9},{9,8},{10,11... | collective-permute-start | bytes 393224 | tf_op jit(solution)/shard_map/ppermute | solution.py:37
  3.6 1.2 collective-permute-start
  3.7 1.3 collective-permute-start.1
  4.8 26.6 %copy-start.8 = (bf16[4096,128]{1,0:T(8,128)(2,1)S(1)}, bf16[4096,128]{1,0:T(8,128)(2,1)}, u32[]{:S(2)}) copy-start(bf16[4096,128]{1,0:T(8,128)(2,1)} %own_link.5) | copy-start | bytes 3145732
  5.0 22.2 %collective-permute-start.5 = (bf16[4096,256]{1,0:T(8,128)(2,1)S(1)}, bf16[4096,256]{1,0:T(8,128)(2,1)S(1)}, u32[]{:S(2)}, u32[]{:S(2)}) collective-permute-start(bf16[4096,256]{1,0:T(8,128)(2,1)S(1)} %copy-done), channel_id=1, source_target_pairs={{0,1},{1,0},{2,3},{3,2},{4,5},{5,4},{6,7},{7,6},{8,9},{9,8},{10,11... | collective-permute-start | bytes 6291464 | tf_op jit(solution)/shard_map/ppermute | solution.py:37
  5.4 21.9 %collective-permute-start.6 = (bf16[4096,256]{1,0:T(8,128)(2,1)}, bf16[4096,256]{1,0:T(8,128)(2,1)S(1)}, u32[]{:S(2)}, u32[]{:S(2)}) collective-permute-start(bf16[4096,256]{1,0:T(8,128)(2,1)} %own_link.4), channel_id=1, source_target_pairs={{0,1},{1,0},{2,3},{3,2},{4,5},{5,4},{6,7},{7,6},{8,9},{9,8},{10,11... | collective-permute-start | bytes 6291464 | tf_op jit(solution)/shard_map/ppermute | solution.py:37
  5.5 21.7 %collective-permute-start.4 = (bf16[192,4096]{1,0:T(8,128)(2,1)S(1)}, bf16[192,4096]{1,0:T(8,128)(2,1)S(1)}, u32[]{:S(2)}, u32[]{:S(2)}) collective-permute-start(bf16[192,4096]{1,0:T(8,128)(2,1)S(1)} %get-tuple-element.88.own_link), channel_id=1, source_target_pairs={{0,1},{1,0},{2,3},{3,2},{4,5},{5,4},{6,7},{7,6},{8,9},{9,8},{10,11... | collective-permute-start | bytes 4718600 | tf_op jit(solution)/shard_map/ppermute | solution.py:37
  5.9 21.3 %collective-permute-start.3 = (bf16[192,1536]{1,0:T(8,128)(2,1)S(1)}, bf16[192,1536]{1,0:T(8,128)(2,1)S(1)}, u32[]{:S(2)}, u32[]{:S(2)}) collective-permute-start(bf16[192,1536]{1,0:T(8,128)(2,1)S(1)} %get-tuple-element.87.own_lower), channel_id=1, source_target_pairs={{0,1},{1,0},{2,3},{3,2},{4,5},{5,4},{6,7},{7,6},{8,9},{9,8},{10,11... | collective-permute-start | bytes 1769480 | tf_op jit(solution)/shard_map/ppermute | solution.py:37
  6.0 23.7 %copy-start.7 = (bf16[4096,128]{1,0:T(8,128)(2,1)S(1)}, bf16[4096,128]{1,0:T(8,128)(2,1)}, u32[]{:S(2)}) copy-start(bf16[4096,128]{1,0:T(8,128)(2,1)} %own_lower.3) | copy-start | bytes 3145732
  27.2 22.3 %copy-start.1 = (bf16[4096,256]{1,0:T(8,128)(2,1)S(1)}, bf16[4096,256]{1,0:T(8,128)(2,1)}, u32[]{:S(2)}) copy-start(bf16[4096,256]{1,0:T(8,128)(2,1)} %own_link.4) | copy-start | bytes 6291460
  29.8 9.6 %collective-permute-start.7 = (bf16[4096,128]{1,0:T(8,128)(2,1)S(1)}, bf16[4096,128]{1,0:T(8,128)(2,1)S(1)}, u32[]{:S(2)}, u32[]{:S(2)}) collective-permute-start(bf16[4096,128]{1,0:T(8,128)(2,1)S(1)} %copy-done.7), channel_id=1, source_target_pairs={{0,1},{1,0},{2,3},{3,2},{4,5},{5,4},{6,7},{7,6},{8,9},{9,8},{10,11... | collective-permute-start | bytes 3145736 | tf_op jit(solution)/shard_map/ppermute | solution.py:37
  31.4 8.0 %collective-permute-start.8 = (bf16[4096,128]{1,0:T(8,128)(2,1)S(1)}, bf16[4096,128]{1,0:T(8,128)(2,1)S(1)}, u32[]{:S(2)}, u32[]{:S(2)}) collective-permute-start(bf16[4096,128]{1,0:T(8,128)(2,1)S(1)} %copy-done.8), channel_id=1, source_target_pairs={{0,1},{1,0},{2,3},{3,2},{4,5},{5,4},{6,7},{7,6},{8,9},{9,8},{10,11... | collective-permute-start | bytes 3145736 | tf_op jit(solution)/shard_map/ppermute | solution.py:37
  39.4 22.5 %collective-permute-start.11 = (bf16[4096,128]{1,0:T(8,128)(2,1)S(1)}, bf16[4096,128]{1,0:T(8,128)(2,1)S(1)}, u32[]{:S(2)}, u32[]{:S(2)}) collective-permute-start(bf16[4096,128]{1,0:T(8,128)(2,1)S(1)} %copy-done.5), channel_id=1, source_target_pairs={{0,1},{1,0},{2,3},{3,2},{4,5},{5,4},{6,7},{7,6},{8,9},{9,8},{10,11... | collective-permute-start | bytes 3145736 | tf_op jit(solution)/shard_map/ppermute | solution.py:37
  41.0 20.9 %collective-permute-start.12 = (bf16[4096,128]{1,0:T(8,128)(2,1)S(1)}, bf16[4096,128]{1,0:T(8,128)(2,1)S(1)}, u32[]{:S(2)}, u32[]{:S(2)}) collective-permute-start(bf16[4096,128]{1,0:T(8,128)(2,1)S(1)} %copy-done.6), channel_id=1, source_target_pairs={{0,1},{1,0},{2,3},{3,2},{4,5},{5,4},{6,7},{7,6},{8,9},{9,8},{10,11... | collective-permute-start | bytes 3145736 | tf_op jit(solution)/shard_map/ppermute | solution.py:37
  41.1 20.8 %collective-permute-start.9 = (bf16[64,4096]{1,0:T(8,128)(2,1)}, bf16[64,4096]{1,0:T(8,128)(2,1)S(1)}, u32[]{:S(2)}, u32[]{:S(2)}) collective-permute-start(bf16[64,4096]{1,0:T(8,128)(2,1)} %bitcast.17), channel_id=1, source_target_pairs={{0,1},{1,0},{2,3},{3,2},{4,5},{5,4},{6,7},{7,6},{8,9},{9,8},{10,11... | collective-permute-start | bytes 1572872 | tf_op jit(solution)/shard_map/ppermute | solution.py:37
  41.5 20.4 %collective-permute-start.10 = (bf16[64,4096]{1,0:T(8,128)(2,1)}, bf16[64,4096]{1,0:T(8,128)(2,1)S(1)}, u32[]{:S(2)}, u32[]{:S(2)}) collective-permute-start(bf16[64,4096]{1,0:T(8,128)(2,1)} %bitcast.15), channel_id=1, source_target_pairs={{0,1},{1,0},{2,3},{3,2},{4,5},{5,4},{6,7},{7,6},{8,9},{9,8},{10,11... | collective-permute-start | bytes 1572872 | tf_op jit(solution)/shard_map/ppermute | solution.py:37
  49.4 16.1 %copy-start.9 = (bf16[1536,192]{0,1:T(8,128)(2,1)S(1)}, bf16[1536,192]{0,1:T(8,128)(2,1)}, u32[]{:S(2)}) copy-start(bf16[1536,192]{0,1:T(8,128)(2,1)} %param.26) | copy-start | bytes 1769476
  61.9 25.5 %collective-permute-start.13 = (bf16[4096,256]{1,0:T(8,128)(2,1)S(1)}, bf16[4096,256]{1,0:T(8,128)(2,1)S(1)}, u32[]{:S(2)}, u32[]{:S(2)}) collective-permute-start(bf16[4096,256]{1,0:T(8,128)(2,1)S(1)} %copy-done.3), channel_id=1, source_target_pairs={{0,1},{1,0},{2,3},{3,2},{4,5},{5,4},{6,7},{7,6},{8,9},{9,8},{10,11... | collective-permute-start | bytes 6291464 | tf_op jit(solution)/shard_map/ppermute | solution.py:37
  65.0 22.4 %collective-permute-start.14 = (bf16[4096,256]{1,0:T(8,128)(2,1)S(1)}, bf16[4096,256]{1,0:T(8,128)(2,1)S(1)}, u32[]{:S(2)}, u32[]{:S(2)}) collective-permute-start(bf16[4096,256]{1,0:T(8,128)(2,1)S(1)} %copy-done.2), channel_id=1, source_target_pairs={{0,1},{1,0},{2,3},{3,2},{4,5},{5,4},{6,7},{7,6},{8,9},{9,8},{10,11... | collective-permute-start | bytes 6291464 | tf_op jit(solution)/shard_map/ppermute | solution.py:37
  65.1 22.3 %collective-permute-start.15 = (bf16[192,4096]{1,0:T(8,128)(2,1)S(1)}, bf16[192,4096]{1,0:T(8,128)(2,1)S(1)}, u32[]{:S(2)}, u32[]{:S(2)}) collective-permute-start(bf16[192,4096]{1,0:T(8,128)(2,1)S(1)} %bitcast.10), channel_id=1, source_target_pairs={{0,1},{1,0},{2,3},{3,2},{4,5},{5,4},{6,7},{7,6},{8,9},{9,8},{10,11... | collective-permute-start | bytes 4718600 | tf_op jit(solution)/shard_map/ppermute | solution.py:37
  65.6 21.8 %collective-permute-start.16 = (bf16[192,1536]{1,0:T(8,128)(2,1)S(1)}, bf16[192,1536]{1,0:T(8,128)(2,1)S(1)}, u32[]{:S(2)}, u32[]{:S(2)}) collective-permute-start(bf16[192,1536]{1,0:T(8,128)(2,1)S(1)} %bitcast.13), channel_id=1, source_target_pairs={{0,1},{1,0},{2,3},{3,2},{4,5},{5,4},{6,7},{7,6},{8,9},{9,8},{10,11... | collective-permute-start | bytes 1769480 | tf_op jit(solution)/shard_map/ppermute | solution.py:37
  75.3 23.1 %copy-start.11 = (bf16[4096,64]{0,1:T(8,128)(2,1)S(1)}, bf16[4096,64]{0,1:T(8,128)(2,1)}, u32[]{:S(2)}) copy-start(bf16[4096,64]{0,1:T(8,128)(2,1)} %param.29) | copy-start | bytes 1572868
  76.4 33.1 %copy-start.10 = (bf16[4096,64]{0,1:T(8,128)(2,1)S(1)}, bf16[4096,64]{0,1:T(8,128)(2,1)}, u32[]{:S(2)}) copy-start(bf16[4096,64]{0,1:T(8,128)(2,1)} %param.32) | copy-start | bytes 1572868
  183.5 15.7 %collective-permute-start.17 = (bf16[16,640]{1,0:T(8,128)(2,1)S(1)}, bf16[16,640]{1,0:T(8,128)(2,1)S(1)}, u32[]{:S(2)}, u32[]{:S(2)}) collective-permute-start(bf16[16,640]{1,0:T(8,128)(2,1)S(1)} %get-tuple-element.152), channel_id=1, source_target_pairs={{0,1},{1,0},{2,3},{3,2},{4,5},{5,4},{6,7},{7,6},{8,9},{9,8},{10,11... | collective-permute-start | bytes 61448 | tf_op jit(solution)/shard_map/ppermute | solution.py:37
  (6 other events, 74.8 us)

commit v5 on v4

--- a/solution.py
+++ b/solution.py
@@ -398,15 +398,21 @@
         own_mask, other_mask = piece_masks(masks, level)
         own = own * own_mask
         other = other * other_mask
-    store_copies(out, in_order(own, other))
+        store_copies(out, in_order(own, other))
+    else:
+        out[...] = in_order(own, other).astype(BF16)
 
 
 def out_kernel(
-    gathered, own_owner, other_owner, own_first, other_first, own_second, other_second,
-    own_third, other_third, own_upper, other_upper, out,
+    own_part, first_part, second_part, third_part, own_owner, other_owner, own_first, other_first,
+    own_second, other_second, own_third, other_third, own_upper, other_upper, out, row,
 ):
+    chip = lax.axis_index("x")
     core = core_index()
-    full = joined(gathered)
+    for step, part in enumerate((own_part, first_part, second_part, third_part)):
+        start = pl.multiple_of((chip ^ step) * (2 * LEAF), 128)
+        row[:, pl.ds(start, 2 * LEAF)] = part[...]
+    full = row[...]
     tails = ((own_first, own_second, own_third), (other_first, other_second, other_third))
     placed = []
     uppers = (own_upper, other_upper)
@@ -425,17 +431,19 @@
     out[...] = stacked.T.reshape(64, 8, 128).astype(BF16)
 
 
-def final_kernel(received, own_columns, other_columns, own_out, other_out):
+def final_kernel(received, far, columns, out):
     core = core_index()
-    turned = received[...].reshape(512, 128).astype(F32).T
-    first = jnp.concatenate([turned[:HALF], turned[2 * HALF : 3 * HALF]], axis=1)
-    second = jnp.concatenate([turned[HALF : 2 * HALF], turned[3 * HALF : 4 * HALF]], axis=1)
-    own = jnp.where(core == 0, first, second).astype(BF16)
-    other = jnp.where(core == 0, second, first).astype(BF16)
-    work = ((own, own_columns, own_out), (other, other_columns, other_out))
-    for value, columns, out in work:
-        hot = one_hot(rows_of((640, 1024)) == columns[0:1, :])
-        out[...] = dot_turned(value, hot).astype(BF16)
+    halves = []
+    for ref in (received, far):
+        turned = ref[...].reshape(512, 128).astype(F32).T
+        first = jnp.concatenate([turned[:HALF], turned[2 * HALF : 3 * HALF]], axis=1)
+        second = jnp.concatenate([turned[HALF : 2 * HALF], turned[3 * HALF : 4 * HALF]], axis=1)
+        halves.append(jnp.where(core == 0, first, second))
+    top = jnp.where(core == 0, halves[0], halves[1])
+    bottom = jnp.where(core == 0, halves[1], halves[0])
+    value = jnp.concatenate([top, bottom], axis=0).astype(BF16)
+    hot = one_hot(rows_of((640, 1024)) == columns[0:1, :])
+    out[...] = dot_turned(value, hot).astype(BF16)
 
 
 def per_device(
@@ -461,7 +469,6 @@
     pattern_second,
     pattern_third,
 ):
-    core = lax.axis_index("c")
     factors = {
         "lower1": lower_first,
         "down2": downlink_second,
@@ -612,36 +619,36 @@
         level_x[level] = (own_x, other_x)
         gathered = exchange(copies, level)
         below = level - 1
+        shape = (HALF, 2 * WIDTHS[below])
         copies = call(
             functools.partial(back_kernel, below),
             "back_%d" % below,
-            [((MEMBERS[below], HALF, 2 * WIDTHS[below]), BF16)],
+            [((MEMBERS[below],) + shape if below else shape, BF16)],
             (gathered, masks) + patterns + level_y[below] + pairs["back%d" % level],
         )[0]
-    gathered = exchange(copies, 0)
+    parts = [copies]
+    for step in (1, 2, 3):
+        ring = [(source, source ^ step) for source in range(4)]
+        parts.append(lax.ppermute(copies, "x", ring))
     outbound = call(
         out_kernel,
         "leaf_solution",
         [((64, 8, 128), BF16)],
-        (gathered, own_columns, other_columns)
+        tuple(parts)
+        + (own_columns, other_columns)
         + level_x[1]
         + level_x[2]
         + level_x[3]
         + pairs["upper0"],
+        scratch=[pltpu.VMEM((HALF, 8 * LEAF), BF16)],
     )[0]
     returned = exchange(outbound, 4)
-    own_half, other_half = call(
+    return call(
         final_kernel,
         "natural_order",
-        [((HALF, 640), BF16), ((HALF, 640), BF16)],
-        (returned, own_columns, other_columns),
-    )
-    far_half = swap(other_half)
-    return jnp.where(
-        core == 0,
-        jnp.concatenate([own_half, far_half]),
-        jnp.concatenate([far_half, own_half]),
-    )
+        [((2 * HALF, 640), BF16)],
+        (returned, swap(returned), own_columns),
+    )[0]
 
 
 def solution(mesh):

time: 200 us -> 200 us (level)
  blocking collectives: 157 us -> 151 us
  starting transfers between devices: 25.5 us -> 29.3 us
    all_to_all x15 -> x14, blocking collectives: 157 us -> 151 us  [exchange(): lax.all_to_all(value, CHIPS[level], split_axis=0, concat_axis=0, tiled=True)]
    ppermute x0 -> x3, starting transfers between devices: none -> 3.28 us  [per_device(): parts.append(lax.ppermute(copies, 'x', ring))]
  transfers between devices with their start and end apart: 18 -> 21, of which waited for: 3 -> 5; matrix products, arithmetic and copies ran while one was open for 0% -> 0% of each run, Pallas kernels for 2% -> 2%
where the time goes in v5:
time: 200 us; the launch traced here: 199 us
  blocking collectives  151 us (76%)
  starting transfers between devices  29.3 us (15%)
  Pallas kernels  15.2 us (8%)
  waiting for transfers between devices  3.65 us (2%)
    all_to_all x14, blocking collectives, exchange(): lax.all_to_all(value, CHIPS[level], split_axis=0, concat_axis=0, tiled=True)  151 us
    ppermute x18, starting transfers between devices, swap(): return lax.ppermute(value, 'c', [(0, 1), (1, 0)])  26 us
    pallas_call x18, Pallas kernels, call(): pl.pallas_call(body, name=name, out_shape=[jax.ShapeDtypeStruct(shape, dt...  15.2 us
  transfers between devices with their start and end apart: 21, of which 5 were waited for; matrix products, arithmetic and copies ran while one was open for 0% of the time, Pallas kernels for 2%

profile of v5, /device:TPU:1, one launch (start us, length us, event | category | flops | bytes accessed | tf_op | source)
XLA Modules:
  0.0 199.2 jit_solution(9517478722972872433)
XLA Ops:
  0.0 2.1 %start.1 = (bf16[16,8,128]{2,1,0:T(8,128)(2,1)S(1)}, bf16[16,8,128]{2,1,0:T(8,128)(2,1)S(1)}, bf16[16,4096]{1,0:T(8,128)(2,1)S(1)}, f32[8,896]{1,0:T(8,128)S(1)}...) custom-call(s32[14]{0:T(128)} %live.1, s32[640]{0:T(1024)} %send_order.1, ...), custom_call_target="tpu_custom_call" | custom-call | tf_op jit(solution)/shard_map/start/pallas_call | solution.py:49
  2.1 1.5 collective-permute-start.2
  6.0 21.1 %all_to_all.70.received = bf16[64,16,128]{2,1,0:T(8,128)(2,1)S(1)} all-to-all(bf16[64,16,128]{2,1,0:T(8,128)(2,1)S(1)} %bitcast.12), channel_id=1, replica_groups=mesh['z1'=2,'z0'=2,'y1'=2,'y0'=2,'x'=4,'c'=2] {'z1','z0','y1','y0','x'}, dimensions={0} | all-to-all | bytes 524288 | tf_op jit(solution)/shard_map/all_to_all | solution.py:41
  27.2 2.0 %leaf_front.1 = (bf16[16,192]{1,0:T(8,128)(2,1)S(1)}, bf16[16,192]{1,0:T(8,128)(2,1)S(1)}, bf16[32,1024]{1,0:T(8,128)(2,1)S(1)}, bf16[8,16,512]{2,1,0:T(8,128)(2,1)S(1)}) custom-call(bf16[64,16,128]{2,1,0:T(8,128)(2,1)S(1)} %all_to_all.70.received, bf16[16,4096]{1,0:T(8,128)(2,1)S(1)} %get-tuple-element.80.own_pattern, ...), custom_call_target="tpu_custom_call" | custom-call | tf_op jit(solution)/shard_map/leaf_front/pallas_call | solution.py:49
  29.8 1.6 collective-permute-start.7
  31.5 7.8 %all_to_all.71.received = bf16[8,16,512]{2,1,0:T(8,128)(2,1)S(1)} all-to-all(bf16[8,16,512]{2,1,0:T(8,128)(2,1)S(1)} %get-tuple-element.100), channel_id=1, replica_groups=mesh['z1'=2,'z0'=2,'y1'=2,'y0'=2,'x'=4,'c'=2] {'y0','x'}, dimensions={0} | all-to-all | bytes 262144 | tf_op jit(solution)/shard_map/all_to_all | solution.py:41
  39.4 1.6 collective-permute-start.11
  41.6 7.8 %all_to_all.72.gathered = bf16[8,16,512]{2,1,0:T(8,128)(2,1)S(1)} all-to-all(bf16[8,16,512]{2,1,0:T(8,128)(2,1)S(1)} %reduce_1.1), channel_id=1, replica_groups=mesh['z1'=2,'z0'=2,'y1'=2,'y0'=2,'x'=4,'c'=2] {'y0','x'}, dimensions={0} | all-to-all | bytes 262144 | tf_op jit(solution)/shard_map/all_to_all | solution.py:41
  49.5 2.0 %up_1.1 = (bf16[16,256]{1,0:T(8,128)(2,1)S(1)}, bf16[16,256]{1,0:T(8,128)(2,1)S(1)}, bf16[16,16,256]{2,1,0:T(8,128)(2,1)S(1)}) custom-call(bf16[8,16,512]{2,1,0:T(8,128)(2,1)S(1)} %all_to_all.72.gathered, f32[8,896]{1,0:T(8,128)S(1)} %get-tuple-element.102.masks, bf16[16,4096]{1,0:T(8,128)(2,1)S(1)} %get-tuple-element.80.own_pattern, ...), custom_call_target="tpu_custom_call" | custom-call | tf_op jit(solution)/shard_map/up_1/pallas_call | solution.py:49
  51.5 10.4 %all_to_all.73.received = bf16[16,16,256]{2,1,0:T(8,128)(2,1)S(1)} all-to-all(bf16[16,16,256]{2,1,0:T(8,128)(2,1)S(1)} %get-tuple-element.109), channel_id=1, replica_groups=mesh['z1'=2,'z0'=2,'y1'=2,'y0'=2,'x'=4,'c'=2] {'y1','y0','x'}, dimensions={0} | all-to-all | bytes 262144 | tf_op jit(solution)/shard_map/all_to_all | solution.py:41
  61.9 3.1 %collective-permute-start.13 = (bf16[4096,256]{1,0:T(8,128)(2,1)S(1)}, bf16[4096,256]{1,0:T(8,128)(2,1)S(1)}, u32[]{:S(2)}, u32[]{:S(2)}) collective-permute-start(bf16[4096,256]{1,0:T(8,128)(2,1)S(1)} %copy-done.3), channel_id=1, source_target_pairs={{0,1},{1,0},{2,3},{3,2},{4,5},{5,4},{6,7},{7,6},{8,9},{9,8},{10,11... | collective-permute-start | bytes 6291464 | tf_op jit(solution)/shard_map/ppermute | solution.py:37
  65.7 9.6 %all_to_all.74.gathered = bf16[16,16,256]{2,1,0:T(8,128)(2,1)S(1)} all-to-all(bf16[16,16,256]{2,1,0:T(8,128)(2,1)S(1)} %reduce_2.1), channel_id=1, replica_groups=mesh['z1'=2,'z0'=2,'y1'=2,'y0'=2,'x'=4,'c'=2] {'y1','y0','x'}, dimensions={0} | all-to-all | bytes 262144 | tf_op jit(solution)/shard_map/all_to_all | solution.py:41
  76.4 10.9 %all_to_all.75.received = bf16[32,16,128]{2,1,0:T(8,128)(2,1)S(1)} all-to-all(bf16[32,16,128]{2,1,0:T(8,128)(2,1)S(1)} %get-tuple-element.119), channel_id=1, replica_groups=mesh['z1'=2,'z0'=2,'y1'=2,'y0'=2,'x'=4,'c'=2] {'z0','y1','y0','x'}, dimensions={0} | all-to-all | bytes 262144 | tf_op jit(solution)/shard_map/all_to_all | solution.py:41
  87.4 10.9 %all_to_all.76.gathered = bf16[32,16,128]{2,1,0:T(8,128)(2,1)S(1)} all-to-all(bf16[32,16,128]{2,1,0:T(8,128)(2,1)S(1)} %reduce_3.1), channel_id=1, replica_groups=mesh['z1'=2,'z0'=2,'y1'=2,'y0'=2,'x'=4,'c'=2] {'z0','y1','y0','x'}, dimensions={0} | all-to-all | bytes 262144 | tf_op jit(solution)/shard_map/all_to_all | solution.py:41
  98.8 10.7 %all_to_all.77.gathered = bf16[32,16,128]{2,1,0:T(8,128)(2,1)S(1)} all-to-all(bf16[32,16,128]{2,1,0:T(8,128)(2,1)S(1)} %top_lower.1), channel_id=1, replica_groups=mesh['z1'=2,'z0'=2,'y1'=2,'y0'=2,'x'=4,'c'=2] {'z0','y1','y0','x'}, dimensions={0} | all-to-all | bytes 262144 | tf_op jit(solution)/shard_map/all_to_all | solution.py:41
  110.0 10.7 %all_to_all.78.gathered = bf16[32,16,128]{2,1,0:T(8,128)(2,1)S(1)} all-to-all(bf16[32,16,128]{2,1,0:T(8,128)(2,1)S(1)} %get-tuple-element.128), channel_id=1, replica_groups=mesh['z1'=2,'z0'=2,'y1'=2,'y0'=2,'x'=4,'c'=2] {'z0','y1','y0','x'}, dimensions={0} | all-to-all | bytes 262144 | tf_op jit(solution)/shard_map/all_to_all | solution.py:41
  121.2 10.0 %all_to_all.79.gathered = bf16[16,16,256]{2,1,0:T(8,128)(2,1)S(1)} all-to-all(bf16[16,16,256]{2,1,0:T(8,128)(2,1)S(1)} %back_2.1), channel_id=1, replica_groups=mesh['z1'=2,'z0'=2,'y1'=2,'y0'=2,'x'=4,'c'=2] {'y1','y0','x'}, dimensions={0} | all-to-all | bytes 262144 | tf_op jit(solution)/shard_map/all_to_all | solution.py:41
  131.6 9.6 %all_to_all.80.gathered = bf16[16,16,256]{2,1,0:T(8,128)(2,1)S(1)} all-to-all(bf16[16,16,256]{2,1,0:T(8,128)(2,1)S(1)} %get-tuple-element.133), channel_id=1, replica_groups=mesh['z1'=2,'z0'=2,'y1'=2,'y0'=2,'x'=4,'c'=2] {'y1','y0','x'}, dimensions={0} | all-to-all | bytes 262144 | tf_op jit(solution)/shard_map/all_to_all | solution.py:41
  142.1 8.2 %all_to_all.81.gathered = bf16[8,16,512]{2,1,0:T(8,128)(2,1)S(1)} all-to-all(bf16[8,16,512]{2,1,0:T(8,128)(2,1)S(1)} %back_1.1), channel_id=1, replica_groups=mesh['z1'=2,'z0'=2,'y1'=2,'y0'=2,'x'=4,'c'=2] {'y0','x'}, dimensions={0} | all-to-all | bytes 262144 | tf_op jit(solution)/shard_map/all_to_all | solution.py:41
  151.0 7.8 %all_to_all.82.gathered = bf16[8,16,512]{2,1,0:T(8,128)(2,1)S(1)} all-to-all(bf16[8,16,512]{2,1,0:T(8,128)(2,1)S(1)} %get-tuple-element.138), channel_id=1, replica_groups=mesh['z1'=2,'z0'=2,'y1'=2,'y0'=2,'x'=4,'c'=2] {'y0','x'}, dimensions={0} | all-to-all | bytes 262144 | tf_op jit(solution)/shard_map/all_to_all | solution.py:41
  161.0 1.4 collective-permute-start.18
  165.0 1.6 leaf_solution.1
  166.6 15.2 %all_to_all.83.received = bf16[64,8,128]{2,1,0:T(8,128)(2,1)S(1)} all-to-all(bf16[64,8,128]{2,1,0:T(8,128)(2,1)S(1)} %leaf_solution.1), channel_id=1, replica_groups=mesh['z1'=2,'z0'=2,'y1'=2,'y0'=2,'x'=4,'c'=2] {'z1','z0','y1','y0','x'}, dimensions={0} | all-to-all | bytes 262144 | tf_op jit(solution)/shard_map/all_to_all | solution.py:41
  181.8 15.3 %collective-permute-start.20 = (bf16[64,8,128]{2,1,0:T(8,128)(2,1)S(1)}, bf16[64,8,128]{2,1,0:T(8,128)(2,1)S(1)}, u32[]{:S(2)}, u32[]{:S(2)}) collective-permute-start(bf16[64,8,128]{2,1,0:T(8,128)(2,1)S(1)} %all_to_all.83.received), channel_id=1, source_target_pairs={{0,1},{1,0},{2,3},{3,2},{4,5},{5,4},{6,7},{7,6},{8,9},{9,8},{10,11... | collective-permute-start | bytes 393224 | tf_op jit(solution)/shard_map/ppermute | solution.py:37
  (74 shorter events, 15.9 us)
Async XLA Ops:
  2.1 2.9 %collective-permute-start.2 = (bf16[16,4096]{1,0:T(8,128)(2,1)S(1)}, bf16[16,4096]{1,0:T(8,128)(2,1)S(1)}, u32[]{:S(2)}, u32[]{:S(2)}) collective-permute-start(bf16[16,4096]{1,0:T(8,128)(2,1)S(1)} %get-tuple-element.80.own_pattern), channel_id=1, source_target_pairs={{0,1},{1,0},{2,3},{3,2},{4,5},{5,4},{6,7},{7,6},{8,9},{9,8},{10,11... | collective-permute-start | bytes 393224 | tf_op jit(solution)/shard_map/ppermute | solution.py:37
  3.6 1.2 collective-permute-start
  3.7 1.3 collective-permute-start.1
  4.8 26.6 %copy-start.8 = (bf16[4096,128]{1,0:T(8,128)(2,1)S(1)}, bf16[4096,128]{1,0:T(8,128)(2,1)}, u32[]{:S(2)}) copy-start(bf16[4096,128]{1,0:T(8,128)(2,1)} %own_link.5) | copy-start | bytes 3145732
  5.0 22.2 %collective-permute-start.5 = (bf16[4096,256]{1,0:T(8,128)(2,1)S(1)}, bf16[4096,256]{1,0:T(8,128)(2,1)S(1)}, u32[]{:S(2)}, u32[]{:S(2)}) collective-permute-start(bf16[4096,256]{1,0:T(8,128)(2,1)S(1)} %copy-done), channel_id=1, source_target_pairs={{0,1},{1,0},{2,3},{3,2},{4,5},{5,4},{6,7},{7,6},{8,9},{9,8},{10,11... | collective-permute-start | bytes 6291464 | tf_op jit(solution)/shard_map/ppermute | solution.py:37
  5.4 21.9 %collective-permute-start.6 = (bf16[4096,256]{1,0:T(8,128)(2,1)}, bf16[4096,256]{1,0:T(8,128)(2,1)S(1)}, u32[]{:S(2)}, u32[]{:S(2)}) collective-permute-start(bf16[4096,256]{1,0:T(8,128)(2,1)} %own_link.4), channel_id=1, source_target_pairs={{0,1},{1,0},{2,3},{3,2},{4,5},{5,4},{6,7},{7,6},{8,9},{9,8},{10,11... | collective-permute-start | bytes 6291464 | tf_op jit(solution)/shard_map/ppermute | solution.py:37
  5.5 21.7 %collective-permute-start.4 = (bf16[192,4096]{1,0:T(8,128)(2,1)S(1)}, bf16[192,4096]{1,0:T(8,128)(2,1)S(1)}, u32[]{:S(2)}, u32[]{:S(2)}) collective-permute-start(bf16[192,4096]{1,0:T(8,128)(2,1)S(1)} %get-tuple-element.86.own_link), channel_id=1, source_target_pairs={{0,1},{1,0},{2,3},{3,2},{4,5},{5,4},{6,7},{7,6},{8,9},{9,8},{10,11... | collective-permute-start | bytes 4718600 | tf_op jit(solution)/shard_map/ppermute | solution.py:37
  5.9 21.3 %collective-permute-start.3 = (bf16[192,1536]{1,0:T(8,128)(2,1)S(1)}, bf16[192,1536]{1,0:T(8,128)(2,1)S(1)}, u32[]{:S(2)}, u32[]{:S(2)}) collective-permute-start(bf16[192,1536]{1,0:T(8,128)(2,1)S(1)} %get-tuple-element.85.own_lower), channel_id=1, source_target_pairs={{0,1},{1,0},{2,3},{3,2},{4,5},{5,4},{6,7},{7,6},{8,9},{9,8},{10,11... | collective-permute-start | bytes 1769480 | tf_op jit(solution)/shard_map/ppermute | solution.py:37
  6.0 23.7 %copy-start.7 = (bf16[4096,128]{1,0:T(8,128)(2,1)S(1)}, bf16[4096,128]{1,0:T(8,128)(2,1)}, u32[]{:S(2)}) copy-start(bf16[4096,128]{1,0:T(8,128)(2,1)} %own_lower.3) | copy-start | bytes 3145732
  29.8 9.6 %collective-permute-start.7 = (bf16[4096,128]{1,0:T(8,128)(2,1)S(1)}, bf16[4096,128]{1,0:T(8,128)(2,1)S(1)}, u32[]{:S(2)}, u32[]{:S(2)}) collective-permute-start(bf16[4096,128]{1,0:T(8,128)(2,1)S(1)} %copy-done.7), channel_id=1, source_target_pairs={{0,1},{1,0},{2,3},{3,2},{4,5},{5,4},{6,7},{7,6},{8,9},{9,8},{10,11... | collective-permute-start | bytes 3145736 | tf_op jit(solution)/shard_map/ppermute | solution.py:37
  31.4 8.0 %collective-permute-start.8 = (bf16[4096,128]{1,0:T(8,128)(2,1)S(1)}, bf16[4096,128]{1,0:T(8,128)(2,1)S(1)}, u32[]{:S(2)}, u32[]{:S(2)}) collective-permute-start(bf16[4096,128]{1,0:T(8,128)(2,1)S(1)} %copy-done.8), channel_id=1, source_target_pairs={{0,1},{1,0},{2,3},{3,2},{4,5},{5,4},{6,7},{7,6},{8,9},{9,8},{10,11... | collective-permute-start | bytes 3145736 | tf_op jit(solution)/shard_map/ppermute | solution.py:37
  39.4 22.5 %collective-permute-start.11 = (bf16[4096,128]{1,0:T(8,128)(2,1)S(1)}, bf16[4096,128]{1,0:T(8,128)(2,1)S(1)}, u32[]{:S(2)}, u32[]{:S(2)}) collective-permute-start(bf16[4096,128]{1,0:T(8,128)(2,1)S(1)} %copy-done.5), channel_id=1, source_target_pairs={{0,1},{1,0},{2,3},{3,2},{4,5},{5,4},{6,7},{7,6},{8,9},{9,8},{10,11... | collective-permute-start | bytes 3145736 | tf_op jit(solution)/shard_map/ppermute | solution.py:37
  41.0 20.9 %collective-permute-start.12 = (bf16[4096,128]{1,0:T(8,128)(2,1)S(1)}, bf16[4096,128]{1,0:T(8,128)(2,1)S(1)}, u32[]{:S(2)}, u32[]{:S(2)}) collective-permute-start(bf16[4096,128]{1,0:T(8,128)(2,1)S(1)} %copy-done.6), channel_id=1, source_target_pairs={{0,1},{1,0},{2,3},{3,2},{4,5},{5,4},{6,7},{7,6},{8,9},{9,8},{10,11... | collective-permute-start | bytes 3145736 | tf_op jit(solution)/shard_map/ppermute | solution.py:37
  41.1 20.8 %collective-permute-start.9 = (bf16[64,4096]{1,0:T(8,128)(2,1)}, bf16[64,4096]{1,0:T(8,128)(2,1)S(1)}, u32[]{:S(2)}, u32[]{:S(2)}) collective-permute-start(bf16[64,4096]{1,0:T(8,128)(2,1)} %bitcast.17), channel_id=1, source_target_pairs={{0,1},{1,0},{2,3},{3,2},{4,5},{5,4},{6,7},{7,6},{8,9},{9,8},{10,11... | collective-permute-start | bytes 1572872 | tf_op jit(solution)/shard_map/ppermute | solution.py:37
  41.5 20.4 %collective-permute-start.10 = (bf16[64,4096]{1,0:T(8,128)(2,1)}, bf16[64,4096]{1,0:T(8,128)(2,1)S(1)}, u32[]{:S(2)}, u32[]{:S(2)}) collective-permute-start(bf16[64,4096]{1,0:T(8,128)(2,1)} %bitcast.15), channel_id=1, source_target_pairs={{0,1},{1,0},{2,3},{3,2},{4,5},{5,4},{6,7},{7,6},{8,9},{9,8},{10,11... | collective-permute-start | bytes 1572872 | tf_op jit(solution)/shard_map/ppermute | solution.py:37
  61.9 25.5 %collective-permute-start.13 = (bf16[4096,256]{1,0:T(8,128)(2,1)S(1)}, bf16[4096,256]{1,0:T(8,128)(2,1)S(1)}, u32[]{:S(2)}, u32[]{:S(2)}) collective-permute-start(bf16[4096,256]{1,0:T(8,128)(2,1)S(1)} %copy-done.3), channel_id=1, source_target_pairs={{0,1},{1,0},{2,3},{3,2},{4,5},{5,4},{6,7},{7,6},{8,9},{9,8},{10,11... | collective-permute-start | bytes 6291464 | tf_op jit(solution)/shard_map/ppermute | solution.py:37
  65.0 22.4 %collective-permute-start.14 = (bf16[4096,256]{1,0:T(8,128)(2,1)S(1)}, bf16[4096,256]{1,0:T(8,128)(2,1)S(1)}, u32[]{:S(2)}, u32[]{:S(2)}) collective-permute-start(bf16[4096,256]{1,0:T(8,128)(2,1)S(1)} %copy-done.2), channel_id=1, source_target_pairs={{0,1},{1,0},{2,3},{3,2},{4,5},{5,4},{6,7},{7,6},{8,9},{9,8},{10,11... | collective-permute-start | bytes 6291464 | tf_op jit(solution)/shard_map/ppermute | solution.py:37
  65.1 22.3 %collective-permute-start.15 = (bf16[192,4096]{1,0:T(8,128)(2,1)S(1)}, bf16[192,4096]{1,0:T(8,128)(2,1)S(1)}, u32[]{:S(2)}, u32[]{:S(2)}) collective-permute-start(bf16[192,4096]{1,0:T(8,128)(2,1)S(1)} %bitcast.10), channel_id=1, source_target_pairs={{0,1},{1,0},{2,3},{3,2},{4,5},{5,4},{6,7},{7,6},{8,9},{9,8},{10,11... | collective-permute-start | bytes 4718600 | tf_op jit(solution)/shard_map/ppermute | solution.py:37
  65.6 21.8 %collective-permute-start.16 = (bf16[192,1536]{1,0:T(8,128)(2,1)S(1)}, bf16[192,1536]{1,0:T(8,128)(2,1)S(1)}, u32[]{:S(2)}, u32[]{:S(2)}) collective-permute-start(bf16[192,1536]{1,0:T(8,128)(2,1)S(1)} %bitcast.13), channel_id=1, source_target_pairs={{0,1},{1,0},{2,3},{3,2},{4,5},{5,4},{6,7},{7,6},{8,9},{9,8},{10,11... | collective-permute-start | bytes 1769480 | tf_op jit(solution)/shard_map/ppermute | solution.py:37
  76.4 33.1 %copy-start.10 = (bf16[4096,64]{0,1:T(8,128)(2,1)S(1)}, bf16[4096,64]{0,1:T(8,128)(2,1)}, u32[]{:S(2)}) copy-start(bf16[4096,64]{0,1:T(8,128)(2,1)} %param.32) | copy-start | bytes 1572868
  160.0 3.8 %collective-permute-start.19 = (bf16[16,384]{1,0:T(8,128)(2,1)S(1)}, bf16[16,384]{1,0:T(8,128)(2,1)S(1)}, u32[]{:S(2)}, u32[]{:S(2)}) collective-permute-start(bf16[16,384]{1,0:T(8,128)(2,1)S(1)} %back_0.1.own_part), channel_id=1, source_target_pairs={{0,6},{2,4},{4,2},{6,0},{1,7},{3,5},{5,3},{7,1},{8,14},{10,12},{12... | collective-permute-start | bytes 36872 | tf_op jit(solution)/shard_map/ppermute | solution.py:632
  161.0 4.0 %collective-permute-start.18 = (bf16[16,384]{1,0:T(8,128)(2,1)S(1)}, bf16[16,384]{1,0:T(8,128)(2,1)S(1)}, u32[]{:S(2)}, u32[]{:S(2)}) collective-permute-start(bf16[16,384]{1,0:T(8,128)(2,1)S(1)} %back_0.1.own_part), channel_id=1, source_target_pairs={{0,4},{2,6},{4,0},{6,2},{1,5},{3,7},{5,1},{7,3},{8,12},{10,14},{12... | collective-permute-start | bytes 36872 | tf_op jit(solution)/shard_map/ppermute | solution.py:632
  162.4 2.7 %collective-permute-start.17 = (bf16[16,384]{1,0:T(8,128)(2,1)S(1)}, bf16[16,384]{1,0:T(8,128)(2,1)S(1)}, u32[]{:S(2)}, u32[]{:S(2)}) collective-permute-start(bf16[16,384]{1,0:T(8,128)(2,1)S(1)} %back_0.1.own_part), channel_id=1, source_target_pairs={{0,2},{2,0},{4,6},{6,4},{1,3},{3,1},{5,7},{7,5},{8,10},{10,8},{12,... | collective-permute-start | bytes 36872 | tf_op jit(solution)/shard_map/ppermute | solution.py:632
  181.8 16.3 %collective-permute-start.20 = (bf16[64,8,128]{2,1,0:T(8,128)(2,1)S(1)}, bf16[64,8,128]{2,1,0:T(8,128)(2,1)S(1)}, u32[]{:S(2)}, u32[]{:S(2)}) collective-permute-start(bf16[64,8,128]{2,1,0:T(8,128)(2,1)S(1)} %all_to_all.83.received), channel_id=1, source_target_pairs={{0,1},{1,0},{2,3},{3,2},{4,5},{5,4},{6,7},{7,6},{8,9},{9,8},{10,11... | collective-permute-start | bytes 393224 | tf_op jit(solution)/shard_map/ppermute | solution.py:37
  (9 other events, 136.3 us)

commit v6 on v5

--- a/solution.py
+++ b/solution.py
@@ -123,16 +123,12 @@
     return [patterns[start + row : start + row + 1, :].astype(F32) for row in range(count)]
 
 
-def pick_rows(send_order, owner_order, right, mine, theirs):
+def pick_rows(send_order, owner_order, right, order, mine, theirs):
     core = core_index()
     send = send_order[...].reshape(1, 640)
     owner = owner_order[...].reshape(1, 640)
     natural = dot(right[...], one_hot(rows_of((640, 640)) == send)).astype(BF16)
-    lane = lanes((1, 1024))
-    turn = lane & 7
-    wanted = (((lane >> 3) & 15) * 8 + (lane >> 7)) * 5 + turn
-    wanted = jnp.where(turn < 5, wanted, -1)
-    picked = dot(natural, one_hot(rows_of((640, 1024)) == wanted))
+    picked = dot(natural, order)
     source, turn = source_and_turn(owner)
     high = jnp.broadcast_to(source[:, :256].astype(F32), (8, 256))
     low = jnp.broadcast_to(turn[:, :256].astype(F32), (8, 256))
@@ -171,7 +167,9 @@
         out[:, copy] = tiles
 
 
-def make_tables(live, send_order, owner_order, first, second, third, wide, masks, columns):
+def make_tables(
+    live, send_order, owner_order, first, second, third, order, wide, masks, columns
+):
     hot = one_hot(lanes((BLOCK, SEP)) // BLOCK == rows_of((BLOCK, SEP)))
     start = 0
     wide[...] = jnp.zeros_like(wide)
@@ -189,11 +187,6 @@
         row = (member * 4 + chip) * width + lanes((8, width))
         count = live[FIRST_NODE[level] + (leaf >> level)]
         masks[:, start : start + width] = (row < count).astype(F32)
-    lane = lanes((1, 1024))
-    turn = lane & 7
-    device = ((lane >> 3) & 63) * 2 + (lane >> 9)
-    wanted = jnp.where(turn < 5, device * 5 + turn, -1)
-    hot = one_hot(rows_of((640, 1024)) == wanted)
     send = send_order[...].reshape(1, 640) + 1
     stacked = jnp.concatenate(
         [
@@ -202,7 +195,7 @@
         ],
         axis=0,
     )
-    placed = dot(stacked.astype(BF16), hot)
+    placed = dot(stacked.astype(BF16), order)
     row = rows_of((8, 1024))
     owner = jnp.broadcast_to(owner_order[...].reshape(1, 640), (8, 640))
     owner = jnp.concatenate([owner, jnp.zeros((8, 384), jnp.int32)], axis=1)
@@ -223,10 +216,14 @@
     copies = fetch(sources, buffers, semaphores)
     for copy in copies[:7]:
         copy.wait()
-    pick_rows(send_buffer, owner_buffer, right_buffer, mine, theirs)
+    lane = lanes((1, 1024))
+    turn = lane & 7
+    wanted = (((lane >> 3) & 15) * 8 + (lane >> 7)) * 5 + turn
+    order = one_hot(rows_of((640, 1024)) == jnp.where(turn < 5, wanted, -1))
+    pick_rows(send_buffer, owner_buffer, right_buffer, order, mine, theirs)
     make_tables(
-        live_buffer, send_buffer, owner_buffer, first_buffer, second_buffer, third_buffer, wide,
-        masks, columns,
+        live_buffer, send_buffer, owner_buffer, first_buffer, second_buffer, third_buffer, order,
+        wide, masks, columns,
     )
     for copy in copies[7:]:
         copy.wait()
@@ -294,9 +291,26 @@
     return jnp.concatenate([gathered[index] for index in range(gathered.shape[0])], axis=1)
 
 
+def pick_rest(turned, own_columns, other_columns, outs):
+    core = core_index()
+    chip = lax.axis_index("x")
+    parts = []
+    for columns, which in ((own_columns, core), (other_columns, 1 - core)):
+        source, turn = source_and_turn(columns[1:2, :640])
+        hot = one_hot(rows_of((1024, 640)) == source * 8 + turn)
+        start = pl.multiple_of(chip * 32 + which * HALF, HALF)
+        parts.append(dot(turned[pl.ds(start, HALF), :], hot))
+    offset = LEAF
+    for out in outs:
+        width = out.shape[1] // 2
+        own, other = (part[:, offset : offset + width] for part in parts)
+        out[...] = in_order(own, other).astype(BF16)
+        offset += width
+
+
 def in_kernel(
     received, own_pattern, other_pattern, own_lower, other_lower, own_link, other_link,
-    own_out, other_out, rows_out, out, turned,
+    own_columns, other_columns, own_out, other_out, first_out, second_out, third_out, out, turned,
 ):
     flat = received[...].reshape(1024, 128)
     turned[...] = flat.astype(F32).T.astype(BF16)
@@ -322,8 +336,7 @@
         fronts.append(
             jnp.where(lanes((HALF, 384)) < LEAF, picked[:HALF], picked[HALF:]).astype(BF16)
         )
-    start = pl.multiple_of(lax.axis_index("x") * 32, 32)
-    rows_out[...] = turned[pl.ds(start, 32), :]
+    pick_rest(turned, own_columns, other_columns, (first_out, second_out, third_out))
     front = jnp.concatenate(fronts, axis=1)
     own = apply_factor(front, own_lower).astype(BF16)
     other = apply_factor(front, other_lower).astype(BF16)
@@ -331,22 +344,6 @@
     other_out[...] = other
     pieces = (own.astype(F32), other.astype(F32))
     down_product(1, pieces, (own_link, other_link), (own_pattern, other_pattern), out)
-
-
-def rest_kernel(turned, own_owner, other_owner, first_out, second_out, third_out):
-    core = core_index()
-    parts = []
-    for owner, which in ((own_owner, core), (other_owner, 1 - core)):
-        source, turn = source_and_turn(owner[1:2, :640])
-        hot = one_hot(rows_of((1024, 640)) == source * 8 + turn)
-        rows = turned[pl.ds(pl.multiple_of(which * HALF, HALF), HALF), :]
-        parts.append(dot(rows, hot))
-    offset = LEAF
-    for out in (first_out, second_out, third_out):
-        width = out.shape[1] // 2
-        own, other = (part[:, offset : offset + width] for part in parts)
-        out[...] = in_order(own, other).astype(BF16)
-        offset += width
 
 
 def reduce_kernel(level, received, right, masks, out):
@@ -435,10 +432,20 @@
     core = core_index()
     halves = []
     for ref in (received, far):
-        turned = ref[...].reshape(512, 128).astype(F32).T
-        first = jnp.concatenate([turned[:HALF], turned[2 * HALF : 3 * HALF]], axis=1)
-        second = jnp.concatenate([turned[HALF : 2 * HALF], turned[3 * HALF : 4 * HALF]], axis=1)
-        halves.append(jnp.where(core == 0, first, second))
+        tiles = ref[...].astype(F32).reshape(16, 4, 8, 128)
+        tiles = jnp.concatenate([tiles[:, chip] for chip in range(4)], axis=0)
+        turned = tiles.reshape(512, 128).T
+        values = []
+        for half in range(2):
+            pieces = []
+            for chip in range(4):
+                for part in range(2):
+                    start = (2 * part + half) * HALF
+                    pieces.append(
+                        turned[start : start + HALF, chip * 128 : (chip + 1) * 128]
+                    )
+            values.append(jnp.concatenate(pieces, axis=1))
+        halves.append(jnp.where(core == 0, values[0], values[1]))
     top = jnp.where(core == 0, halves[0], halves[1])
     bottom = jnp.where(core == 0, halves[1], halves[0])
     value = jnp.concatenate([top, bottom], axis=0).astype(BF16)
@@ -544,31 +551,30 @@
     patterns = (own_patterns, other_patterns)
     payload = begin(payload, FIRST)
     received = finish(exchange(payload.reshape(64, 16, 128), 4), FIRST)
-    own_y, other_y, own_rows, term = call(
+    own_y, other_y, *rights, term = call(
         in_kernel,
         "leaf_front",
         [
             ((HALF, LEAF), BF16),
             ((HALF, LEAF), BF16),
-            ((32, 1024), BF16),
+            ((HALF, 512), BF16),
+            ((HALF, 256), BF16),
+            ((HALF, 128), BF16),
             ((8, HALF, 512), BF16),
         ],
-        (received,) + patterns + pairs["lower0"] + pairs["down1"],
+        (received,)
+        + patterns
+        + pairs["lower0"]
+        + pairs["down1"]
+        + (own_columns, other_columns),
         scratch=[pltpu.VMEM((128, 1024), BF16)],
     )
     level_y = {0: (own_y, other_y)}
-    rights = call(
-        rest_kernel,
-        "separator_rows",
-        [((HALF, 512), BF16), ((HALF, 256), BF16), ((HALF, 128), BF16)],
-        (own_rows, own_columns, other_columns),
-    )
     for level in (1, 2, 3):
         members = MEMBERS[level]
         chip_width = SEP // members
         piece = ((HALF, WIDTHS[level]), BF16)
         if level == 1:
-            term, rights = lax.optimization_barrier((term, rights))
             term = begin(term, SECOND)
         shared = exchange(term, level)
         reduced = call(

time: 200 us -> 200 us (level)
    pallas_call x18 -> x17, Pallas kernels: 15.2 us -> 15.3 us  [call(): pl.pallas_call(body, name=name, out_shape=[jax.ShapeDtypeStruct(shape, dt...]
where the time goes in v6:
time: 200 us; the launch traced here: 199 us
  blocking collectives  151 us (76%)
  starting transfers between devices  29.3 us (15%)
  Pallas kernels  15.3 us (8%)
  waiting for transfers between devices  3.65 us (2%)
    all_to_all x14, blocking collectives, exchange(): lax.all_to_all(value, CHIPS[level], split_axis=0, concat_axis=0, tiled=True)  151 us
    ppermute x18, starting transfers between devices, swap(): return lax.ppermute(value, 'c', [(0, 1), (1, 0)])  26 us
    pallas_call x17, Pallas kernels, call(): pl.pallas_call(body, name=name, out_shape=[jax.ShapeDtypeStruct(shape, dt...  15.3 us
  transfers between devices with their start and end apart: 21, of which 5 were waited for; matrix products, arithmetic and copies ran while one was open for 0% of the time, Pallas kernels for 2%

profile of v6, /device:TPU:1, one launch (start us, length us, event | category | flops | bytes accessed | tf_op | source)
XLA Modules:
  0.0 199.2 jit_solution(12390277581752814929)
XLA Ops:
  0.0 2.1 %start.1 = (bf16[16,8,128]{2,1,0:T(8,128)(2,1)S(1)}, bf16[16,8,128]{2,1,0:T(8,128)(2,1)S(1)}, bf16[16,4096]{1,0:T(8,128)(2,1)S(1)}, f32[8,896]{1,0:T(8,128)S(1)}...) custom-call(s32[14]{0:T(128)} %live.1, s32[640]{0:T(1024)} %send_order.1, ...), custom_call_target="tpu_custom_call" | custom-call | tf_op jit(solution)/shard_map/start/pallas_call | solution.py:49
  2.1 1.5 collective-permute-start.2
  6.0 21.1 %all_to_all.70.received = bf16[64,16,128]{2,1,0:T(8,128)(2,1)S(1)} all-to-all(bf16[64,16,128]{2,1,0:T(8,128)(2,1)S(1)} %bitcast.12), channel_id=1, replica_groups=mesh['z1'=2,'z0'=2,'y1'=2,'y0'=2,'x'=4,'c'=2] {'z1','z0','y1','y0','x'}, dimensions={0} | all-to-all | bytes 524288 | tf_op jit(solution)/shard_map/all_to_all | solution.py:41
  27.2 2.7 %leaf_front.1 = (bf16[16,192]{1,0:T(8,128)(2,1)S(1)}, bf16[16,192]{1,0:T(8,128)(2,1)S(1)}, bf16[16,512]{1,0:T(8,128)(2,1)S(1)}, bf16[16,256]{1,0:T(8,128)(2,1)S(...) custom-call(bf16[64,16,128]{2,1,0:T(8,128)(2,1)S(1)} %all_to_all.70.received, ...), custom_call_target="tpu_custom_call" | custom-call | tf_op jit(solution)/shard_map/leaf_front/pallas_call | solution.py:49
  29.9 1.6 collective-permute-start.7
  31.6 7.8 %all_to_all.71.received = bf16[8,16,512]{2,1,0:T(8,128)(2,1)S(1)} all-to-all(bf16[8,16,512]{2,1,0:T(8,128)(2,1)S(1)} %get-tuple-element.90), channel_id=1, replica_groups=mesh['z1'=2,'z0'=2,'y1'=2,'y0'=2,'x'=4,'c'=2] {'y0','x'}, dimensions={0} | all-to-all | bytes 262144 | tf_op jit(solution)/shard_map/all_to_all | solution.py:41
  39.5 1.6 collective-permute-start.11
  41.7 7.8 %all_to_all.72.gathered = bf16[8,16,512]{2,1,0:T(8,128)(2,1)S(1)} all-to-all(bf16[8,16,512]{2,1,0:T(8,128)(2,1)S(1)} %reduce_1.1), channel_id=1, replica_groups=mesh['z1'=2,'z0'=2,'y1'=2,'y0'=2,'x'=4,'c'=2] {'y0','x'}, dimensions={0} | all-to-all | bytes 262144 | tf_op jit(solution)/shard_map/all_to_all | solution.py:41
  49.6 2.0 %up_1.1 = (bf16[16,256]{1,0:T(8,128)(2,1)S(1)}, bf16[16,256]{1,0:T(8,128)(2,1)S(1)}, bf16[16,16,256]{2,1,0:T(8,128)(2,1)S(1)}) custom-call(bf16[8,16,512]{2,1,0:T(8,128)(2,1)S(1)} %all_to_all.72.gathered, f32[8,896]{1,0:T(8,128)S(1)} %get-tuple-element.92.masks, bf16[16,4096]{1,0:T(8,128)(2,1)S(1)} %get-tuple-element.75.own_pattern, ...), custom_call_target="tpu_custom_call" | custom-call | tf_op jit(solution)/shard_map/up_1/pallas_call | solution.py:49
  51.6 10.4 %all_to_all.73.received = bf16[16,16,256]{2,1,0:T(8,128)(2,1)S(1)} all-to-all(bf16[16,16,256]{2,1,0:T(8,128)(2,1)S(1)} %get-tuple-element.99), channel_id=1, replica_groups=mesh['z1'=2,'z0'=2,'y1'=2,'y0'=2,'x'=4,'c'=2] {'y1','y0','x'}, dimensions={0} | all-to-all | bytes 262144 | tf_op jit(solution)/shard_map/all_to_all | solution.py:41
  62.1 3.1 %collective-permute-start.13 = (bf16[4096,256]{1,0:T(8,128)(2,1)S(1)}, bf16[4096,256]{1,0:T(8,128)(2,1)S(1)}, u32[]{:S(2)}, u32[]{:S(2)}) collective-permute-start(bf16[4096,256]{1,0:T(8,128)(2,1)S(1)} %copy-done.3), channel_id=1, source_target_pairs={{0,1},{1,0},{2,3},{3,2},{4,5},{5,4},{6,7},{7,6},{8,9},{9,8},{10,11... | collective-permute-start | bytes 6291464 | tf_op jit(solution)/shard_map/ppermute | solution.py:37
  65.8 9.6 %all_to_all.74.gathered = bf16[16,16,256]{2,1,0:T(8,128)(2,1)S(1)} all-to-all(bf16[16,16,256]{2,1,0:T(8,128)(2,1)S(1)} %reduce_2.1), channel_id=1, replica_groups=mesh['z1'=2,'z0'=2,'y1'=2,'y0'=2,'x'=4,'c'=2] {'y1','y0','x'}, dimensions={0} | all-to-all | bytes 262144 | tf_op jit(solution)/shard_map/all_to_all | solution.py:41
  76.5 10.9 %all_to_all.75.received = bf16[32,16,128]{2,1,0:T(8,128)(2,1)S(1)} all-to-all(bf16[32,16,128]{2,1,0:T(8,128)(2,1)S(1)} %get-tuple-element.109), channel_id=1, replica_groups=mesh['z1'=2,'z0'=2,'y1'=2,'y0'=2,'x'=4,'c'=2] {'z0','y1','y0','x'}, dimensions={0} | all-to-all | bytes 262144 | tf_op jit(solution)/shard_map/all_to_all | solution.py:41
  87.6 10.7 %all_to_all.76.gathered = bf16[32,16,128]{2,1,0:T(8,128)(2,1)S(1)} all-to-all(bf16[32,16,128]{2,1,0:T(8,128)(2,1)S(1)} %reduce_3.1), channel_id=1, replica_groups=mesh['z1'=2,'z0'=2,'y1'=2,'y0'=2,'x'=4,'c'=2] {'z0','y1','y0','x'}, dimensions={0} | all-to-all | bytes 262144 | tf_op jit(solution)/shard_map/all_to_all | solution.py:41
  98.8 10.7 %all_to_all.77.gathered = bf16[32,16,128]{2,1,0:T(8,128)(2,1)S(1)} all-to-all(bf16[32,16,128]{2,1,0:T(8,128)(2,1)S(1)} %top_lower.1), channel_id=1, replica_groups=mesh['z1'=2,'z0'=2,'y1'=2,'y0'=2,'x'=4,'c'=2] {'z0','y1','y0','x'}, dimensions={0} | all-to-all | bytes 262144 | tf_op jit(solution)/shard_map/all_to_all | solution.py:41
  110.0 10.7 %all_to_all.78.gathered = bf16[32,16,128]{2,1,0:T(8,128)(2,1)S(1)} all-to-all(bf16[32,16,128]{2,1,0:T(8,128)(2,1)S(1)} %get-tuple-element.118), channel_id=1, replica_groups=mesh['z1'=2,'z0'=2,'y1'=2,'y0'=2,'x'=4,'c'=2] {'z0','y1','y0','x'}, dimensions={0} | all-to-all | bytes 262144 | tf_op jit(solution)/shard_map/all_to_all | solution.py:41
  121.2 10.0 %all_to_all.79.gathered = bf16[16,16,256]{2,1,0:T(8,128)(2,1)S(1)} all-to-all(bf16[16,16,256]{2,1,0:T(8,128)(2,1)S(1)} %back_2.1), channel_id=1, replica_groups=mesh['z1'=2,'z0'=2,'y1'=2,'y0'=2,'x'=4,'c'=2] {'y1','y0','x'}, dimensions={0} | all-to-all | bytes 262144 | tf_op jit(solution)/shard_map/all_to_all | solution.py:41
  131.5 9.6 %all_to_all.80.gathered = bf16[16,16,256]{2,1,0:T(8,128)(2,1)S(1)} all-to-all(bf16[16,16,256]{2,1,0:T(8,128)(2,1)S(1)} %get-tuple-element.123), channel_id=1, replica_groups=mesh['z1'=2,'z0'=2,'y1'=2,'y0'=2,'x'=4,'c'=2] {'y1','y0','x'}, dimensions={0} | all-to-all | bytes 262144 | tf_op jit(solution)/shard_map/all_to_all | solution.py:41
  142.0 8.2 %all_to_all.81.gathered = bf16[8,16,512]{2,1,0:T(8,128)(2,1)S(1)} all-to-all(bf16[8,16,512]{2,1,0:T(8,128)(2,1)S(1)} %back_1.1), channel_id=1, replica_groups=mesh['z1'=2,'z0'=2,'y1'=2,'y0'=2,'x'=4,'c'=2] {'y0','x'}, dimensions={0} | all-to-all | bytes 262144 | tf_op jit(solution)/shard_map/all_to_all | solution.py:41
  150.9 7.8 %all_to_all.82.gathered = bf16[8,16,512]{2,1,0:T(8,128)(2,1)S(1)} all-to-all(bf16[8,16,512]{2,1,0:T(8,128)(2,1)S(1)} %get-tuple-element.128), channel_id=1, replica_groups=mesh['z1'=2,'z0'=2,'y1'=2,'y0'=2,'x'=4,'c'=2] {'y0','x'}, dimensions={0} | all-to-all | bytes 262144 | tf_op jit(solution)/shard_map/all_to_all | solution.py:41
  160.9 1.4 collective-permute-start.18
  165.0 1.6 leaf_solution.1
  166.6 15.2 %all_to_all.83.received = bf16[64,8,128]{2,1,0:T(8,128)(2,1)S(1)} all-to-all(bf16[64,8,128]{2,1,0:T(8,128)(2,1)S(1)} %leaf_solution.1), channel_id=1, replica_groups=mesh['z1'=2,'z0'=2,'y1'=2,'y0'=2,'x'=4,'c'=2] {'z1','z0','y1','y0','x'}, dimensions={0} | all-to-all | bytes 262144 | tf_op jit(solution)/shard_map/all_to_all | solution.py:41
  181.8 15.3 %collective-permute-start.20 = (bf16[64,8,128]{2,1,0:T(8,128)(2,1)S(1)}, bf16[64,8,128]{2,1,0:T(8,128)(2,1)S(1)}, u32[]{:S(2)}, u32[]{:S(2)}) collective-permute-start(bf16[64,8,128]{2,1,0:T(8,128)(2,1)S(1)} %all_to_all.83.received), channel_id=1, source_target_pairs={{0,1},{1,0},{2,3},{3,2},{4,5},{5,4},{6,7},{7,6},{8,9},{9,8},{10,11... | collective-permute-start | bytes 393224 | tf_op jit(solution)/shard_map/ppermute | solution.py:37
  (73 shorter events, 15.3 us)
Async XLA Ops:
  2.1 2.9 %collective-permute-start.2 = (bf16[16,4096]{1,0:T(8,128)(2,1)S(1)}, bf16[16,4096]{1,0:T(8,128)(2,1)S(1)}, u32[]{:S(2)}, u32[]{:S(2)}) collective-permute-start(bf16[16,4096]{1,0:T(8,128)(2,1)S(1)} %get-tuple-element.75.own_pattern), channel_id=1, source_target_pairs={{0,1},{1,0},{2,3},{3,2},{4,5},{5,4},{6,7},{7,6},{8,9},{9,8},{10,11... | collective-permute-start | bytes 393224 | tf_op jit(solution)/shard_map/ppermute | solution.py:37
  3.6 1.2 collective-permute-start
  3.7 1.3 collective-permute-start.1
  4.8 26.7 %copy-start.8 = (bf16[4096,128]{1,0:T(8,128)(2,1)S(1)}, bf16[4096,128]{1,0:T(8,128)(2,1)}, u32[]{:S(2)}) copy-start(bf16[4096,128]{1,0:T(8,128)(2,1)} %own_link.5) | copy-start | bytes 3145732
  5.0 22.2 %collective-permute-start.5 = (bf16[4096,256]{1,0:T(8,128)(2,1)S(1)}, bf16[4096,256]{1,0:T(8,128)(2,1)S(1)}, u32[]{:S(2)}, u32[]{:S(2)}) collective-permute-start(bf16[4096,256]{1,0:T(8,128)(2,1)S(1)} %copy-done), channel_id=1, source_target_pairs={{0,1},{1,0},{2,3},{3,2},{4,5},{5,4},{6,7},{7,6},{8,9},{9,8},{10,11... | collective-permute-start | bytes 6291464 | tf_op jit(solution)/shard_map/ppermute | solution.py:37
  5.3 21.9 %collective-permute-start.6 = (bf16[4096,256]{1,0:T(8,128)(2,1)}, bf16[4096,256]{1,0:T(8,128)(2,1)S(1)}, u32[]{:S(2)}, u32[]{:S(2)}) collective-permute-start(bf16[4096,256]{1,0:T(8,128)(2,1)} %own_link.4), channel_id=1, source_target_pairs={{0,1},{1,0},{2,3},{3,2},{4,5},{5,4},{6,7},{7,6},{8,9},{9,8},{10,11... | collective-permute-start | bytes 6291464 | tf_op jit(solution)/shard_map/ppermute | solution.py:37
  5.5 21.7 %collective-permute-start.4 = (bf16[192,4096]{1,0:T(8,128)(2,1)S(1)}, bf16[192,4096]{1,0:T(8,128)(2,1)S(1)}, u32[]{:S(2)}, u32[]{:S(2)}) collective-permute-start(bf16[192,4096]{1,0:T(8,128)(2,1)S(1)} %get-tuple-element.81.own_link), channel_id=1, source_target_pairs={{0,1},{1,0},{2,3},{3,2},{4,5},{5,4},{6,7},{7,6},{8,9},{9,8},{10,11... | collective-permute-start | bytes 4718600 | tf_op jit(solution)/shard_map/ppermute | solution.py:37
  5.9 21.3 %collective-permute-start.3 = (bf16[192,1536]{1,0:T(8,128)(2,1)S(1)}, bf16[192,1536]{1,0:T(8,128)(2,1)S(1)}, u32[]{:S(2)}, u32[]{:S(2)}) collective-permute-start(bf16[192,1536]{1,0:T(8,128)(2,1)S(1)} %get-tuple-element.80.own_lower), channel_id=1, source_target_pairs={{0,1},{1,0},{2,3},{3,2},{4,5},{5,4},{6,7},{7,6},{8,9},{9,8},{10,11... | collective-permute-start | bytes 1769480 | tf_op jit(solution)/shard_map/ppermute | solution.py:37
  6.0 23.9 %copy-start.7 = (bf16[4096,128]{1,0:T(8,128)(2,1)S(1)}, bf16[4096,128]{1,0:T(8,128)(2,1)}, u32[]{:S(2)}) copy-start(bf16[4096,128]{1,0:T(8,128)(2,1)} %own_lower.3) | copy-start | bytes 3145732
  29.9 9.6 %collective-permute-start.7 = (bf16[4096,128]{1,0:T(8,128)(2,1)S(1)}, bf16[4096,128]{1,0:T(8,128)(2,1)S(1)}, u32[]{:S(2)}, u32[]{:S(2)}) collective-permute-start(bf16[4096,128]{1,0:T(8,128)(2,1)S(1)} %copy-done.7), channel_id=1, source_target_pairs={{0,1},{1,0},{2,3},{3,2},{4,5},{5,4},{6,7},{7,6},{8,9},{9,8},{10,11... | collective-permute-start | bytes 3145736 | tf_op jit(solution)/shard_map/ppermute | solution.py:37
  31.5 8.0 %collective-permute-start.8 = (bf16[4096,128]{1,0:T(8,128)(2,1)S(1)}, bf16[4096,128]{1,0:T(8,128)(2,1)S(1)}, u32[]{:S(2)}, u32[]{:S(2)}) collective-permute-start(bf16[4096,128]{1,0:T(8,128)(2,1)S(1)} %copy-done.8), channel_id=1, source_target_pairs={{0,1},{1,0},{2,3},{3,2},{4,5},{5,4},{6,7},{7,6},{8,9},{9,8},{10,11... | collective-permute-start | bytes 3145736 | tf_op jit(solution)/shard_map/ppermute | solution.py:37
  39.5 22.5 %collective-permute-start.11 = (bf16[4096,128]{1,0:T(8,128)(2,1)S(1)}, bf16[4096,128]{1,0:T(8,128)(2,1)S(1)}, u32[]{:S(2)}, u32[]{:S(2)}) collective-permute-start(bf16[4096,128]{1,0:T(8,128)(2,1)S(1)} %copy-done.5), channel_id=1, source_target_pairs={{0,1},{1,0},{2,3},{3,2},{4,5},{5,4},{6,7},{7,6},{8,9},{9,8},{10,11... | collective-permute-start | bytes 3145736 | tf_op jit(solution)/shard_map/ppermute | solution.py:37
  41.1 20.9 %collective-permute-start.12 = (bf16[4096,128]{1,0:T(8,128)(2,1)S(1)}, bf16[4096,128]{1,0:T(8,128)(2,1)S(1)}, u32[]{:S(2)}, u32[]{:S(2)}) collective-permute-start(bf16[4096,128]{1,0:T(8,128)(2,1)S(1)} %copy-done.6), channel_id=1, source_target_pairs={{0,1},{1,0},{2,3},{3,2},{4,5},{5,4},{6,7},{7,6},{8,9},{9,8},{10,11... | collective-permute-start | bytes 3145736 | tf_op jit(solution)/shard_map/ppermute | solution.py:37
  41.2 20.8 %collective-permute-start.9 = (bf16[64,4096]{1,0:T(8,128)(2,1)}, bf16[64,4096]{1,0:T(8,128)(2,1)S(1)}, u32[]{:S(2)}, u32[]{:S(2)}) collective-permute-start(bf16[64,4096]{1,0:T(8,128)(2,1)} %bitcast.17), channel_id=1, source_target_pairs={{0,1},{1,0},{2,3},{3,2},{4,5},{5,4},{6,7},{7,6},{8,9},{9,8},{10,11... | collective-permute-start | bytes 1572872 | tf_op jit(solution)/shard_map/ppermute | solution.py:37
  41.6 20.4 %collective-permute-start.10 = (bf16[64,4096]{1,0:T(8,128)(2,1)}, bf16[64,4096]{1,0:T(8,128)(2,1)S(1)}, u32[]{:S(2)}, u32[]{:S(2)}) collective-permute-start(bf16[64,4096]{1,0:T(8,128)(2,1)} %bitcast.15), channel_id=1, source_target_pairs={{0,1},{1,0},{2,3},{3,2},{4,5},{5,4},{6,7},{7,6},{8,9},{9,8},{10,11... | collective-permute-start | bytes 1572872 | tf_op jit(solution)/shard_map/ppermute | solution.py:37
  62.1 25.5 %collective-permute-start.13 = (bf16[4096,256]{1,0:T(8,128)(2,1)S(1)}, bf16[4096,256]{1,0:T(8,128)(2,1)S(1)}, u32[]{:S(2)}, u32[]{:S(2)}) collective-permute-start(bf16[4096,256]{1,0:T(8,128)(2,1)S(1)} %copy-done.3), channel_id=1, source_target_pairs={{0,1},{1,0},{2,3},{3,2},{4,5},{5,4},{6,7},{7,6},{8,9},{9,8},{10,11... | collective-permute-start | bytes 6291464 | tf_op jit(solution)/shard_map/ppermute | solution.py:37
  65.2 22.4 %collective-permute-start.14 = (bf16[4096,256]{1,0:T(8,128)(2,1)S(1)}, bf16[4096,256]{1,0:T(8,128)(2,1)S(1)}, u32[]{:S(2)}, u32[]{:S(2)}) collective-permute-start(bf16[4096,256]{1,0:T(8,128)(2,1)S(1)} %copy-done.2), channel_id=1, source_target_pairs={{0,1},{1,0},{2,3},{3,2},{4,5},{5,4},{6,7},{7,6},{8,9},{9,8},{10,11... | collective-permute-start | bytes 6291464 | tf_op jit(solution)/shard_map/ppermute | solution.py:37
  65.3 22.3 %collective-permute-start.15 = (bf16[192,4096]{1,0:T(8,128)(2,1)S(1)}, bf16[192,4096]{1,0:T(8,128)(2,1)S(1)}, u32[]{:S(2)}, u32[]{:S(2)}) collective-permute-start(bf16[192,4096]{1,0:T(8,128)(2,1)S(1)} %bitcast.10), channel_id=1, source_target_pairs={{0,1},{1,0},{2,3},{3,2},{4,5},{5,4},{6,7},{7,6},{8,9},{9,8},{10,11... | collective-permute-start | bytes 4718600 | tf_op jit(solution)/shard_map/ppermute | solution.py:37
  65.7 21.9 %collective-permute-start.16 = (bf16[192,1536]{1,0:T(8,128)(2,1)S(1)}, bf16[192,1536]{1,0:T(8,128)(2,1)S(1)}, u32[]{:S(2)}, u32[]{:S(2)}) collective-permute-start(bf16[192,1536]{1,0:T(8,128)(2,1)S(1)} %bitcast.13), channel_id=1, source_target_pairs={{0,1},{1,0},{2,3},{3,2},{4,5},{5,4},{6,7},{7,6},{8,9},{9,8},{10,11... | collective-permute-start | bytes 1769480 | tf_op jit(solution)/shard_map/ppermute | solution.py:37
  76.5 33.0 %copy-start.10 = (bf16[4096,64]{0,1:T(8,128)(2,1)S(1)}, bf16[4096,64]{0,1:T(8,128)(2,1)}, u32[]{:S(2)}) copy-start(bf16[4096,64]{0,1:T(8,128)(2,1)} %param.32) | copy-start | bytes 1572868
  159.9 3.8 %collective-permute-start.19 = (bf16[16,384]{1,0:T(8,128)(2,1)S(1)}, bf16[16,384]{1,0:T(8,128)(2,1)S(1)}, u32[]{:S(2)}, u32[]{:S(2)}) collective-permute-start(bf16[16,384]{1,0:T(8,128)(2,1)S(1)} %back_0.1.own_part), channel_id=1, source_target_pairs={{0,6},{2,4},{4,2},{6,0},{1,7},{3,5},{5,3},{7,1},{8,14},{10,12},{12... | collective-permute-start | bytes 36872 | tf_op jit(solution)/shard_map/ppermute | solution.py:638
  160.9 4.0 %collective-permute-start.18 = (bf16[16,384]{1,0:T(8,128)(2,1)S(1)}, bf16[16,384]{1,0:T(8,128)(2,1)S(1)}, u32[]{:S(2)}, u32[]{:S(2)}) collective-permute-start(bf16[16,384]{1,0:T(8,128)(2,1)S(1)} %back_0.1.own_part), channel_id=1, source_target_pairs={{0,4},{2,6},{4,0},{6,2},{1,5},{3,7},{5,1},{7,3},{8,12},{10,14},{12... | collective-permute-start | bytes 36872 | tf_op jit(solution)/shard_map/ppermute | solution.py:638
  162.3 2.7 %collective-permute-start.17 = (bf16[16,384]{1,0:T(8,128)(2,1)S(1)}, bf16[16,384]{1,0:T(8,128)(2,1)S(1)}, u32[]{:S(2)}, u32[]{:S(2)}) collective-permute-start(bf16[16,384]{1,0:T(8,128)(2,1)S(1)} %back_0.1.own_part), channel_id=1, source_target_pairs={{0,2},{2,0},{4,6},{6,4},{1,3},{3,1},{5,7},{7,5},{8,10},{10,8},{12,... | collective-permute-start | bytes 36872 | tf_op jit(solution)/shard_map/ppermute | solution.py:638
  181.8 16.3 %collective-permute-start.20 = (bf16[64,8,128]{2,1,0:T(8,128)(2,1)S(1)}, bf16[64,8,128]{2,1,0:T(8,128)(2,1)S(1)}, u32[]{:S(2)}, u32[]{:S(2)}) collective-permute-start(bf16[64,8,128]{2,1,0:T(8,128)(2,1)S(1)} %all_to_all.83.received), channel_id=1, source_target_pairs={{0,1},{1,0},{2,3},{3,2},{4,5},{5,4},{6,7},{7,6},{8,9},{9,8},{10,11... | collective-permute-start | bytes 393224 | tf_op jit(solution)/shard_map/ppermute | solution.py:37
  (9 other events, 136.5 us)

commit v7 on v6

--- a/solution.py
+++ b/solution.py
@@ -17,10 +17,11 @@
     4: ("z1", "z0", "y1", "y0", "x"),
 }
 MEMBERS = {0: 4, 1: 8, 2: 16, 3: 32, 4: 64}
-FIRST = ("lower0", "down1", "lower1", "down2")
-SECOND = ("lower2", "down3")
-THIRD = ("lower3", "upper3", "back3", "upper2")
-FOURTH = ("back2", "upper1", "back1", "upper0")
+FIRST = ("leaf", "lower1", "down2")
+SECOND = ("second",)
+THIRD = ("third", "back2")
+FOURTH = ("middle", "upper1", "last")
+LEAF_ROWS = 1536
 HALF = 16
 SEP = 4096
 BLOCK = 64
@@ -65,6 +66,37 @@
     for copy in copies:
         copy.start()
     return copies
+
+
+def windowed(body, place, *windows):
+    def run(*refs):
+        pair = refs[place : place + 2]
+        pieces = [ref.at[window] for window in windows for ref in pair]
+        body(*refs[:place], *pieces, *refs[place + 2 :])
+
+    return run
+
+
+def fetching(body, sources, leading, targets):
+    def run(*refs):
+        rest = refs[sources:]
+        extra = len({place for place, _ in targets})
+        joint = rest[leading : leading + extra]
+        goals = [joint[place].at[window] for place, window in targets]
+        copies = fetch(refs[:sources], goals, refs[-1])
+        body(*rest[:leading], *rest[leading + extra : -1])
+        for copy in copies:
+            copy.wait()
+
+    return run
+
+
+LEFT = (slice(None), slice(0, 128))
+RIGHT = (slice(None), slice(128, 256))
+UPPER = (slice(0, 64), slice(None))
+LOWER = (slice(64, 128), slice(None))
+LEAF_LEFT = (slice(None), slice(0, LEAF_ROWS))
+LEAF_RIGHT = (slice(None), slice(LEAF_ROWS, LEAF_ROWS + SEP))
 
 
 def dot(left, right):
@@ -205,12 +237,12 @@
 
 def start_kernel(
     live, send_order, owner_order, right, first, second, third, lower, link, mine, theirs, wide,
-    masks, columns, lower_out, link_out, live_buffer, send_buffer, owner_buffer, right_buffer,
+    masks, columns, leaf_out, live_buffer, send_buffer, owner_buffer, right_buffer,
     first_buffer, second_buffer, third_buffer, semaphores,
 ):
     buffers = (
         live_buffer, send_buffer, owner_buffer, right_buffer, first_buffer, second_buffer,
-        third_buffer, lower_out, link_out,
+        third_buffer, leaf_out.at[LEAF_LEFT], leaf_out.at[LEAF_RIGHT],
     )
     sources = (live, send_order, owner_order, right, first, second, third, lower, link)
     copies = fetch(sources, buffers, semaphores)
@@ -479,16 +511,8 @@
     factors = {
         "lower1": lower_first,
         "down2": downlink_second,
-        "lower2": lower_second,
-        "down3": downlink_third,
-        "lower3": lower_third.T,
-        "upper3": upper_third.T,
-        "back3": uplink_third,
-        "upper2": upper_second,
         "back2": uplink_second,
         "upper1": upper_first,
-        "back1": uplink_first.T,
-        "upper0": upper_leaf.T,
     }
     pairs = {}
 
@@ -504,7 +528,7 @@
             pairs[name] = (pairs[name][0], other)
         return tied[0]
 
-    mine, theirs, own_patterns, masks, own_columns, own_lower, own_link = call(
+    mine, theirs, own_patterns, masks, own_columns, own_leaf = call(
         start_kernel,
         "start",
         [
@@ -513,8 +537,7 @@
             ((16, SEP), BF16),
             ((8, 896), F32),
             ((8, 1024), jnp.int32),
-            ((LEAF, 8 * LEAF), BF16),
-            ((LEAF, SEP), BF16),
+            ((LEAF, LEAF_ROWS + SEP), BF16),
         ],
         (),
         distant=(
@@ -538,8 +561,7 @@
             pltpu.VMEM((2, BLOCK), jnp.int32),
         ],
     )
-    factors["lower0"] = own_lower
-    factors["down1"] = own_link
+    factors["leaf"] = own_leaf
     other_columns = swap(own_columns)
     other_patterns = swap(own_patterns)
     payload = call(
@@ -551,8 +573,13 @@
     patterns = (own_patterns, other_patterns)
     payload = begin(payload, FIRST)
     received = finish(exchange(payload.reshape(64, 16, 128), 4), FIRST)
-    own_y, other_y, *rights, term = call(
-        in_kernel,
+    own_y, other_y, *rights, term, factors["second"], factors["third"] = call(
+        fetching(
+            windowed(in_kernel, 3, LEAF_LEFT, LEAF_RIGHT),
+            4,
+            13,
+            ((0, LEFT), (0, RIGHT), (1, UPPER), (1, LOWER)),
+        ),
         "leaf_front",
         [
             ((HALF, LEAF), BF16),
@@ -561,12 +588,11 @@
             ((HALF, 256), BF16),
             ((HALF, 128), BF16),
             ((8, HALF, 512), BF16),
+            ((SEP, 256), BF16),
+            ((128, SEP), BF16),
         ],
-        (received,)
-        + patterns
-        + pairs["lower0"]
-        + pairs["down1"]
-        + (own_columns, other_columns),
+        (received,) + patterns + pairs["leaf"] + (own_columns, other_columns),
+        distant=(lower_second, downlink_third, lower_third.T, upper_third.T),
         scratch=[pltpu.VMEM((128, 1024), BF16)],
     )
     level_y = {0: (own_y, other_y)}
@@ -592,52 +618,61 @@
         gathered = exchange(reduced, level)
         if level < 3:
             above = MEMBERS[level + 1]
-            own_y, other_y, term = call(
-                functools.partial(up_kernel, level),
-                "up_%d" % level,
-                [piece, piece, ((above, HALF, SEP // above), BF16)],
-                (gathered, masks)
-                + patterns
-                + pairs["lower%d" % level]
-                + pairs["down%d" % (level + 1)],
-            )
+            outs = [piece, piece, ((above, HALF, SEP // above), BF16)]
+            operands = (gathered, masks) + patterns
+            body = functools.partial(up_kernel, level)
+            if level == 1:
+                own_y, other_y, term, factors["middle"], factors["last"] = call(
+                    fetching(body, 4, 11, ((0, LEFT), (0, RIGHT), (1, LEAF_RIGHT), (1, LEAF_LEFT))),
+                    "up_1",
+                    outs + [((SEP, 256), BF16), ((LEAF, LEAF_ROWS + SEP), BF16)],
+                    operands + pairs["lower1"] + pairs["down2"],
+                    distant=(uplink_third, upper_second, uplink_first.T, upper_leaf.T),
+                )
+            else:
+                own_y, other_y, term = call(
+                    windowed(body, 4, LEFT, RIGHT), "up_2", outs, operands + pairs["second"]
+                )
         else:
             copies = call(
-                functools.partial(top_kernel, level),
+                windowed(functools.partial(top_kernel, level), 2, UPPER),
                 "top_lower",
                 [((members, HALF, chip_width), BF16)],
-                (gathered, masks) + pairs["lower3"],
+                (gathered, masks) + pairs["third"],
             )[0]
             break
         level_y[level] = (own_y, other_y)
     level_x = {}
+    whole = (slice(None), slice(None))
+    uppers = {3: ("third", LOWER), 2: ("middle", RIGHT), 1: ("upper1", whole)}
+    backs = {3: ("middle", LEFT), 2: ("back2", whole), 1: ("last", LEAF_RIGHT)}
     for level in (3, 2, 1):
         members = MEMBERS[level]
         chip_width = SEP // members
         piece = ((HALF, WIDTHS[level]), BF16)
         gathered = exchange(copies, level)
         own_x, other_x, copies = call(
-            functools.partial(solve_kernel, level),
+            windowed(functools.partial(solve_kernel, level), 2, uppers[level][1]),
             "solve_%d" % level,
             [piece, piece, ((members, HALF, chip_width), BF16)],
-            (gathered, masks) + pairs["upper%d" % level],
+            (gathered, masks) + pairs[uppers[level][0]],
         )
         level_x[level] = (own_x, other_x)
         gathered = exchange(copies, level)
         below = level - 1
         shape = (HALF, 2 * WIDTHS[below])
         copies = call(
-            functools.partial(back_kernel, below),
+            windowed(functools.partial(back_kernel, below), 6, backs[level][1]),
             "back_%d" % below,
             [((MEMBERS[below],) + shape if below else shape, BF16)],
-            (gathered, masks) + patterns + level_y[below] + pairs["back%d" % level],
+            (gathered, masks) + patterns + level_y[below] + pairs[backs[level][0]],
         )[0]
     parts = [copies]
     for step in (1, 2, 3):
         ring = [(source, source ^ step) for source in range(4)]
         parts.append(lax.ppermute(copies, "x", ring))
     outbound = call(
-        out_kernel,
+        windowed(out_kernel, 12, LEAF_LEFT),
         "leaf_solution",
         [((64, 8, 128), BF16)],
         tuple(parts)
@@ -645,7 +680,7 @@
         + level_x[1]
         + level_x[2]
         + level_x[3]
-        + pairs["upper0"],
+        + pairs["last"],
         scratch=[pltpu.VMEM((HALF, 8 * LEAF), BF16)],
     )[0]
     returned = exchange(outbound, 4)

time: 200 us -> 200 us (level)
  Pallas kernels: 15.3 us -> 17.6 us
    pallas_call x17, Pallas kernels: 15.3 us -> 17.6 us  [call(): pl.pallas_call(body, name=name, out_shape=[jax.ShapeDtypeStruct(shape, dt...]
    ppermute x18 -> x13, starting transfers between devices: 26 us -> 24.2 us  [swap(): return lax.ppermute(value, 'c', [(0, 1), (1, 0)])]
  transfers between devices with their start and end apart: 21 -> 16, of which waited for: 5 -> 5; matrix products, arithmetic and copies ran while one was open for 0% -> 0% of each run, Pallas kernels for 2% -> 2%
where the time goes in v7:
time: 200 us; the launch traced here: 199 us
  blocking collectives  150 us (75%)
  starting transfers between devices  27.5 us (14%)
  Pallas kernels  17.6 us (9%)
  waiting for transfers between devices  3.64 us (2%)
    all_to_all x14, blocking collectives, exchange(): lax.all_to_all(value, CHIPS[level], split_axis=0, concat_axis=0, tiled=True)  150 us
    ppermute x13, starting transfers between devices, swap(): return lax.ppermute(value, 'c', [(0, 1), (1, 0)])  24.2 us
    pallas_call x17, Pallas kernels, call(): pl.pallas_call(body, name=name, out_shape=[jax.ShapeDtypeStruct(shape, dt...  17.6 us
  transfers between devices with their start and end apart: 16, of which 5 were waited for; matrix products, arithmetic and copies ran while one was open for 0% of the time, Pallas kernels for 2%

profile of v7, /device:TPU:1, one launch (start us, length us, event | category | flops | bytes accessed | tf_op | source)
XLA Modules:
  0.0 199.5 jit_solution(16143131045045447556)
XLA Ops:
  0.0 2.1 %start.1 = (bf16[16,8,128]{2,1,0:T(8,128)(2,1)S(1)}, bf16[16,8,128]{2,1,0:T(8,128)(2,1)S(1)}, bf16[16,4096]{1,0:T(8,128)(2,1)S(1)}, f32[8,896]{1,0:T(8,128)S(1)}...) custom-call(s32[14]{0:T(128)} %live.1, s32[640]{0:T(1024)} %send_order.1, s32[640]{0:T(1024)} %owner_order.1, ...), custom_call_target="tpu_custom_call" | custom-call | tf_op jit(solution)/shard_map/start/pallas_call | solution.py:50
  2.1 1.5 collective-permute-start.2
  5.9 21.2 %all_to_all.70.refs_4_ = bf16[64,16,128]{2,1,0:T(8,128)(2,1)S(1)} all-to-all(bf16[64,16,128]{2,1,0:T(8,128)(2,1)S(1)} %bitcast.10), channel_id=1, replica_groups=mesh['z1'=2,'z0'=2,'y1'=2,'y0'=2,'x'=4,'c'=2] {'z1','z0','y1','y0','x'}, dimensions={0} | all-to-all | bytes 524288 | tf_op jit(solution)/shard_map/all_to_all | solution.py:42
  27.1 3.8 %leaf_front.1 = (bf16[16,192]{1,0:T(8,128)(2,1)S(1)}, bf16[16,192]{1,0:T(8,128)(2,1)S(1)}, bf16[16,512]{1,0:T(8,128)(2,1)S(1)}, bf16[16,256]{1,0:T(8,128)(2,1)S(...) custom-call(bf16[4096,128]{1,0:T(8,128)(2,1)} %refs_0_.2, ...), custom_call_target="tpu_custom_call" | custom-call | tf_op jit(solution)/shard_map/leaf_front/pallas_call | solution.py:50
  30.9 1.5 collective-permute-start.6
  32.3 7.8 %all_to_all.71.received = bf16[8,16,512]{2,1,0:T(8,128)(2,1)S(1)} all-to-all(bf16[8,16,512]{2,1,0:T(8,128)(2,1)S(1)} %get-tuple-element.81), channel_id=1, replica_groups=mesh['z1'=2,'z0'=2,'y1'=2,'y0'=2,'x'=4,'c'=2] {'y0','x'}, dimensions={0} | all-to-all | bytes 262144 | tf_op jit(solution)/shard_map/all_to_all | solution.py:42
  40.2 1.4 collective-permute-start.8
  41.8 7.8 %all_to_all.72.refs_4_ = bf16[8,16,512]{2,1,0:T(8,128)(2,1)S(1)} all-to-all(bf16[8,16,512]{2,1,0:T(8,128)(2,1)S(1)} %reduce_1.1), channel_id=1, replica_groups=mesh['z1'=2,'z0'=2,'y1'=2,'y0'=2,'x'=4,'c'=2] {'y0','x'}, dimensions={0} | all-to-all | bytes 262144 | tf_op jit(solution)/shard_map/all_to_all | solution.py:42
  49.6 3.4 %up_1.1 = (bf16[16,256]{1,0:T(8,128)(2,1)S(1)}, bf16[16,256]{1,0:T(8,128)(2,1)S(1)}, bf16[16,16,256]{2,1,0:T(8,128)(2,1)S(1)}, bf16[4096,256]{1,0:T(8,128)(2,1)S(1)}, bf16[192,5632]{1,0:T(8,128)(2,1)S(1)}) custom-call(bf16[4096,128]{1,0:T(8,128)(2,1)} %refs_0_.3, bf16[4096,128]{1,0:T(8,128)(2,1)} %refs_1_.3, bf16[192,4096]{1,0:T(8,128)(2,1)} %bitcast.12, ...), custom_call_target="tpu_custom_call" | custom-call | tf_op jit(solution)/shard_map/up_1/pallas_call | solution.py:50
  52.9 10.2 %all_to_all.73.received = bf16[16,16,256]{2,1,0:T(8,128)(2,1)S(1)} all-to-all(bf16[16,16,256]{2,1,0:T(8,128)(2,1)S(1)} %get-tuple-element.90), channel_id=1, replica_groups=mesh['z1'=2,'z0'=2,'y1'=2,'y0'=2,'x'=4,'c'=2] {'y1','y0','x'}, dimensions={0} | all-to-all | bytes 262144 | tf_op jit(solution)/shard_map/all_to_all | solution.py:42
  63.2 3.1 %collective-permute-start.11 = (bf16[192,5632]{1,0:T(8,128)(2,1)S(1)}, bf16[192,5632]{1,0:T(8,128)(2,1)S(1)}, u32[]{:S(2)}, u32[]{:S(2)}) collective-permute-start(bf16[192,5632]{1,0:T(8,128)(2,1)S(1)} %get-tuple-element.103.refs_6_.refs_12_), channel_id=1, source_target_pairs={{0,1},{1,0},{2,3},{3,2},{4,5},{5,4},{6,7},{7,6},{8,9},{9,8},{10,11... | collective-permute-start | bytes 6488072 | tf_op jit(solution)/shard_map/ppermute | solution.py:38
  66.8 9.6 %all_to_all.74.refs_0_ = bf16[16,16,256]{2,1,0:T(8,128)(2,1)S(1)} all-to-all(bf16[16,16,256]{2,1,0:T(8,128)(2,1)S(1)} %reduce_2.1), channel_id=1, replica_groups=mesh['z1'=2,'z0'=2,'y1'=2,'y0'=2,'x'=4,'c'=2] {'y1','y0','x'}, dimensions={0} | all-to-all | bytes 262144 | tf_op jit(solution)/shard_map/all_to_all | solution.py:42
  77.5 10.8 %all_to_all.75.received = bf16[32,16,128]{2,1,0:T(8,128)(2,1)S(1)} all-to-all(bf16[32,16,128]{2,1,0:T(8,128)(2,1)S(1)} %get-tuple-element.99), channel_id=1, replica_groups=mesh['z1'=2,'z0'=2,'y1'=2,'y0'=2,'x'=4,'c'=2] {'z0','y1','y0','x'}, dimensions={0} | all-to-all | bytes 262144 | tf_op jit(solution)/shard_map/all_to_all | solution.py:42
  88.4 10.7 %all_to_all.76.refs_0_ = bf16[32,16,128]{2,1,0:T(8,128)(2,1)S(1)} all-to-all(bf16[32,16,128]{2,1,0:T(8,128)(2,1)S(1)} %reduce_3.1), channel_id=1, replica_groups=mesh['z1'=2,'z0'=2,'y1'=2,'y0'=2,'x'=4,'c'=2] {'z0','y1','y0','x'}, dimensions={0} | all-to-all | bytes 262144 | tf_op jit(solution)/shard_map/all_to_all | solution.py:42
  99.6 10.8 %all_to_all.77.refs_0_ = bf16[32,16,128]{2,1,0:T(8,128)(2,1)S(1)} all-to-all(bf16[32,16,128]{2,1,0:T(8,128)(2,1)S(1)} %top_lower.1), channel_id=1, replica_groups=mesh['z1'=2,'z0'=2,'y1'=2,'y0'=2,'x'=4,'c'=2] {'z0','y1','y0','x'}, dimensions={0} | all-to-all | bytes 262144 | tf_op jit(solution)/shard_map/all_to_all | solution.py:42
  110.8 10.7 %all_to_all.78.refs_0_ = bf16[32,16,128]{2,1,0:T(8,128)(2,1)S(1)} all-to-all(bf16[32,16,128]{2,1,0:T(8,128)(2,1)S(1)} %get-tuple-element.106), channel_id=1, replica_groups=mesh['z1'=2,'z0'=2,'y1'=2,'y0'=2,'x'=4,'c'=2] {'z0','y1','y0','x'}, dimensions={0} | all-to-all | bytes 262144 | tf_op jit(solution)/shard_map/all_to_all | solution.py:42
  122.0 10.0 %all_to_all.79.refs_0_ = bf16[16,16,256]{2,1,0:T(8,128)(2,1)S(1)} all-to-all(bf16[16,16,256]{2,1,0:T(8,128)(2,1)S(1)} %back_2.1), channel_id=1, replica_groups=mesh['z1'=2,'z0'=2,'y1'=2,'y0'=2,'x'=4,'c'=2] {'y1','y0','x'}, dimensions={0} | all-to-all | bytes 262144 | tf_op jit(solution)/shard_map/all_to_all | solution.py:42
  132.3 9.6 %all_to_all.80.refs_0_ = bf16[16,16,256]{2,1,0:T(8,128)(2,1)S(1)} all-to-all(bf16[16,16,256]{2,1,0:T(8,128)(2,1)S(1)} %get-tuple-element.110), channel_id=1, replica_groups=mesh['z1'=2,'z0'=2,'y1'=2,'y0'=2,'x'=4,'c'=2] {'y1','y0','x'}, dimensions={0} | all-to-all | bytes 262144 | tf_op jit(solution)/shard_map/all_to_all | solution.py:42
  142.8 8.1 %all_to_all.81.refs_0_ = bf16[8,16,512]{2,1,0:T(8,128)(2,1)S(1)} all-to-all(bf16[8,16,512]{2,1,0:T(8,128)(2,1)S(1)} %back_1.1), channel_id=1, replica_groups=mesh['z1'=2,'z0'=2,'y1'=2,'y0'=2,'x'=4,'c'=2] {'y0','x'}, dimensions={0} | all-to-all | bytes 262144 | tf_op jit(solution)/shard_map/all_to_all | solution.py:42
  151.6 7.8 %all_to_all.82.refs_0_ = bf16[8,16,512]{2,1,0:T(8,128)(2,1)S(1)} all-to-all(bf16[8,16,512]{2,1,0:T(8,128)(2,1)S(1)} %get-tuple-element.115), channel_id=1, replica_groups=mesh['z1'=2,'z0'=2,'y1'=2,'y0'=2,'x'=4,'c'=2] {'y0','x'}, dimensions={0} | all-to-all | bytes 262144 | tf_op jit(solution)/shard_map/all_to_all | solution.py:42
  161.6 1.4 collective-permute-start.13
  165.7 1.6 leaf_solution.1
  167.3 15.3 %all_to_all.83.received = bf16[64,8,128]{2,1,0:T(8,128)(2,1)S(1)} all-to-all(bf16[64,8,128]{2,1,0:T(8,128)(2,1)S(1)} %leaf_solution.1), channel_id=1, replica_groups=mesh['z1'=2,'z0'=2,'y1'=2,'y0'=2,'x'=4,'c'=2] {'z1','z0','y1','y0','x'}, dimensions={0} | all-to-all | bytes 262144 | tf_op jit(solution)/shard_map/all_to_all | solution.py:42
  182.6 14.7 %collective-permute-start.15 = (bf16[64,8,128]{2,1,0:T(8,128)(2,1)S(1)}, bf16[64,8,128]{2,1,0:T(8,128)(2,1)S(1)}, u32[]{:S(2)}, u32[]{:S(2)}) collective-permute-start(bf16[64,8,128]{2,1,0:T(8,128)(2,1)S(1)} %all_to_all.83.received), channel_id=1, source_target_pairs={{0,1},{1,0},{2,3},{3,2},{4,5},{5,4},{6,7},{7,6},{8,9},{9,8},{10,11... | collective-permute-start | bytes 393224 | tf_op jit(solution)/shard_map/ppermute | solution.py:38
  (47 shorter events, 14.3 us)
Async XLA Ops:
  0.0 5.3 %copy-start.2 = (bf16[4096,256]{1,0:T(8,128)(2,1)S(1)}, bf16[4096,256]{1,0:T(8,128)(2,1)}, u32[]{:S(2)}) copy-start(bf16[4096,256]{1,0:T(8,128)(2,1)} %refs_8_.1) | copy-start | bytes 6291460
  2.1 2.9 %collective-permute-start.2 = (bf16[16,4096]{1,0:T(8,128)(2,1)S(1)}, bf16[16,4096]{1,0:T(8,128)(2,1)S(1)}, u32[]{:S(2)}, u32[]{:S(2)}) collective-permute-start(bf16[16,4096]{1,0:T(8,128)(2,1)S(1)} %get-tuple-element.68.refs_5_.refs_6_.refs_2_), channel_id=1, source_target_pairs={{0,1},{1,0},{2,3},{3,2},{4,5},{5,4},{6,7},{7,6},{8,9},{9,8},{10,11... | collective-permute-start | bytes 393224 | tf_op jit(solution)/shard_map/ppermute | solution.py:38
  3.6 1.2 collective-permute-start
  3.7 1.3 collective-permute-start.1
  5.0 22.0 %collective-permute-start.3 = (bf16[192,5632]{1,0:T(8,128)(2,1)S(1)}, bf16[192,5632]{1,0:T(8,128)(2,1)S(1)}, u32[]{:S(2)}, u32[]{:S(2)}) collective-permute-start(bf16[192,5632]{1,0:T(8,128)(2,1)S(1)} %get-tuple-element.72.refs_7_), channel_id=1, source_target_pairs={{0,1},{1,0},{2,3},{3,2},{4,5},{5,4},{6,7},{7,6},{8,9},{9,8},{10,11... | collective-permute-start | bytes 6488072 | tf_op jit(solution)/shard_map/ppermute | solution.py:38
  5.3 21.7 %collective-permute-start.4 = (bf16[4096,256]{1,0:T(8,128)(2,1)S(1)}, bf16[4096,256]{1,0:T(8,128)(2,1)S(1)}, u32[]{:S(2)}, u32[]{:S(2)}) collective-permute-start(bf16[4096,256]{1,0:T(8,128)(2,1)S(1)} %copy-done.2), channel_id=1, source_target_pairs={{0,1},{1,0},{2,3},{3,2},{4,5},{5,4},{6,7},{7,6},{8,9},{9,8},{10,11... | collective-permute-start | bytes 6291464 | tf_op jit(solution)/shard_map/ppermute | solution.py:38
  5.5 21.5 %collective-permute-start.5 = (bf16[4096,256]{1,0:T(8,128)(2,1)}, bf16[4096,256]{1,0:T(8,128)(2,1)S(1)}, u32[]{:S(2)}, u32[]{:S(2)}) collective-permute-start(bf16[4096,256]{1,0:T(8,128)(2,1)} %refs_10_.1), channel_id=1, source_target_pairs={{0,1},{1,0},{2,3},{3,2},{4,5},{5,4},{6,7},{7,6},{8,9},{9,8},{10,11... | collective-permute-start | bytes 6291464 | tf_op jit(solution)/shard_map/ppermute | solution.py:38
  27.0 13.2 %copy-start.1 = (bf16[4096,256]{1,0:T(8,128)(2,1)S(1)}, bf16[4096,256]{1,0:T(8,128)(2,1)}, u32[]{:S(2)}) copy-start(bf16[4096,256]{1,0:T(8,128)(2,1)} %refs_6_.1) | copy-start | bytes 6291460
  27.0 22.5 %copy-start.3 = (bf16[4096,256]{1,0:T(8,128)(2,1)S(1)}, bf16[4096,256]{1,0:T(8,128)(2,1)}, u32[]{:S(2)}) copy-start(bf16[4096,256]{1,0:T(8,128)(2,1)} %refs_10_.1) | copy-start | bytes 6291460
  30.9 9.3 %collective-permute-start.6 = (bf16[4096,256]{1,0:T(8,128)(2,1)S(1)}, bf16[4096,256]{1,0:T(8,128)(2,1)S(1)}, u32[]{:S(2)}, u32[]{:S(2)}) collective-permute-start(bf16[4096,256]{1,0:T(8,128)(2,1)S(1)} %get-tuple-element.84.refs_4_), channel_id=1, source_target_pairs={{0,1},{1,0},{2,3},{3,2},{4,5},{5,4},{6,7},{7,6},{8,9},{9,8},{10,11... | collective-permute-start | bytes 6291464 | tf_op jit(solution)/shard_map/ppermute | solution.py:38
  40.2 22.9 %collective-permute-start.8 = (bf16[4096,256]{1,0:T(8,128)(2,1)S(1)}, bf16[4096,256]{1,0:T(8,128)(2,1)S(1)}, u32[]{:S(2)}, u32[]{:S(2)}) collective-permute-start(bf16[4096,256]{1,0:T(8,128)(2,1)S(1)} %copy-done.1), channel_id=1, source_target_pairs={{0,1},{1,0},{2,3},{3,2},{4,5},{5,4},{6,7},{7,6},{8,9},{9,8},{10,11... | collective-permute-start | bytes 6291464 | tf_op jit(solution)/shard_map/ppermute | solution.py:38
  41.7 21.5 %collective-permute-start.7 = (bf16[128,4096]{1,0:T(8,128)(2,1)S(1)}, bf16[128,4096]{1,0:T(8,128)(2,1)S(1)}, u32[]{:S(2)}, u32[]{:S(2)}) collective-permute-start(bf16[128,4096]{1,0:T(8,128)(2,1)S(1)} %get-tuple-element.92.refs_2_), channel_id=1, source_target_pairs={{0,1},{1,0},{2,3},{3,2},{4,5},{5,4},{6,7},{7,6},{8,9},{9,8},{10,11... | collective-permute-start | bytes 3145736 | tf_op jit(solution)/shard_map/ppermute | solution.py:38
  49.6 16.8 %copy-start = (bf16[4096,256]{1,0:T(8,128)(2,1)S(1)}, bf16[4096,256]{1,0:T(8,128)(2,1)}, u32[]{:S(2)}) copy-start(bf16[4096,256]{1,0:T(8,128)(2,1)} %refs_2_.1) | copy-start | bytes 6291460
  63.2 25.2 %collective-permute-start.11 = (bf16[192,5632]{1,0:T(8,128)(2,1)S(1)}, bf16[192,5632]{1,0:T(8,128)(2,1)S(1)}, u32[]{:S(2)}, u32[]{:S(2)}) collective-permute-start(bf16[192,5632]{1,0:T(8,128)(2,1)S(1)} %get-tuple-element.103.refs_6_.refs_12_), channel_id=1, source_target_pairs={{0,1},{1,0},{2,3},{3,2},{4,5},{5,4},{6,7},{7,6},{8,9},{9,8},{10,11... | collective-permute-start | bytes 6488072 | tf_op jit(solution)/shard_map/ppermute | solution.py:38
  66.2 22.1 %collective-permute-start.9 = (bf16[4096,256]{1,0:T(8,128)(2,1)S(1)}, bf16[4096,256]{1,0:T(8,128)(2,1)S(1)}, u32[]{:S(2)}, u32[]{:S(2)}) collective-permute-start(bf16[4096,256]{1,0:T(8,128)(2,1)S(1)} %get-tuple-element.101.refs_6_.refs_2_), channel_id=1, source_target_pairs={{0,1},{1,0},{2,3},{3,2},{4,5},{5,4},{6,7},{7,6},{8,9},{9,8},{10,11... | collective-permute-start | bytes 6291464 | tf_op jit(solution)/shard_map/ppermute | solution.py:38
  66.3 22.0 %collective-permute-start.10 = (bf16[4096,256]{1,0:T(8,128)(2,1)S(1)}, bf16[4096,256]{1,0:T(8,128)(2,1)S(1)}, u32[]{:S(2)}, u32[]{:S(2)}) collective-permute-start(bf16[4096,256]{1,0:T(8,128)(2,1)S(1)} %copy-done), channel_id=1, source_target_pairs={{0,1},{1,0},{2,3},{3,2},{4,5},{5,4},{6,7},{7,6},{8,9},{9,8},{10,11... | collective-permute-start | bytes 6291464 | tf_op jit(solution)/shard_map/ppermute | solution.py:38
  160.6 3.8 %collective-permute-start.14 = (bf16[16,384]{1,0:T(8,128)(2,1)S(1)}, bf16[16,384]{1,0:T(8,128)(2,1)S(1)}, u32[]{:S(2)}, u32[]{:S(2)}) collective-permute-start(bf16[16,384]{1,0:T(8,128)(2,1)S(1)} %back_0.1.refs_0_), channel_id=1, source_target_pairs={{0,6},{2,4},{4,2},{6,0},{1,7},{3,5},{5,3},{7,1},{8,14},{10,12},{12... | collective-permute-start | bytes 36872 | tf_op jit(solution)/shard_map/ppermute | solution.py:673
  161.6 4.0 %collective-permute-start.13 = (bf16[16,384]{1,0:T(8,128)(2,1)S(1)}, bf16[16,384]{1,0:T(8,128)(2,1)S(1)}, u32[]{:S(2)}, u32[]{:S(2)}) collective-permute-start(bf16[16,384]{1,0:T(8,128)(2,1)S(1)} %back_0.1.refs_0_), channel_id=1, source_target_pairs={{0,4},{2,6},{4,0},{6,2},{1,5},{3,7},{5,1},{7,3},{8,12},{10,14},{12... | collective-permute-start | bytes 36872 | tf_op jit(solution)/shard_map/ppermute | solution.py:673
  163.0 2.7 %collective-permute-start.12 = (bf16[16,384]{1,0:T(8,128)(2,1)S(1)}, bf16[16,384]{1,0:T(8,128)(2,1)S(1)}, u32[]{:S(2)}, u32[]{:S(2)}) collective-permute-start(bf16[16,384]{1,0:T(8,128)(2,1)S(1)} %back_0.1.refs_0_), channel_id=1, source_target_pairs={{0,2},{2,0},{4,6},{6,4},{1,3},{3,1},{5,7},{7,5},{8,10},{10,8},{12,... | collective-permute-start | bytes 36872 | tf_op jit(solution)/shard_map/ppermute | solution.py:673
  182.6 15.7 %collective-permute-start.15 = (bf16[64,8,128]{2,1,0:T(8,128)(2,1)S(1)}, bf16[64,8,128]{2,1,0:T(8,128)(2,1)S(1)}, u32[]{:S(2)}, u32[]{:S(2)}) collective-permute-start(bf16[64,8,128]{2,1,0:T(8,128)(2,1)S(1)} %all_to_all.83.received), channel_id=1, source_target_pairs={{0,1},{1,0},{2,3},{3,2},{4,5},{5,4},{6,7},{7,6},{8,9},{9,8},{10,11... | collective-permute-start | bytes 393224 | tf_op jit(solution)/shard_map/ppermute | solution.py:38

commit v8 on v7

--- a/solution.py
+++ b/solution.py
@@ -18,9 +18,9 @@
 }
 MEMBERS = {0: 4, 1: 8, 2: 16, 3: 32, 4: 64}
 FIRST = ("leaf", "lower1", "down2")
-SECOND = ("second",)
+SECOND = ("lower2", "down3")
 THIRD = ("third", "back2")
-FOURTH = ("middle", "upper1", "last")
+FOURTH = ("middle", "upper1", "back1", "upper0")
 LEAF_ROWS = 1536
 HALF = 16
 SEP = 4096
@@ -511,6 +511,10 @@
     factors = {
         "lower1": lower_first,
         "down2": downlink_second,
+        "lower2": lower_second,
+        "down3": downlink_third,
+        "back1": uplink_first.T,
+        "upper0": upper_leaf.T,
         "back2": uplink_second,
         "upper1": upper_first,
     }
@@ -573,12 +577,12 @@
     patterns = (own_patterns, other_patterns)
     payload = begin(payload, FIRST)
     received = finish(exchange(payload.reshape(64, 16, 128), 4), FIRST)
-    own_y, other_y, *rights, term, factors["second"], factors["third"] = call(
+    own_y, other_y, *rights, term, factors["third"] = call(
         fetching(
             windowed(in_kernel, 3, LEAF_LEFT, LEAF_RIGHT),
-            4,
+            2,
             13,
-            ((0, LEFT), (0, RIGHT), (1, UPPER), (1, LOWER)),
+            ((0, UPPER), (0, LOWER)),
         ),
         "leaf_front",
         [
@@ -588,11 +592,10 @@
             ((HALF, 256), BF16),
             ((HALF, 128), BF16),
             ((8, HALF, 512), BF16),
-            ((SEP, 256), BF16),
             ((128, SEP), BF16),
         ],
         (received,) + patterns + pairs["leaf"] + (own_columns, other_columns),
-        distant=(lower_second, downlink_third, lower_third.T, upper_third.T),
+        distant=(lower_third.T, upper_third.T),
         scratch=[pltpu.VMEM((128, 1024), BF16)],
     )
     level_y = {0: (own_y, other_y)}
@@ -622,16 +625,16 @@
             operands = (gathered, masks) + patterns
             body = functools.partial(up_kernel, level)
             if level == 1:
-                own_y, other_y, term, factors["middle"], factors["last"] = call(
-                    fetching(body, 4, 11, ((0, LEFT), (0, RIGHT), (1, LEAF_RIGHT), (1, LEAF_LEFT))),
+                own_y, other_y, term, factors["middle"] = call(
+                    fetching(body, 2, 11, ((0, LEFT), (0, RIGHT))),
                     "up_1",
-                    outs + [((SEP, 256), BF16), ((LEAF, LEAF_ROWS + SEP), BF16)],
+                    outs + [((SEP, 256), BF16)],
                     operands + pairs["lower1"] + pairs["down2"],
-                    distant=(uplink_third, upper_second, uplink_first.T, upper_leaf.T),
+                    distant=(uplink_third, upper_second),
                 )
             else:
                 own_y, other_y, term = call(
-                    windowed(body, 4, LEFT, RIGHT), "up_2", outs, operands + pairs["second"]
+                    body, "up_2", outs, operands + pairs["lower2"] + pairs["down3"]
                 )
         else:
             copies = call(
@@ -645,7 +648,7 @@
     level_x = {}
     whole = (slice(None), slice(None))
     uppers = {3: ("third", LOWER), 2: ("middle", RIGHT), 1: ("upper1", whole)}
-    backs = {3: ("middle", LEFT), 2: ("back2", whole), 1: ("last", LEAF_RIGHT)}
+    backs = {3: ("middle", LEFT), 2: ("back2", whole), 1: ("back1", whole)}
     for level in (3, 2, 1):
         members = MEMBERS[level]
         chip_width = SEP // members
@@ -672,7 +675,7 @@
         ring = [(source, source ^ step) for source in range(4)]
         parts.append(lax.ppermute(copies, "x", ring))
     outbound = call(
-        windowed(out_kernel, 12, LEAF_LEFT),
+        out_kernel,
         "leaf_solution",
         [((64, 8, 128), BF16)],
         tuple(parts)
@@ -680,7 +683,7 @@
         + level_x[1]
         + level_x[2]
         + level_x[3]
-        + pairs["last"],
+        + pairs["upper0"],
         scratch=[pltpu.VMEM((HALF, 8 * LEAF), BF16)],
     )[0]
     returned = exchange(outbound, 4)

time: 200 us -> 201 us (level)
    ppermute x13 -> x15, starting transfers between devices: 24.2 us -> 25.2 us  [swap(): return lax.ppermute(value, 'c', [(0, 1), (1, 0)])]
  transfers between devices with their start and end apart: 16 -> 18, of which waited for: 5 -> 5; matrix products, arithmetic and copies ran while one was open for 0% -> 0% of each run, Pallas kernels for 2% -> 2%
where the time goes in v8:
time: 201 us; the launch traced here: 200 us
  blocking collectives  151 us (75%)
  starting transfers between devices  28.4 us (14%)
  Pallas kernels  16.8 us (8%)
  waiting for transfers between devices  3.64 us (2%)
    all_to_all x14, blocking collectives, exchange(): lax.all_to_all(value, CHIPS[level], split_axis=0, concat_axis=0, tiled=True)  151 us
    ppermute x15, starting transfers between devices, swap(): return lax.ppermute(value, 'c', [(0, 1), (1, 0)])  25.2 us
    pallas_call x17, Pallas kernels, call(): pl.pallas_call(body, name=name, out_shape=[jax.ShapeDtypeStruct(shape, dt...  16.8 us
  transfers between devices with their start and end apart: 18, of which 5 were waited for; matrix products, arithmetic and copies ran while one was open for 0% of the time, Pallas kernels for 2%

profile of v8, /device:TPU:1, one launch (start us, length us, event | category | flops | bytes accessed | tf_op | source)
XLA Modules:
  0.0 199.9 jit_solution(16887198269610202071)
XLA Ops:
  0.0 2.1 %start.1 = (bf16[16,8,128]{2,1,0:T(8,128)(2,1)S(1)}, bf16[16,8,128]{2,1,0:T(8,128)(2,1)S(1)}, bf16[16,4096]{1,0:T(8,128)(2,1)S(1)}, f32[8,896]{1,0:T(8,128)S(1)}...) custom-call(s32[14]{0:T(128)} %live.1, s32[640]{0:T(1024)} %send_order.1, s32[640]{0:T(1024)} %owner_order.1, ...), custom_call_target="tpu_custom_call" | custom-call | tf_op jit(solution)/shard_map/start/pallas_call | solution.py:50
  2.1 1.5 collective-permute-start.2
  5.9 21.3 %all_to_all.70.refs_2_ = bf16[64,16,128]{2,1,0:T(8,128)(2,1)S(1)} all-to-all(bf16[64,16,128]{2,1,0:T(8,128)(2,1)S(1)} %bitcast.12), channel_id=1, replica_groups=mesh['z1'=2,'z0'=2,'y1'=2,'y0'=2,'x'=4,'c'=2] {'z1','z0','y1','y0','x'}, dimensions={0} | all-to-all | bytes 524288 | tf_op jit(solution)/shard_map/all_to_all | solution.py:42
  27.2 2.8 %leaf_front.1 = (bf16[16,192]{1,0:T(8,128)(2,1)S(1)}, bf16[16,192]{1,0:T(8,128)(2,1)S(1)}, bf16[16,512]{1,0:T(8,128)(2,1)S(1)}, bf16[16,256]{1,0:T(8,128)(2,1)S(...) custom-call(bf16[64,4096]{1,0:T(8,128)(2,1)} %bitcast.17, ...), custom_call_target="tpu_custom_call" | custom-call | tf_op jit(solution)/shard_map/leaf_front/pallas_call | solution.py:50
  30.0 1.5 collective-permute-start.6
  31.6 7.8 %all_to_all.71.received = bf16[8,16,512]{2,1,0:T(8,128)(2,1)S(1)} all-to-all(bf16[8,16,512]{2,1,0:T(8,128)(2,1)S(1)} %get-tuple-element.82), channel_id=1, replica_groups=mesh['z1'=2,'z0'=2,'y1'=2,'y0'=2,'x'=4,'c'=2] {'y0','x'}, dimensions={0} | all-to-all | bytes 262144 | tf_op jit(solution)/shard_map/all_to_all | solution.py:42
  39.5 1.6 collective-permute-start.9
  41.2 7.8 %all_to_all.72.refs_2_ = bf16[8,16,512]{2,1,0:T(8,128)(2,1)S(1)} all-to-all(bf16[8,16,512]{2,1,0:T(8,128)(2,1)S(1)} %reduce_1.1), channel_id=1, replica_groups=mesh['z1'=2,'z0'=2,'y1'=2,'y0'=2,'x'=4,'c'=2] {'y0','x'}, dimensions={0} | all-to-all | bytes 262144 | tf_op jit(solution)/shard_map/all_to_all | solution.py:42
  49.1 3.4 %up_1.1 = (bf16[16,256]{1,0:T(8,128)(2,1)S(1)}, bf16[16,256]{1,0:T(8,128)(2,1)S(1)}, bf16[16,16,256]{2,1,0:T(8,128)(2,1)S(1)}, bf16[4096,256]{1,0:T(8,128)(2,1)S(1)}) custom-call(bf16[4096,128]{1,0:T(8,128)(2,1)} %refs_0_.1, bf16[4096,128]{1,0:T(8,128)(2,1)} %refs_1_.1, bf16[8,16,512]{2,1,0:T(8,128)(2,1)S(1)} %all_to_all.72.refs_2_, ...), custom_call_target="tpu_custom_call" | custom-call | tf_op jit(solution)/shard_map/up_1/pallas_call | solution.py:50
  52.5 10.4 %all_to_all.73.received = bf16[16,16,256]{2,1,0:T(8,128)(2,1)S(1)} all-to-all(bf16[16,16,256]{2,1,0:T(8,128)(2,1)S(1)} %get-tuple-element.92), channel_id=1, replica_groups=mesh['z1'=2,'z0'=2,'y1'=2,'y0'=2,'x'=4,'c'=2] {'y1','y0','x'}, dimensions={0} | all-to-all | bytes 262144 | tf_op jit(solution)/shard_map/all_to_all | solution.py:42
  62.9 3.1 %collective-permute-start.10 = (bf16[4096,256]{1,0:T(8,128)(2,1)S(1)}, bf16[4096,256]{1,0:T(8,128)(2,1)S(1)}, u32[]{:S(2)}, u32[]{:S(2)}) collective-permute-start(bf16[4096,256]{1,0:T(8,128)(2,1)S(1)} %get-tuple-element.103.refs_6_.refs_2_), channel_id=1, source_target_pairs={{0,1},{1,0},{2,3},{3,2},{4,5},{5,4},{6,7},{7,6},{8,9},{9,8},{10,11... | collective-permute-start | bytes 6291464 | tf_op jit(solution)/shard_map/ppermute | solution.py:38
  66.6 9.6 %all_to_all.74.gathered = bf16[16,16,256]{2,1,0:T(8,128)(2,1)S(1)} all-to-all(bf16[16,16,256]{2,1,0:T(8,128)(2,1)S(1)} %reduce_2.1), channel_id=1, replica_groups=mesh['z1'=2,'z0'=2,'y1'=2,'y0'=2,'x'=4,'c'=2] {'y1','y0','x'}, dimensions={0} | all-to-all | bytes 262144 | tf_op jit(solution)/shard_map/all_to_all | solution.py:42
  77.4 10.8 %all_to_all.75.received = bf16[32,16,128]{2,1,0:T(8,128)(2,1)S(1)} all-to-all(bf16[32,16,128]{2,1,0:T(8,128)(2,1)S(1)} %get-tuple-element.101), channel_id=1, replica_groups=mesh['z1'=2,'z0'=2,'y1'=2,'y0'=2,'x'=4,'c'=2] {'z0','y1','y0','x'}, dimensions={0} | all-to-all | bytes 262144 | tf_op jit(solution)/shard_map/all_to_all | solution.py:42
  88.3 10.7 %all_to_all.76.refs_0_ = bf16[32,16,128]{2,1,0:T(8,128)(2,1)S(1)} all-to-all(bf16[32,16,128]{2,1,0:T(8,128)(2,1)S(1)} %reduce_3.1), channel_id=1, replica_groups=mesh['z1'=2,'z0'=2,'y1'=2,'y0'=2,'x'=4,'c'=2] {'z0','y1','y0','x'}, dimensions={0} | all-to-all | bytes 262144 | tf_op jit(solution)/shard_map/all_to_all | solution.py:42
  99.5 10.7 %all_to_all.77.refs_0_ = bf16[32,16,128]{2,1,0:T(8,128)(2,1)S(1)} all-to-all(bf16[32,16,128]{2,1,0:T(8,128)(2,1)S(1)} %top_lower.1), channel_id=1, replica_groups=mesh['z1'=2,'z0'=2,'y1'=2,'y0'=2,'x'=4,'c'=2] {'z0','y1','y0','x'}, dimensions={0} | all-to-all | bytes 262144 | tf_op jit(solution)/shard_map/all_to_all | solution.py:42
  110.7 10.7 %all_to_all.78.refs_0_ = bf16[32,16,128]{2,1,0:T(8,128)(2,1)S(1)} all-to-all(bf16[32,16,128]{2,1,0:T(8,128)(2,1)S(1)} %get-tuple-element.109), channel_id=1, replica_groups=mesh['z1'=2,'z0'=2,'y1'=2,'y0'=2,'x'=4,'c'=2] {'z0','y1','y0','x'}, dimensions={0} | all-to-all | bytes 262144 | tf_op jit(solution)/shard_map/all_to_all | solution.py:42
  121.8 10.0 %all_to_all.79.refs_0_ = bf16[16,16,256]{2,1,0:T(8,128)(2,1)S(1)} all-to-all(bf16[16,16,256]{2,1,0:T(8,128)(2,1)S(1)} %back_2.1), channel_id=1, replica_groups=mesh['z1'=2,'z0'=2,'y1'=2,'y0'=2,'x'=4,'c'=2] {'y1','y0','x'}, dimensions={0} | all-to-all | bytes 262144 | tf_op jit(solution)/shard_map/all_to_all | solution.py:42
  132.2 9.6 %all_to_all.80.refs_0_ = bf16[16,16,256]{2,1,0:T(8,128)(2,1)S(1)} all-to-all(bf16[16,16,256]{2,1,0:T(8,128)(2,1)S(1)} %get-tuple-element.113), channel_id=1, replica_groups=mesh['z1'=2,'z0'=2,'y1'=2,'y0'=2,'x'=4,'c'=2] {'y1','y0','x'}, dimensions={0} | all-to-all | bytes 262144 | tf_op jit(solution)/shard_map/all_to_all | solution.py:42
  142.7 8.2 %all_to_all.81.refs_0_ = bf16[8,16,512]{2,1,0:T(8,128)(2,1)S(1)} all-to-all(bf16[8,16,512]{2,1,0:T(8,128)(2,1)S(1)} %back_1.1), channel_id=1, replica_groups=mesh['z1'=2,'z0'=2,'y1'=2,'y0'=2,'x'=4,'c'=2] {'y0','x'}, dimensions={0} | all-to-all | bytes 262144 | tf_op jit(solution)/shard_map/all_to_all | solution.py:42
  151.6 7.8 %all_to_all.82.refs_0_ = bf16[8,16,512]{2,1,0:T(8,128)(2,1)S(1)} all-to-all(bf16[8,16,512]{2,1,0:T(8,128)(2,1)S(1)} %get-tuple-element.118), channel_id=1, replica_groups=mesh['z1'=2,'z0'=2,'y1'=2,'y0'=2,'x'=4,'c'=2] {'y0','x'}, dimensions={0} | all-to-all | bytes 262144 | tf_op jit(solution)/shard_map/all_to_all | solution.py:42
  161.6 1.4 collective-permute-start.15
  165.7 1.6 leaf_solution.1
  167.3 15.2 %all_to_all.83.received = bf16[64,8,128]{2,1,0:T(8,128)(2,1)S(1)} all-to-all(bf16[64,8,128]{2,1,0:T(8,128)(2,1)S(1)} %leaf_solution.1), channel_id=1, replica_groups=mesh['z1'=2,'z0'=2,'y1'=2,'y0'=2,'x'=4,'c'=2] {'z1','z0','y1','y0','x'}, dimensions={0} | all-to-all | bytes 262144 | tf_op jit(solution)/shard_map/all_to_all | solution.py:42
  182.4 15.3 %collective-permute-start.17 = (bf16[64,8,128]{2,1,0:T(8,128)(2,1)S(1)}, bf16[64,8,128]{2,1,0:T(8,128)(2,1)S(1)}, u32[]{:S(2)}, u32[]{:S(2)}) collective-permute-start(bf16[64,8,128]{2,1,0:T(8,128)(2,1)S(1)} %all_to_all.83.received), channel_id=1, source_target_pairs={{0,1},{1,0},{2,3},{3,2},{4,5},{5,4},{6,7},{7,6},{8,9},{9,8},{10,11... | collective-permute-start | bytes 393224 | tf_op jit(solution)/shard_map/ppermute | solution.py:38
  (59 shorter events, 14.6 us)
Async XLA Ops:
  2.1 2.9 %collective-permute-start.2 = (bf16[16,4096]{1,0:T(8,128)(2,1)S(1)}, bf16[16,4096]{1,0:T(8,128)(2,1)S(1)}, u32[]{:S(2)}, u32[]{:S(2)}) collective-permute-start(bf16[16,4096]{1,0:T(8,128)(2,1)S(1)} %get-tuple-element.70.refs_3_.refs_4_.own_pattern.refs_2_), channel_id=1, source_target_pairs={{0,1},{1,0},{2,3},{3,2},{4,5},{5,4},{6,7},{7,6},{8,9},{9,8},{10,11... | collective-permute-start | bytes 393224 | tf_op jit(solution)/shard_map/ppermute | solution.py:38
  3.6 1.2 collective-permute-start
  3.7 1.3 collective-permute-start.1
  5.0 22.2 %collective-permute-start.3 = (bf16[192,5632]{1,0:T(8,128)(2,1)S(1)}, bf16[192,5632]{1,0:T(8,128)(2,1)S(1)}, u32[]{:S(2)}, u32[]{:S(2)}) collective-permute-start(bf16[192,5632]{1,0:T(8,128)(2,1)S(1)} %get-tuple-element.74.refs_5_), channel_id=1, source_target_pairs={{0,1},{1,0},{2,3},{3,2},{4,5},{5,4},{6,7},{7,6},{8,9},{9,8},{10,11... | collective-permute-start | bytes 6488072 | tf_op jit(solution)/shard_map/ppermute | solution.py:38
  5.3 21.8 %collective-permute-start.4 = (bf16[4096,256]{1,0:T(8,128)(2,1)S(1)}, bf16[4096,256]{1,0:T(8,128)(2,1)S(1)}, u32[]{:S(2)}, u32[]{:S(2)}) collective-permute-start(bf16[4096,256]{1,0:T(8,128)(2,1)S(1)} %copy-done.2), channel_id=1, source_target_pairs={{0,1},{1,0},{2,3},{3,2},{4,5},{5,4},{6,7},{7,6},{8,9},{9,8},{10,11... | collective-permute-start | bytes 6291464 | tf_op jit(solution)/shard_map/ppermute | solution.py:38
  5.5 21.7 %collective-permute-start.5 = (bf16[4096,256]{1,0:T(8,128)(2,1)}, bf16[4096,256]{1,0:T(8,128)(2,1)S(1)}, u32[]{:S(2)}, u32[]{:S(2)}) collective-permute-start(bf16[4096,256]{1,0:T(8,128)(2,1)} %refs_8_.1), channel_id=1, source_target_pairs={{0,1},{1,0},{2,3},{3,2},{4,5},{5,4},{6,7},{7,6},{8,9},{9,8},{10,11... | collective-permute-start | bytes 6291464 | tf_op jit(solution)/shard_map/ppermute | solution.py:38
  5.9 25.7 %copy-start.6 = (bf16[4096,128]{1,0:T(8,128)(2,1)S(1)}, bf16[4096,128]{1,0:T(8,128)(2,1)}, u32[]{:S(2)}) copy-start(bf16[4096,128]{1,0:T(8,128)(2,1)} %own_link.1) | copy-start | bytes 3145732
  27.2 12.3 %copy-start.1 = (bf16[4096,256]{1,0:T(8,128)(2,1)S(1)}, bf16[4096,256]{1,0:T(8,128)(2,1)}, u32[]{:S(2)}) copy-start(bf16[4096,256]{1,0:T(8,128)(2,1)} %refs_6_.3) | copy-start | bytes 6291460
  27.2 21.9 %copy-start.3 = (bf16[4096,256]{1,0:T(8,128)(2,1)S(1)}, bf16[4096,256]{1,0:T(8,128)(2,1)}, u32[]{:S(2)}) copy-start(bf16[4096,256]{1,0:T(8,128)(2,1)} %refs_8_.1) | copy-start | bytes 6291460
  30.0 9.4 %collective-permute-start.6 = (bf16[4096,128]{1,0:T(8,128)(2,1)S(1)}, bf16[4096,128]{1,0:T(8,128)(2,1)S(1)}, u32[]{:S(2)}, u32[]{:S(2)}) collective-permute-start(bf16[4096,128]{1,0:T(8,128)(2,1)S(1)} %copy-done.5), channel_id=1, source_target_pairs={{0,1},{1,0},{2,3},{3,2},{4,5},{5,4},{6,7},{7,6},{8,9},{9,8},{10,11... | collective-permute-start | bytes 3145736 | tf_op jit(solution)/shard_map/ppermute | solution.py:38
  31.5 8.0 %collective-permute-start.7 = (bf16[4096,128]{1,0:T(8,128)(2,1)S(1)}, bf16[4096,128]{1,0:T(8,128)(2,1)S(1)}, u32[]{:S(2)}, u32[]{:S(2)}) collective-permute-start(bf16[4096,128]{1,0:T(8,128)(2,1)S(1)} %copy-done.6), channel_id=1, source_target_pairs={{0,1},{1,0},{2,3},{3,2},{4,5},{5,4},{6,7},{7,6},{8,9},{9,8},{10,11... | collective-permute-start | bytes 3145736 | tf_op jit(solution)/shard_map/ppermute | solution.py:38
  39.5 23.4 %collective-permute-start.9 = (bf16[4096,256]{1,0:T(8,128)(2,1)S(1)}, bf16[4096,256]{1,0:T(8,128)(2,1)S(1)}, u32[]{:S(2)}, u32[]{:S(2)}) collective-permute-start(bf16[4096,256]{1,0:T(8,128)(2,1)S(1)} %copy-done.1), channel_id=1, source_target_pairs={{0,1},{1,0},{2,3},{3,2},{4,5},{5,4},{6,7},{7,6},{8,9},{9,8},{10,11... | collective-permute-start | bytes 6291464 | tf_op jit(solution)/shard_map/ppermute | solution.py:38
  41.1 21.8 %collective-permute-start.8 = (bf16[128,4096]{1,0:T(8,128)(2,1)S(1)}, bf16[128,4096]{1,0:T(8,128)(2,1)S(1)}, u32[]{:S(2)}, u32[]{:S(2)}) collective-permute-start(bf16[128,4096]{1,0:T(8,128)(2,1)S(1)} %get-tuple-element.94.refs_2_), channel_id=1, source_target_pairs={{0,1},{1,0},{2,3},{3,2},{4,5},{5,4},{6,7},{7,6},{8,9},{9,8},{10,11... | collective-permute-start | bytes 3145736 | tf_op jit(solution)/shard_map/ppermute | solution.py:38
  49.0 17.0 %copy-start = (bf16[4096,256]{1,0:T(8,128)(2,1)S(1)}, bf16[4096,256]{1,0:T(8,128)(2,1)}, u32[]{:S(2)}) copy-start(bf16[4096,256]{1,0:T(8,128)(2,1)} %refs_2_.1) | copy-start | bytes 6291460
  49.0 17.1 %copy-start.4 = (bf16[4096,192]{0,1:T(8,128)(2,1)S(1)}, bf16[4096,192]{0,1:T(8,128)(2,1)}, u32[]{:S(2)}) copy-start(bf16[4096,192]{0,1:T(8,128)(2,1)} %param.36) | copy-start | bytes 4718596
  49.0 17.5 %copy-start.7 = (bf16[1536,192]{0,1:T(8,128)(2,1)S(1)}, bf16[1536,192]{0,1:T(8,128)(2,1)}, u32[]{:S(2)}) copy-start(bf16[1536,192]{0,1:T(8,128)(2,1)} %param.26) | copy-start | bytes 1769476
  62.9 25.3 %collective-permute-start.10 = (bf16[4096,256]{1,0:T(8,128)(2,1)S(1)}, bf16[4096,256]{1,0:T(8,128)(2,1)S(1)}, u32[]{:S(2)}, u32[]{:S(2)}) collective-permute-start(bf16[4096,256]{1,0:T(8,128)(2,1)S(1)} %get-tuple-element.103.refs_6_.refs_2_), channel_id=1, source_target_pairs={{0,1},{1,0},{2,3},{3,2},{4,5},{5,4},{6,7},{7,6},{8,9},{9,8},{10,11... | collective-permute-start | bytes 6291464 | tf_op jit(solution)/shard_map/ppermute | solution.py:38
  66.0 22.3 %collective-permute-start.11 = (bf16[4096,256]{1,0:T(8,128)(2,1)S(1)}, bf16[4096,256]{1,0:T(8,128)(2,1)S(1)}, u32[]{:S(2)}, u32[]{:S(2)}) collective-permute-start(bf16[4096,256]{1,0:T(8,128)(2,1)S(1)} %copy-done), channel_id=1, source_target_pairs={{0,1},{1,0},{2,3},{3,2},{4,5},{5,4},{6,7},{7,6},{8,9},{9,8},{10,11... | collective-permute-start | bytes 6291464 | tf_op jit(solution)/shard_map/ppermute | solution.py:38
  66.1 22.1 %collective-permute-start.12 = (bf16[192,4096]{1,0:T(8,128)(2,1)S(1)}, bf16[192,4096]{1,0:T(8,128)(2,1)S(1)}, u32[]{:S(2)}, u32[]{:S(2)}) collective-permute-start(bf16[192,4096]{1,0:T(8,128)(2,1)S(1)} %bitcast.10), channel_id=1, source_target_pairs={{0,1},{1,0},{2,3},{3,2},{4,5},{5,4},{6,7},{7,6},{8,9},{9,8},{10,11... | collective-permute-start | bytes 4718600 | tf_op jit(solution)/shard_map/ppermute | solution.py:38
  66.5 21.7 %collective-permute-start.13 = (bf16[192,1536]{1,0:T(8,128)(2,1)S(1)}, bf16[192,1536]{1,0:T(8,128)(2,1)S(1)}, u32[]{:S(2)}, u32[]{:S(2)}) collective-permute-start(bf16[192,1536]{1,0:T(8,128)(2,1)S(1)} %bitcast.13), channel_id=1, source_target_pairs={{0,1},{1,0},{2,3},{3,2},{4,5},{5,4},{6,7},{7,6},{8,9},{9,8},{10,11... | collective-permute-start | bytes 1769480 | tf_op jit(solution)/shard_map/ppermute | solution.py:38
  160.6 3.8 %collective-permute-start.16 = (bf16[16,384]{1,0:T(8,128)(2,1)S(1)}, bf16[16,384]{1,0:T(8,128)(2,1)S(1)}, u32[]{:S(2)}, u32[]{:S(2)}) collective-permute-start(bf16[16,384]{1,0:T(8,128)(2,1)S(1)} %back_0.1.own_part), channel_id=1, source_target_pairs={{0,6},{2,4},{4,2},{6,0},{1,7},{3,5},{5,3},{7,1},{8,14},{10,12},{12... | collective-permute-start | bytes 36872 | tf_op jit(solution)/shard_map/ppermute | solution.py:676
  161.6 4.0 %collective-permute-start.15 = (bf16[16,384]{1,0:T(8,128)(2,1)S(1)}, bf16[16,384]{1,0:T(8,128)(2,1)S(1)}, u32[]{:S(2)}, u32[]{:S(2)}) collective-permute-start(bf16[16,384]{1,0:T(8,128)(2,1)S(1)} %back_0.1.own_part), channel_id=1, source_target_pairs={{0,4},{2,6},{4,0},{6,2},{1,5},{3,7},{5,1},{7,3},{8,12},{10,14},{12... | collective-permute-start | bytes 36872 | tf_op jit(solution)/shard_map/ppermute | solution.py:676
  163.0 2.7 %collective-permute-start.14 = (bf16[16,384]{1,0:T(8,128)(2,1)S(1)}, bf16[16,384]{1,0:T(8,128)(2,1)S(1)}, u32[]{:S(2)}, u32[]{:S(2)}) collective-permute-start(bf16[16,384]{1,0:T(8,128)(2,1)S(1)} %back_0.1.own_part), channel_id=1, source_target_pairs={{0,2},{2,0},{4,6},{6,4},{1,3},{3,1},{5,7},{7,5},{8,10},{10,8},{12,... | collective-permute-start | bytes 36872 | tf_op jit(solution)/shard_map/ppermute | solution.py:676
  182.4 16.3 %collective-permute-start.17 = (bf16[64,8,128]{2,1,0:T(8,128)(2,1)S(1)}, bf16[64,8,128]{2,1,0:T(8,128)(2,1)S(1)}, u32[]{:S(2)}, u32[]{:S(2)}) collective-permute-start(bf16[64,8,128]{2,1,0:T(8,128)(2,1)S(1)} %all_to_all.83.received), channel_id=1, source_target_pairs={{0,1},{1,0},{2,3},{3,2},{4,5},{5,4},{6,7},{7,6},{8,9},{9,8},{10,11... | collective-permute-start | bytes 393224 | tf_op jit(solution)/shard_map/ppermute | solution.py:38
  (2 other events, 8.2 us)
